TPU v7x, 512 devices: a whole 4x8x8 slice. The times are simulated.
512 devices in a mesh: dp: 4 (over y_lo), seq: 32 (over z, y_hi, core), tensor: 4 (over x).
Axes of the slice: x: 4, y: 8 (y_hi: 2, y_lo: 4; y = y_hi * 4 + y_lo), z: 8, core: 2. Of those that a mesh axis runs over, the one named last changes fastest.
Arguments:
- queries: bfloat16 [4, 16384, 512], P('dp', 'seq', 'tensor'), may hold values from -6 to 6
- values: bfloat16 [4, 16384, 512], P('dp', 'seq', 'tensor'), may hold values from -6 to 6
- filt: float32 [16384, 512], P('seq', 'tensor'), may hold values from -4 to 4
- w_out: bfloat16 [512, 4096], P('tensor'), may hold values from -0.375 to 0.375
- cotangent: bfloat16 [4, 16384, 4096], P('dp', 'seq', 'tensor'), may hold values from -6 to 6
Outputs:
- mixed: bfloat16 [4, 16384, 4096], P('dp', 'seq', 'tensor')
- grad_query: bfloat16 [4, 16384, 512], P('dp', 'seq', 'tensor')
- grad_value: bfloat16 [4, 16384, 512], P('dp', 'seq', 'tensor')
- grad_filt: float32 [16384, 512], P('seq', 'tensor')
All inputs are finite; a program needn't handle non-finite values.
Results may differ from a plain program's by a relative error of at most 0.024.
Values may be sent and summed in bfloat16 or wider, within the bound.
No kernel may reach another device: no remote copies, remote signals or barrier semaphores. Data moves between devices by JAX's collectives and lax.ppermute only.
A program may use at most 64 MiB of HBM per device.

v0:
```python
import math

import jax
import jax.numpy as jnp
from jax import lax
from jax.sharding import PartitionSpec as P

HIGHEST = lax.Precision.HIGHEST


def for_sending(array):
    return jax.tree.map(lambda a: a.astype(jnp.bfloat16) if a.dtype == jnp.float32 else a, array)


def angle_table(first, second, period):
    index = first[:, None] * second[None, :] % period
    angle = -2.0 * math.pi / period * index.astype(jnp.float32)
    return (jnp.cos(angle), jnp.sin(angle))


def product(table_real, table_imag, data_real, data_imag, form):

    def apply(left, right):
        return jnp.einsum(form, left, right, precision=HIGHEST)

    return (
        apply(table_real, data_real) - apply(table_imag, data_imag),
        apply(table_real, data_imag) + apply(table_imag, data_real),
    )


def split_length(length):
    levels = length.bit_length() - 1
    inner = 1 << levels // 2
    return (inner, length // inner)


def local_forward(data_real, data_imag, freq_index, total):
    pair, length, width = data_real.shape
    inner, outer = split_length(length)
    cos_t, sin_t = angle_table(freq_index, jnp.arange(length, dtype=jnp.int32), total)
    cos_t = cos_t[:, :, None]
    sin_t = sin_t[:, :, None]
    data_real, data_imag = (
        data_real * cos_t - data_imag * sin_t,
        data_real * sin_t + data_imag * cos_t,
    )
    data_real = data_real.reshape(pair, outer, inner, width)
    data_imag = data_imag.reshape(pair, outer, inner, width)
    outer_c, outer_s = angle_table(
        jnp.arange(outer, dtype=jnp.int32), jnp.arange(outer, dtype=jnp.int32), outer
    )
    data_real, data_imag = product(outer_c, outer_s, data_real, data_imag, "ab,ebcd->eacd")
    mid_c, mid_s = angle_table(
        jnp.arange(outer, dtype=jnp.int32), jnp.arange(inner, dtype=jnp.int32), length
    )
    mid_c = mid_c[None, :, :, None]
    mid_s = mid_s[None, :, :, None]
    data_real, data_imag = (
        data_real * mid_c - data_imag * mid_s,
        data_real * mid_s + data_imag * mid_c,
    )
    inner_c, inner_s = angle_table(
        jnp.arange(inner, dtype=jnp.int32), jnp.arange(inner, dtype=jnp.int32), inner
    )
    return product(inner_c, inner_s, data_real, data_imag, "ab,ecbd->ecad")


def local_inverse(spec_real, spec_imag, freq_index, total):
    pair, outer, inner, width = spec_real.shape
    length = outer * inner
    inner_c, inner_s = angle_table(
        jnp.arange(inner, dtype=jnp.int32), jnp.arange(inner, dtype=jnp.int32), inner
    )
    data_real, data_imag = product(
        inner_c / inner, -inner_s / inner, spec_real, spec_imag, "ab,ecbd->ecad"
    )
    mid_c, mid_s = angle_table(
        jnp.arange(outer, dtype=jnp.int32), jnp.arange(inner, dtype=jnp.int32), length
    )
    mid_c = mid_c[None, :, :, None]
    mid_s = mid_s[None, :, :, None]
    data_real, data_imag = (
        data_real * mid_c + data_imag * mid_s,
        data_imag * mid_c - data_real * mid_s,
    )
    outer_c, outer_s = angle_table(
        jnp.arange(outer, dtype=jnp.int32), jnp.arange(outer, dtype=jnp.int32), outer
    )
    data_real, data_imag = product(
        outer_c / outer, -outer_s / outer, data_real, data_imag, "ab,ebcd->eacd"
    )
    data_real = data_real.reshape(pair, length, width)
    data_imag = data_imag.reshape(pair, length, width)
    cos_t, sin_t = angle_table(freq_index, jnp.arange(length, dtype=jnp.int32), total)
    cos_t = cos_t[:, :, None]
    sin_t = sin_t[:, :, None]
    return (data_real * cos_t + data_imag * sin_t, data_imag * cos_t - data_real * sin_t)


def forward_transform(signal):
    count = lax.axis_size("seq")
    place = lax.axis_index("seq")
    length, width = signal.shape
    total = 2 * count * length
    pieces = lax.all_to_all(
        signal.reshape(count, length // count, width).astype(jnp.bfloat16),
        "seq",
        split_axis=0,
        concat_axis=0,
        tiled=True,
    ).astype(jnp.float32)
    cos_t, sin_t = angle_table(
        jnp.arange(2 * count, dtype=jnp.int32), jnp.arange(count, dtype=jnp.int32), 2 * count
    )
    mixed_real = jnp.einsum("ka,arc->krc", cos_t, pieces, precision=HIGHEST)
    mixed_imag = jnp.einsum("ka,arc->krc", sin_t, pieces, precision=HIGHEST)
    mixed_real, mixed_imag = (
        lax.all_to_all(
            for_sending(mixed_real), "seq", split_axis=0, concat_axis=1, tiled=True
        ).astype(mixed_real.dtype),
        lax.all_to_all(
            for_sending(mixed_imag), "seq", split_axis=0, concat_axis=1, tiled=True
        ).astype(mixed_imag.dtype),
    )
    freq_index = 2 * place + jnp.arange(2, dtype=jnp.int32)
    return (local_forward(mixed_real, mixed_imag, freq_index, total), freq_index)


def inverse_transform(spectrum, freq_index):
    count = lax.axis_size("seq")
    pair, outer, inner, width = spectrum[0].shape
    length = outer * inner
    total = 2 * count * length
    data_real, data_imag = local_inverse(spectrum[0], spectrum[1], freq_index, total)
    part_real, part_imag = (
        lax.all_to_all(
            for_sending(data_real), "seq", split_axis=1, concat_axis=0, tiled=True
        ).astype(data_real.dtype),
        lax.all_to_all(
            for_sending(data_imag), "seq", split_axis=1, concat_axis=0, tiled=True
        ).astype(data_imag.dtype),
    )
    cos_t, sin_t = angle_table(
        jnp.arange(2 * count, dtype=jnp.int32), jnp.arange(count, dtype=jnp.int32), 2 * count
    )
    signal = (
        jnp.einsum("ka,krc->arc", cos_t, part_real, precision=HIGHEST)
        + jnp.einsum("ka,krc->arc", sin_t, part_imag, precision=HIGHEST)
    ) / (2 * count)
    signal = lax.all_to_all(
        for_sending(signal), "seq", split_axis=0, concat_axis=0, tiled=True
    ).astype(signal.dtype)
    return signal.reshape(length, width)


def split_spec(spectrum, width):
    first = (spectrum[0][..., :width], spectrum[1][..., :width])
    second = (spectrum[0][..., width:], spectrum[1][..., width:])
    return (first, second)


def times_spec(left, right):
    return (left[0] * right[0] - left[1] * right[1], left[0] * right[1] + left[1] * right[0])


def conj_times(left, right):
    return (left[0] * right[0] + left[1] * right[1], left[0] * right[1] - left[1] * right[0])


def per_device(queries, values, filt, w_out, cotangent):
    query = queries[0].astype(jnp.float32)
    value = values[0].astype(jnp.float32)
    width = filt.shape[1]
    joined = jnp.concatenate([value, filt], axis=1)
    spectrum, freq_index = forward_transform(joined)
    value_spec, filt_spec = split_spec(spectrum, width)
    conv = inverse_transform(times_spec(value_spec, filt_spec), freq_index)
    gated = (query * conv).astype(jnp.bfloat16)
    partial_sum = jnp.dot(gated, w_out, preferred_element_type=jnp.float32)
    mixed = lax.psum_scatter(
        partial_sum.astype(jnp.bfloat16), "tensor", scatter_dimension=1, tiled=True
    )
    grad_gated = lax.dot_general(
        lax.all_gather(cotangent[0], "tensor", axis=1, tiled=True),
        w_out,
        (((1,), (1,)), ((), ())),
        preferred_element_type=jnp.float32,
    )
    grad_query = (grad_gated * conv).astype(jnp.bfloat16)
    grad_conv = grad_gated * query
    grad_spec = forward_transform(grad_conv)[0]
    back_value = conj_times(filt_spec, grad_spec)
    back_filt = conj_times(value_spec, grad_spec)
    both_spec = (
        jnp.concatenate([back_value[0], back_filt[0]], axis=3),
        jnp.concatenate([back_value[1], back_filt[1]], axis=3),
    )
    result = inverse_transform(both_spec, freq_index)
    grad_value = result[:, :width].astype(jnp.bfloat16)
    grad_filt = lax.psum(result[:, width:].astype(jnp.bfloat16), "dp").astype(jnp.float32)
    return (mixed[None], grad_query[None], grad_value[None], grad_filt)


def solution(mesh):
    placed = (
        P("dp", "seq", "tensor"),
        P("dp", "seq", "tensor"),
        P("seq", "tensor"),
        P("tensor", None),
        P("dp", "seq", "tensor"),
    )
    return jax.shard_map(
        per_device,
        mesh=mesh,
        in_specs=placed,
        out_specs=(
            P("dp", "seq", "tensor"),
            P("dp", "seq", "tensor"),
            P("dp", "seq", "tensor"),
            P("seq", "tensor"),
        ),
        check_vma=False,
    )
```

profile of v0, /device:TPU:1, one launch (start us, length us, event | category | flops | bytes accessed | tf_op | source)
XLA Modules:
  0.0 429.1 jit_solution(16543263097162809174)
XLA Ops:
  7.9 1.0 convert.18
  8.9 0.9 pad_maximum_fusion.6
  9.8 30.7 %all_to_all.128 = bf16[32,16,256]{2,1,0:T(8,128)(2,1)S(1)} all-to-all(bf16[32,16,256]{2,1,0:T(8,128)(2,1)S(1)} %bitcast.303), channel_id=1, replica_groups=mesh['dp'=4,'seq'=32,'tensor'=4] {'seq'}, dimensions={0} | all-to-all | bytes 524288 | tf_op jit(solution)/shard_map/all_to_all | solution.py:106
  41.2 1.1 copy.71
  42.3 5.8 %all-to-all-start.1 = ((bf16[64,16,256]{2,1,0:T(8,128)(2,1)}), bf16[64,16,256]{2,1,0:T(8,128)(2,1)S(1)}, u32[]{:S(2)}, u32[]{:S(2)}) async-start(bf16[64,16,256]{2,1,0:T(8,128)(2,1)} %copy.71), calls=%async_computation.1 | async-start | bytes 1048576 | tf_op jit(solution)/shard_map/all_to_all | solution.py:119
  48.8 1.1 copy.74
  49.9 14.1 %all-to-all-done.1 = bf16[64,16,256]{2,1,0:T(8,128)(2,1)S(1)} async-done(((bf16[64,16,256]{2,1,0:T(8,128)(2,1)}), bf16[64,16,256]{2,1,0:T(8,128)(2,1)S(1)}, u32[]{:S(2)}, u32[]{:S(2)}) %all-to-all-start.1) | async-done | bytes 524320 | tf_op jit(solution)/shard_map/all_to_all | solution.py:119
  64.0 9.6 %all-to-all-start.2 = ((bf16[64,16,256]{2,1,0:T(8,128)(2,1)}), bf16[64,16,256]{2,1,0:T(8,128)(2,1)}, u32[]{:S(2)}, u32[]{:S(2)}) async-start(bf16[64,16,256]{2,1,0:T(8,128)(2,1)} %copy.74), calls=%async_computation.2 | async-start | bytes 1048576 | tf_op jit(solution)/shard_map/all_to_all | solution.py:122
  74.3 15.0 %all-to-all-done.2 = bf16[64,16,256]{2,1,0:T(8,128)(2,1)} async-done(((bf16[64,16,256]{2,1,0:T(8,128)(2,1)}), bf16[64,16,256]{2,1,0:T(8,128)(2,1)}, u32[]{:S(2)}, u32[]{:S(2)}) %all-to-all-start.2) | async-done | bytes 524320 | tf_op jit(solution)/shard_map/all_to_all | solution.py:122
  89.3 1.2 convert.22
  90.5 2.4 fusion.61
  92.9 2.4 fusion.65
  95.2 2.4 fusion.7
  97.7 3.8 multiply_subtract_fusion
  101.5 4.3 fusion.58
  105.8 9.8 %all-to-all-start.6 = ((bf16[32,16,128]{2,1,0:T(8,128)(2,1)}), bf16[32,16,128]{2,1,0:T(8,128)(2,1)S(1)}, u32[]{:S(2)}, u32[]{:S(2)}) async-start(bf16[32,16,128]{2,1,0:T(8,128)(2,1)} %bitcast.55), calls=%async_computation.7 | async-start | bytes 262144 | tf_op jit(solution)/shard_map/all_to_all | solution.py:106
  115.6 2.6 fusion.34
  118.2 9.6 %all-to-all-done.6 = bf16[32,16,128]{2,1,0:T(8,128)(2,1)S(1)} async-done(((bf16[32,16,128]{2,1,0:T(8,128)(2,1)}), bf16[32,16,128]{2,1,0:T(8,128)(2,1)S(1)}, u32[]{:S(2)}, u32[]{:S(2)}) %all-to-all-start.6) | async-done | bytes 131104 | tf_op jit(solution)/shard_map/all_to_all | solution.py:106
  129.2 4.6 %all-to-all-start.7 = ((bf16[64,16,128]{2,1,0:T(8,128)(2,1)}), bf16[64,16,128]{2,1,0:T(8,128)(2,1)}, u32[]{:S(2)}, u32[]{:S(2)}) async-start(bf16[64,16,128]{2,1,0:T(8,128)(2,1)} %copy.96), calls=%async_computation.8 | async-start | bytes 524288 | tf_op jit(solution)/shard_map/all_to_all | solution.py:119
  133.9 3.8 fusion.5
  139.1 8.6 %all-to-all-done.7 = bf16[64,16,128]{2,1,0:T(8,128)(2,1)} async-done(((bf16[64,16,128]{2,1,0:T(8,128)(2,1)}), bf16[64,16,128]{2,1,0:T(8,128)(2,1)}, u32[]{:S(2)}, u32[]{:S(2)}) %all-to-all-start.7) | async-done | bytes 262176 | tf_op jit(solution)/shard_map/all_to_all | solution.py:119
  147.7 5.8 %all-to-all-start.8 = ((bf16[64,16,128]{2,1,0:T(8,128)(2,1)}), bf16[64,16,128]{2,1,0:T(8,128)(2,1)S(1)}, u32[]{:S(2)}, u32[]{:S(2)}) async-start(bf16[64,16,128]{2,1,0:T(8,128)(2,1)} %copy.99), calls=%async_computation.9 | async-start | bytes 524288 | tf_op jit(solution)/shard_map/all_to_all | solution.py:122
  153.5 1.6 fusion.30
  155.1 1.6 fusion.4
  156.8 1.0 convert.23
  157.8 9.4 %all-to-all-done.8 = bf16[64,16,128]{2,1,0:T(8,128)(2,1)S(1)} async-done(((bf16[64,16,128]{2,1,0:T(8,128)(2,1)}), bf16[64,16,128]{2,1,0:T(8,128)(2,1)S(1)}, u32[]{:S(2)}, u32[]{:S(2)}) %all-to-all-start.8) | async-done | bytes 262176 | tf_op jit(solution)/shard_map/all_to_all | solution.py:122
  167.2 1.3 fusion.72
  168.5 1.3 fusion.76
  169.8 1.3 fusion.12
  171.1 1.4 multiply_subtract_fusion.3
  172.6 0.9 fusion.48
  173.5 0.9 fusion.44
  174.4 0.9 fusion.9
  175.3 1.4 multiply_subtract_fusion.2
  177.4 1.1 fusion.36
  178.4 1.1 fusion.37
  179.5 1.1 convolution_add_fusion.1
  180.6 1.4 add_bitcast_fusion
  182.0 1.7 fusion.28
  183.7 1.7 fusion.24
  185.4 1.7 fusion.3
  187.2 1.9 fusion.2
  190.4 1.1 fusion.21
  191.5 1.4 copy.116
  192.9 5.8 %all-to-all-start.10 = ((bf16[2,512,256]{2,0,1:T(2,128)(2,1)}), bf16[2,512,256]{2,0,1:T(2,128)(2,1)S(1)}, u32[]{:S(2)}, u32[]{:S(2)}) async-start(bf16[2,512,256]{2,0,1:T(2,128)(2,1)} %copy.116), calls=%async_computation.11 | async-start | bytes 1048576 | tf_op jit(solution)/shard_map/all_to_all | solution.py:140
  198.7 2.4 copy.113
  203.8 10.6 %all-to-all-done.10 = bf16[2,512,256]{2,0,1:T(2,128)(2,1)S(1)} async-done(((bf16[2,512,256]{2,0,1:T(2,128)(2,1)}), bf16[2,512,256]{2,0,1:T(2,128)(2,1)S(1)}, u32[]{:S(2)}, u32[]{:S(2)}) %all-to-all-start.10) | async-done | bytes 524320 | tf_op jit(solution)/shard_map/all_to_all | solution.py:140
  214.5 9.3 %all-to-all-start.9 = ((bf16[2,512,256]{2,0,1:T(2,128)(2,1)}), bf16[2,512,256]{2,0,1:T(2,128)(2,1)}, u32[]{:S(2)}, u32[]{:S(2)}) async-start(bf16[2,512,256]{2,0,1:T(2,128)(2,1)} %copy.113), calls=%async_computation.10 | async-start | bytes 1048576 | tf_op jit(solution)/shard_map/all_to_all | solution.py:137
  227.1 1.0 copy.91
  228.1 11.6 %all-to-all-done.9 = bf16[2,512,256]{2,0,1:T(2,128)(2,1)} async-done(((bf16[2,512,256]{2,0,1:T(2,128)(2,1)}), bf16[2,512,256]{2,0,1:T(2,128)(2,1)}, u32[]{:S(2)}, u32[]{:S(2)}) %all-to-all-start.9) | async-done | bytes 524320 | tf_op jit(solution)/shard_map/all_to_all | solution.py:137
  239.7 9.6 %all-to-all-start.4 = ((bf16[2,512,128]{2,0,1:T(2,128)(2,1)}), bf16[2,512,128]{2,0,1:T(2,128)(2,1)S(1)}, u32[]{:S(2)}, u32[]{:S(2)}) async-start(bf16[2,512,128]{2,0,1:T(2,128)(2,1)} %copy.91), calls=%async_computation.4 | async-start | bytes 524288 | tf_op jit(solution)/shard_map/all_to_all | solution.py:140
  249.3 1.0 copy.88
  251.1 1.1 copy.114
  253.0 9.8 %all-to-all-done.4 = bf16[2,512,128]{2,0,1:T(2,128)(2,1)S(1)} async-done(((bf16[2,512,128]{2,0,1:T(2,128)(2,1)}), bf16[2,512,128]{2,0,1:T(2,128)(2,1)S(1)}, u32[]{:S(2)}, u32[]{:S(2)}) %all-to-all-start.4) | async-done | bytes 262176 | tf_op jit(solution)/shard_map/all_to_all | solution.py:140
  262.8 5.8 %all-to-all-start.3 = ((bf16[2,512,128]{2,0,1:T(2,128)(2,1)}), bf16[2,512,128]{2,0,1:T(2,128)(2,1)S(1)}, u32[]{:S(2)}, u32[]{:S(2)}) async-start(bf16[2,512,128]{2,0,1:T(2,128)(2,1)} %copy.88), calls=%async_computation.3 | async-start | bytes 524288 | tf_op jit(solution)/shard_map/all_to_all | solution.py:137
  270.4 11.9 %all-to-all-done.3 = bf16[2,512,128]{2,0,1:T(2,128)(2,1)S(1)} async-done(((bf16[2,512,128]{2,0,1:T(2,128)(2,1)}), bf16[2,512,128]{2,0,1:T(2,128)(2,1)S(1)}, u32[]{:S(2)}, u32[]{:S(2)}) %all-to-all-start.3) | async-done | bytes 262176 | tf_op jit(solution)/shard_map/all_to_all | solution.py:137
  282.3 5.8 %all-to-all-start.11 = ((bf16[32,16,256]{2,1,0:T(8,128)(2,1)}), bf16[32,16,256]{2,1,0:T(8,128)(2,1)S(1)}, u32[]{:S(2)}, u32[]{:S(2)}) async-start(bf16[32,16,256]{2,1,0:T(8,128)(2,1)} %copy.119), calls=%async_computation.12 | async-start | bytes 524288 | tf_op jit(solution)/shard_map/all_to_all | solution.py:151
  290.2 11.6 %all-to-all-done.11 = bf16[32,16,256]{2,1,0:T(8,128)(2,1)S(1)} async-done(((bf16[32,16,256]{2,1,0:T(8,128)(2,1)}), bf16[32,16,256]{2,1,0:T(8,128)(2,1)S(1)}, u32[]{:S(2)}, u32[]{:S(2)}) %all-to-all-start.11) | async-done | bytes 262176 | tf_op jit(solution)/shard_map/all_to_all | solution.py:151
  301.8 5.8 %all-to-all-start.5 = ((bf16[32,16,128]{2,1,0:T(8,128)(2,1)}), bf16[32,16,128]{2,1,0:T(8,128)(2,1)S(1)}, u32[]{:S(2)}, u32[]{:S(2)}) async-start(bf16[32,16,128]{2,1,0:T(8,128)(2,1)} %copy.94), calls=%async_computation.5 | async-start | bytes 262144 | tf_op jit(solution)/shard_map/all_to_all | solution.py:151
  308.4 11.5 %all-to-all-done.5 = bf16[32,16,128]{2,1,0:T(8,128)(2,1)S(1)} async-done(((bf16[32,16,128]{2,1,0:T(8,128)(2,1)}), bf16[32,16,128]{2,1,0:T(8,128)(2,1)S(1)}, u32[]{:S(2)}, u32[]{:S(2)}) %all-to-all-start.5) | async-done | bytes 131104 | tf_op jit(solution)/shard_map/all_to_all | solution.py:151
  320.0 3.2 convolution_convert_fusion
  323.9 41.7 %all-reduce.2.cloned.1.call-done = bf16[512,128]{1,0:T(8,128)(2,1)} async-done(((bf16[512,128]{1,0:T(8,128)(2,1)}), bf16[512,128]{1,0:T(8,128)(2,1)}) %all-reduce.2.cloned.1.call-update) | async-done | bytes 131088 | tf_op jit(solution)/shard_map/psum | solution.py:201
  365.7 1.6 convert_element_type.305
  367.3 55.0 %reduce-scatter.2.cloned.1.call-done = bf16[512,1024]{1,0:T(8,128)(2,1)} async-done(((bf16[512,4096]{1,0:T(8,128)(2,1)}), bf16[512,1024]{1,0:T(8,128)(2,1)}) %reduce-scatter.2.cloned.1.call-update) | async-done | bytes 1048592 | tf_op jit(solution)/shard_map/reduce_scatter | solution.py:181
  (64 shorter events, 20.3 us)
Async XLA Ops:
  7.2 94.4 %copy-start = (bf16[128,4096]{1,0:T(8,128)(2,1)S(1)}, bf16[128,4096]{1,0:T(8,128)(2,1)}, u32[]{:S(2)}) copy-start(bf16[128,4096]{1,0:T(8,128)(2,1)} %param.8) | copy-start | bytes 3145732
  7.2 94.3 %all-gather.3.cloned.1.call-start = ((), (), s32[]{:S(2)}) async-start(), calls=%async_computation.15 | async-start | bytes 5242880 | tf_op jit(solution)/shard_map/all_gather | solution.py:185
  42.3 21.7 %all-to-all-start.1 = ((bf16[64,16,256]{2,1,0:T(8,128)(2,1)}), bf16[64,16,256]{2,1,0:T(8,128)(2,1)S(1)}, u32[]{:S(2)}, u32[]{:S(2)}) async-start(bf16[64,16,256]{2,1,0:T(8,128)(2,1)} %copy.71), calls=%async_computation.1 | async-start | bytes 1048576 | tf_op jit(solution)/shard_map/all_to_all | solution.py:119
  64.0 25.3 %all-to-all-start.2 = ((bf16[64,16,256]{2,1,0:T(8,128)(2,1)}), bf16[64,16,256]{2,1,0:T(8,128)(2,1)}, u32[]{:S(2)}, u32[]{:S(2)}) async-start(bf16[64,16,256]{2,1,0:T(8,128)(2,1)} %copy.74), calls=%async_computation.2 | async-start | bytes 1048576 | tf_op jit(solution)/shard_map/all_to_all | solution.py:122
  97.7 3.9 copy-start.4
  101.5 32.4 %copy-start.1 = (f32[2,32,16,256]{3,1,2,0:T(8,128)S(1)}, f32[2,32,16,256]{3,1,2,0:T(8,128)}, u32[]{:S(2)}) copy-start(f32[2,32,16,256]{3,1,2,0:T(8,128)} %get-tuple-element.11) | copy-start | bytes 3145732
  105.8 22.0 %all-to-all-start.6 = ((bf16[32,16,128]{2,1,0:T(8,128)(2,1)}), bf16[32,16,128]{2,1,0:T(8,128)(2,1)S(1)}, u32[]{:S(2)}, u32[]{:S(2)}) async-start(bf16[32,16,128]{2,1,0:T(8,128)(2,1)} %bitcast.55), calls=%async_computation.7 | async-start | bytes 262144 | tf_op jit(solution)/shard_map/all_to_all | solution.py:106
  129.2 18.4 %all-to-all-start.7 = ((bf16[64,16,128]{2,1,0:T(8,128)(2,1)}), bf16[64,16,128]{2,1,0:T(8,128)(2,1)}, u32[]{:S(2)}, u32[]{:S(2)}) async-start(bf16[64,16,128]{2,1,0:T(8,128)(2,1)} %copy.96), calls=%async_computation.8 | async-start | bytes 524288 | tf_op jit(solution)/shard_map/all_to_all | solution.py:119
  147.7 19.5 %all-to-all-start.8 = ((bf16[64,16,128]{2,1,0:T(8,128)(2,1)}), bf16[64,16,128]{2,1,0:T(8,128)(2,1)S(1)}, u32[]{:S(2)}, u32[]{:S(2)}) async-start(bf16[64,16,128]{2,1,0:T(8,128)(2,1)} %copy.99), calls=%async_computation.9 | async-start | bytes 524288 | tf_op jit(solution)/shard_map/all_to_all | solution.py:122
  169.8 5.5 %copy-start.2 = (f32[2,32,16,256]{3,2,1,0:T(8,128)S(1)}, f32[2,32,16,256]{3,2,1,0:T(8,128)}, u32[]{:S(2)}) copy-start(f32[2,32,16,256]{3,2,1,0:T(8,128)} %fusion.5) | copy-start | bytes 3145732
  192.9 21.6 %all-to-all-start.10 = ((bf16[2,512,256]{2,0,1:T(2,128)(2,1)}), bf16[2,512,256]{2,0,1:T(2,128)(2,1)S(1)}, u32[]{:S(2)}, u32[]{:S(2)}) async-start(bf16[2,512,256]{2,0,1:T(2,128)(2,1)} %copy.116), calls=%async_computation.11 | async-start | bytes 1048576 | tf_op jit(solution)/shard_map/all_to_all | solution.py:140
  214.5 25.2 %all-to-all-start.9 = ((bf16[2,512,256]{2,0,1:T(2,128)(2,1)}), bf16[2,512,256]{2,0,1:T(2,128)(2,1)}, u32[]{:S(2)}, u32[]{:S(2)}) async-start(bf16[2,512,256]{2,0,1:T(2,128)(2,1)} %copy.113), calls=%async_computation.10 | async-start | bytes 1048576 | tf_op jit(solution)/shard_map/all_to_all | solution.py:137
  239.7 23.1 %all-to-all-start.4 = ((bf16[2,512,128]{2,0,1:T(2,128)(2,1)}), bf16[2,512,128]{2,0,1:T(2,128)(2,1)S(1)}, u32[]{:S(2)}, u32[]{:S(2)}) async-start(bf16[2,512,128]{2,0,1:T(2,128)(2,1)} %copy.91), calls=%async_computation.4 | async-start | bytes 524288 | tf_op jit(solution)/shard_map/all_to_all | solution.py:140
  253.0 67.0 %copy-start.5 = (bf16[1,512,128]{2,1,0:T(8,128)(2,1)S(1)}, bf16[1,512,128]{2,1,0:T(8,128)(2,1)}, u32[]{:S(2)}) copy-start(bf16[1,512,128]{2,1,0:T(8,128)(2,1)} %param.5) | copy-start | bytes 393220
  262.8 19.5 %all-to-all-start.3 = ((bf16[2,512,128]{2,0,1:T(2,128)(2,1)}), bf16[2,512,128]{2,0,1:T(2,128)(2,1)S(1)}, u32[]{:S(2)}, u32[]{:S(2)}) async-start(bf16[2,512,128]{2,0,1:T(2,128)(2,1)} %copy.88), calls=%async_computation.3 | async-start | bytes 524288 | tf_op jit(solution)/shard_map/all_to_all | solution.py:137
  282.3 19.5 %all-to-all-start.11 = ((bf16[32,16,256]{2,1,0:T(8,128)(2,1)}), bf16[32,16,256]{2,1,0:T(8,128)(2,1)S(1)}, u32[]{:S(2)}, u32[]{:S(2)}) async-start(bf16[32,16,256]{2,1,0:T(8,128)(2,1)} %copy.119), calls=%async_computation.12 | async-start | bytes 524288 | tf_op jit(solution)/shard_map/all_to_all | solution.py:151
  301.8 18.2 %all-to-all-start.5 = ((bf16[32,16,128]{2,1,0:T(8,128)(2,1)}), bf16[32,16,128]{2,1,0:T(8,128)(2,1)S(1)}, u32[]{:S(2)}, u32[]{:S(2)}) async-start(bf16[32,16,128]{2,1,0:T(8,128)(2,1)} %copy.94), calls=%async_computation.5 | async-start | bytes 262144 | tf_op jit(solution)/shard_map/all_to_all | solution.py:151
  307.6 58.1 %all-reduce.2.cloned.1.call-start = ((), (), s32[]{:S(2)}) async-start(), calls=%async_computation.14 | async-start | bytes 262144 | tf_op jit(solution)/shard_map/psum | solution.py:201
  308.4 113.9 %reduce-scatter.2.cloned.1.call-start = ((), (), s32[]{:S(2)}) async-start(), calls=%async_computation.13 | async-start | bytes 5242880 | tf_op jit(solution)/shard_map/reduce_scatter | solution.py:181
  320.0 3.3 copy-start.3
Sparse Core Ops, SparseCore 0:
  10.1 59.0 all-gather.2
  311.4 54.2 all-reduce.1
  369.3 52.8 reduce-scatter.1
where the time goes:
time: 433 us; the launch traced here: 429 us
  waiting for transfers between devices  221 us (51%)
  starting transfers between devices  78.1 us (18%)
  matrix products  59 us (14%)
  blocking collectives  30.7 us (7%)
  local copies, waits for them, and re-layouts  17.2 us (4%)
  between operations  14.6 us (3%)
  other arithmetic  8.43 us (2%)
    reduce_scatter x1, waiting for transfers between devices, per_device(): lax.psum_scatter(partial_sum.astype(jnp.bfloat16), 'tensor', scatter_dime...  55 us
    dot_general x32, matrix products, apply(): return jnp.einsum(form, left, right, precision=HIGHEST)  47.5 us
    psum x1, waiting for transfers between devices, per_device(): lax.psum(result[:, width:].astype(jnp.bfloat16), 'dp').astype(jnp.float32)  41.7 us
    all_to_all x1, blocking collectives, forward_transform(): lax.all_to_all(signal.reshape(count, length // count, width).astype(jnp.b...  30.7 us
    all_to_all x2, waiting for transfers between devices, forward_transform(): lax.all_to_all(for_sending(mixed_imag), 'seq', split_axis=0, concat_axis=...  24.4 us
    all_to_all x2, waiting for transfers between devices, inverse_transform(): lax.all_to_all(for_sending(data_real), 'seq', split_axis=1, concat_axis=0...  23.5 us
    all_to_all x2, waiting for transfers between devices, inverse_transform(): lax.all_to_all(for_sending(signal), 'seq', split_axis=0, concat_axis=0, t...  23.1 us
    all_to_all x2, waiting for transfers between devices, forward_transform(): lax.all_to_all(for_sending(mixed_real), 'seq', split_axis=0, concat_axis=...  22.7 us
  transfers between devices with their start and end apart: 14, of which 13 were waited for; matrix products, arithmetic and copies ran while one was open for 12% of the time, Pallas kernels for 0%

commit v1 on v0

v1 whole, which is shorter than its diff:
```python
import functools
import math

import jax
import jax.numpy as jnp
import ml_dtypes
import numpy as np
from jax import lax
from jax.experimental import pallas as pl
from jax.experimental.pallas import tpu as pltpu
from jax.sharding import PartitionSpec as P

F32 = jnp.float32
BF16 = jnp.bfloat16
DP = 4
SEQ = 32
ROWS = 4
LANES = 128
SLOTS = 8
HALF = 128


def halves(table):
    high = table.astype(ml_dtypes.bfloat16)
    low = (table - high.astype(np.float64)).astype(ml_dtypes.bfloat16)
    return np.stack([high, low])


@functools.cache
def tables():
    coarse = np.arange(HALF) + 0.5
    row = np.arange(SEQ * SLOTS)
    place = row // SLOTS * ROWS + row % SLOTS % ROWS
    angle = 2 * math.pi / 256 * coarse[:, None] * place[None, :]
    full = np.concatenate([np.cos(angle), -np.sin(angle)])
    first = np.where(row[None, :] % SLOTS < ROWS, full, 0.0)
    second = full - first
    fine = np.arange(LANES)
    angle = 2 * math.pi / LANES * np.outer(fine, fine)
    cos, sin = np.cos(angle), np.sin(angle)
    inner = np.block([[cos, -sin], [sin, cos]])
    angle = 2 * math.pi / 32768 * np.outer(coarse, fine)
    twist = np.stack([np.cos(angle), np.sin(angle)]).astype(np.float32)
    spread = np.zeros((256, 256))
    for channel in range(32):
        for slot in range(SLOTS):
            spread[channel * SLOTS + slot, slot * 32 + channel] = 1.0
    return {
        "fwd_first": halves(first),
        "fwd_second": halves(second),
        "inv_first": halves(first.T / 16384),
        "inv_second": halves(second.T / 16384),
        "inner": halves(inner),
        "inner_t": halves(inner.T),
        "twist": twist,
        "spread": spread.astype(ml_dtypes.bfloat16),
    }


def dot(left, right):
    return jnp.dot(left, right, preferred_element_type=F32)


def split(x):
    high = x.astype(BF16)
    return high, (x - high.astype(F32)).astype(BF16)


def table_dot(table_ref, high, low=None):
    out = dot(table_ref[0], high) + dot(table_ref[1], high)
    if low is not None:
        out = out + dot(table_ref[0], low)
    return out


def dot_table(x, table_ref):
    high, low = split(x)
    return dot(high, table_ref[0]) + dot(low, table_ref[0]) + dot(high, table_ref[1])


def forward(rows, outer_ref, inner_ref, twist_ref):
    coarse = table_dot(outer_ref, rows)
    real, imag = coarse[:HALF], coarse[HALF:]
    cos, sin = twist_ref[0], twist_ref[1]
    turned = jnp.concatenate([real * cos + imag * sin, imag * cos - real * sin], axis=1)
    return dot_table(turned, inner_ref)


def inverse_inner(real, imag, inner_t_ref, twist_ref):
    coarse = dot_table(jnp.concatenate([real, imag], axis=1), inner_t_ref)
    real, imag = coarse[:, :LANES], coarse[:, LANES:]
    cos, sin = twist_ref[0], twist_ref[1]
    return split(jnp.concatenate([real * cos - imag * sin, imag * cos + real * sin], axis=0))


def pack_inputs(values_ref, filt_ref, spread_ref, out_ref):
    dp = lax.axis_index("dp")
    start = pl.multiple_of(dp * LANES, LANES)
    quarter = filt_ref[pl.ds(start, LANES), :].T
    tiles = [values_ref[q * LANES:(q + 1) * LANES, :].astype(F32).T.astype(BF16) for q in range(ROWS)]
    tiles += [jnp.where(dp == q, quarter, 0.0).astype(BF16) for q in range(DP)]
    for part in range(4):
        block = jnp.concatenate([tile[part * 32:(part + 1) * 32] for tile in tiles], axis=0)
        out_ref[part * 256:(part + 1) * 256, :] = dot(spread_ref[...], block).astype(BF16)


def convolve(got_ref, first_ref, second_ref, inv_ref, inner_ref, inner_t_ref, twist_ref, conv_ref, vspec_ref, fspec_ref):
    size = SEQ * SLOTS
    parts = [got_ref[b * size:(b + 1) * size, :] for b in range(DP)]
    filt = ((parts[0].astype(F32) + parts[1].astype(F32)) + (parts[2].astype(F32) + parts[3].astype(F32))).astype(BF16)
    fspec = forward(filt, second_ref, inner_ref, twist_ref)
    fspec_ref[...] = fspec
    f_real, f_imag = fspec[:, :LANES], fspec[:, LANES:]
    for b in range(DP):
        vspec = forward(parts[b], first_ref, inner_ref, twist_ref)
        vspec_ref[b] = vspec
        v_real, v_imag = vspec[:, :LANES], vspec[:, LANES:]
        high, low = inverse_inner(
            v_real * f_real - v_imag * f_imag, v_real * f_imag + v_imag * f_real, inner_t_ref, twist_ref
        )
        conv_ref[b * size:(b + 1) * size, :] = table_dot(inv_ref, high, low).astype(BF16)


def partial_grads(cot_ref, *refs):
    count = len(refs) // 2
    cot = cot_ref[...]
    for w_ref, out_ref in zip(refs[:count], refs[count:]):
        out_ref[...] = lax.dot_general(
            cot, w_ref[...], (((1,), (1,)), ((), ())), preferred_element_type=F32
        ).astype(BF16)


def pack_grads(*refs):
    query_ref, conv_ref, spread_ref = refs[:3]
    pieces, (out_ref, grad_ref) = refs[3:-2], refs[-2:]
    grad = pieces[0][...].astype(F32)
    for piece in pieces[1:]:
        grad = grad + piece[...].astype(F32)
    grad_ref[...] = grad
    grad_conv = grad * query_ref[...].astype(F32)
    tiles = [grad_conv[q * LANES:(q + 1) * LANES, :].T.astype(BF16) for q in range(ROWS)]
    spread = spread_ref[:, 128:]
    for part in range(4):
        block = jnp.concatenate([tile[part * 32:(part + 1) * 32] for tile in tiles], axis=0)
        out_ref[part * 256:(part + 1) * 256, :] = (
            dot(spread, block) + conv_ref[part * 256:(part + 1) * 256, :].astype(F32)
        ).astype(BF16)


def gather_half(got_ref, gather):
    blocks = [dot(gather, got_ref[part * 256:(part + 1) * 256, :]) for part in range(4)]
    return [
        jnp.concatenate([block[q * 32:(q + 1) * 32] for block in blocks], axis=0).T for q in range(gather.shape[0] // 32)
    ]


def unpack_conv(got_ref, query_ref, grad_ref, gather_ref, gated_ref, grad_query_ref):
    for q, conv in enumerate(gather_half(got_ref, gather_ref[:128, :])):
        rows = slice(q * LANES, (q + 1) * LANES)
        gated_ref[rows, :] = (query_ref[rows, :].astype(F32) * conv).astype(BF16)
        grad_query_ref[rows, :] = (grad_ref[rows, :] * conv).astype(BF16)


def correlate(
    got_ref, vspec_ref, fspec_ref, second_ref, inv_first_ref, inv_second_ref, inner_ref, inner_t_ref, twist_ref, out_ref
):
    size = SEQ * SLOTS
    f_real, f_imag = fspec_ref[:, :LANES], fspec_ref[:, LANES:]
    sum_real = sum_imag = None
    inner = []
    for b in range(DP):
        spec = forward(got_ref[b * size:(b + 1) * size, :], second_ref, inner_ref, twist_ref)
        real, imag = spec[:, :LANES], spec[:, LANES:]
        v_real, v_imag = vspec_ref[b, :, :LANES], vspec_ref[b, :, LANES:]
        part_real = real * v_real + imag * v_imag
        part_imag = imag * v_real - real * v_imag
        sum_real = part_real if b == 0 else sum_real + part_real
        sum_imag = part_imag if b == 0 else sum_imag + part_imag
        inner.append(
            inverse_inner(
                real * f_real + imag * f_imag, imag * f_real - real * f_imag, inner_t_ref, twist_ref
            )
        )
    filt = table_dot(inv_second_ref, *inverse_inner(sum_real, sum_imag, inner_t_ref, twist_ref))
    for b in range(DP):
        out_ref[b * size:(b + 1) * size, :] = (table_dot(inv_first_ref, *inner[b]) + filt).astype(BF16)


def unpack_grads(got_ref, gather_ref, value_ref, filt_ref):
    tiles = gather_half(got_ref, gather_ref[...])
    for q in range(ROWS):
        value_ref[q * LANES:(q + 1) * LANES, :] = tiles[q].astype(BF16)
        filt_ref[q * LANES:(q + 1) * LANES, :] = tiles[ROWS + q]


def project(*refs):
    out_ref = refs[-1]
    count = (len(refs) - 1) // 2
    total = dot(refs[0][...], refs[count][...])
    for k in range(1, count):
        total = total + dot(refs[k][...], refs[count + k][...])
    out_ref[...] = total.astype(BF16)


def call(kernel, outs, *operands):
    single = not isinstance(outs, list)
    return pl.pallas_call(
        kernel,
        out_shape=outs if not single else outs,
        name=kernel.__name__,
        compiler_params=pltpu.CompilerParams(vmem_limit_bytes=40 * 1024 * 1024),
    )(*operands)


def exchange(message):
    shape = message.shape
    message = message.reshape(DP * SEQ, SLOTS, LANES)
    return lax.all_to_all(message, ("dp", "seq"), split_axis=0, concat_axis=0, tiled=True).reshape(shape)


def shifted(array, distance, count):
    return lax.ppermute(array, "tensor", [(i, (i + distance) % count) for i in range(count)])


def per_device(queries, values, filt, w_out, cotangent, count):
    t = tables()
    query = queries[0]
    length, width = query.shape
    features = cotangent.shape[2]
    rank = lax.axis_index("tensor")
    message = jax.ShapeDtypeStruct((DP * SEQ * SLOTS, LANES), BF16)
    signal = jax.ShapeDtypeStruct((length, width), BF16)

    columns = []
    for d in range(count):
        piece = lax.dynamic_slice(w_out, (0, (rank + d) % count * features), (width, features))
        columns.append(shifted(piece, d, count) if d else piece)

    got = exchange(call(pack_inputs, message, values[0], filt, t["spread"]))
    conv, value_spec, filt_spec = call(
        convolve,
        [
            message,
            jax.ShapeDtypeStruct((DP, HALF, 2 * LANES), F32),
            jax.ShapeDtypeStruct((HALF, 2 * LANES), F32),
        ],
        got, t["fwd_first"], t["fwd_second"], t["inv_first"], t["inner"], t["inner_t"], t["twist"],
    )
    partial = call(partial_grads, [signal] * count, cotangent[0], *columns)
    partial = [shifted(p, -d, count) if d else p for d, p in enumerate(partial)]
    outgoing, grad_gated = call(
        pack_grads, [message, jax.ShapeDtypeStruct((length, width), F32)], query, conv, t["spread"], *partial
    )
    got = exchange(outgoing)
    gated, grad_query = call(unpack_conv, [signal, signal], got, query, grad_gated, t["spread"].T)
    gathered = [shifted(gated, d, count) if d else gated for d in range(count)]
    got = exchange(
        call(
            correlate, message, got, value_spec, filt_spec, t["fwd_second"], t["inv_first"], t["inv_second"],
            t["inner"], t["inner_t"], t["twist"],
        )
    )
    grad_value, grad_filt = call(
        unpack_grads, [signal, jax.ShapeDtypeStruct((length, width), F32)], got, t["spread"].T
    )
    mixed = call(project, jax.ShapeDtypeStruct((length, features), BF16), *gathered, *columns)
    return (mixed[None], grad_query[None], grad_value[None], grad_filt)


def solution(mesh):
    placed = (
        P("dp", "seq", "tensor"),
        P("dp", "seq", "tensor"),
        P("seq", "tensor"),
        P("tensor", None),
        P("dp", "seq", "tensor"),
    )
    return jax.shard_map(
        functools.partial(per_device, count=mesh.shape["tensor"]),
        mesh=mesh,
        in_specs=placed,
        out_specs=(
            P("dp", "seq", "tensor"),
            P("dp", "seq", "tensor"),
            P("dp", "seq", "tensor"),
            P("seq", "tensor"),
        ),
        check_vma=False,
    )
```

time: 433 us -> 117 us (0.27)
  waiting for transfers between devices: 221 us -> 17.9 us
  matrix products: 59 us -> 0 us
  starting transfers between devices: 78.1 us -> 50.9 us
  Pallas kernels: 0 us -> 14.3 us
  local copies, waits for them, and re-layouts: 17.2 us -> 2.91 us
  between operations: 14.6 us -> 0.98 us
  other arithmetic: 8.43 us -> 0 us
    all_to_all x11 -> x2, waiting for transfers between devices: 124 us -> 0.01 us  [exchange(): lax.all_to_all(message, ('dp', 'seq'), split_axis=0, concat_axis=0, tiled...]
    dot_general x42 -> x0, matrix products: 59 us -> none  [the longest x32 47.5 us: apply(): return jnp.einsum(form, left, right, precision=HIGHEST)]
    reduce_scatter x1 -> x0, waiting for transfers between devices: 55 us -> none  [per_device(): lax.psum_scatter(partial_sum.astype(jnp.bfloat16), 'tensor', scatter_dime...]
    all_to_all x11 -> x2, starting transfers between devices: 78 us -> 24.6 us  [exchange(): lax.all_to_all(message, ('dp', 'seq'), split_axis=0, concat_axis=0, tiled...]
    psum x1 -> x0, waiting for transfers between devices: 41.7 us -> none  [per_device(): lax.psum(result[:, width:].astype(jnp.bfloat16), 'dp').astype(jnp.float32)]
    ppermute x0 -> x9, starting transfers between devices: none -> 26.3 us  [shifted(): lax.ppermute(array, 'tensor', [(i, (i + distance) % count) for i in range...]
    ppermute x0 -> x9, waiting for transfers between devices: none -> 17.9 us  [shifted(): lax.ppermute(array, 'tensor', [(i, (i + distance) % count) for i in range...]
    pallas_call x0 -> x8, Pallas kernels: none -> 14.3 us  [call(): pl.pallas_call(kernel, out_shape=outs if not single else outs, name=kerne...]
  transfers between devices with their start and end apart: 14 -> 11, of which waited for: 13 -> 5; matrix products, arithmetic and copies ran while one was open for 12% -> 0% of each run, Pallas kernels for 0% -> 7%
where the time goes in v1:
time: 117 us
  starting transfers between devices  50.9 us (44%)
  blocking collectives  29.9 us (26%)
  waiting for transfers between devices  17.9 us (15%)
  Pallas kernels  14.3 us (12%)
  local copies, waits for them, and re-layouts  2.91 us (2%)
    all_to_all x1, blocking collectives, exchange(): lax.all_to_all(message, ('dp', 'seq'), split_axis=0, concat_axis=0, tiled...  29.9 us
    ppermute x9, starting transfers between devices, shifted(): lax.ppermute(array, 'tensor', [(i, (i + distance) % count) for i in range...  26.3 us
    all_to_all x2, starting transfers between devices, exchange(): lax.all_to_all(message, ('dp', 'seq'), split_axis=0, concat_axis=0, tiled...  24.6 us
    ppermute x9, waiting for transfers between devices, shifted(): lax.ppermute(array, 'tensor', [(i, (i + distance) % count) for i in range...  17.9 us
    pallas_call x8, Pallas kernels, call(): pl.pallas_call(kernel, out_shape=outs if not single else outs, name=kerne...  14.3 us
    unnamed x30, local copies, waits for them, and re-layouts  2.82 us
  transfers between devices with their start and end apart: 11, of which 5 were waited for; matrix products, arithmetic and copies ran while one was open for 0% of the time, Pallas kernels for 7%

profile of v1, /device:TPU:1, one launch (start us, length us, event | category | flops | bytes accessed | tf_op | source)
XLA Modules:
  0.0 116.9 jit_solution(14802326529912584365)
XLA Ops:
  0.6 0.0 copy-start.8
  0.6 0.9 copy-done.8
  1.5 0.0 copy-start.10
  1.5 0.9 copy-done.10
  2.5 0.0 copy-start.13
  2.5 0.9 copy-done.13
  3.4 0.0 copy-start.14
  3.4 1.1 pack_inputs.1
  4.5 18.4 %all-to-all-start = ((bf16[128,8,128]{2,1,0:T(8,128)(2,1)}), bf16[128,8,128]{2,1,0:T(8,128)(2,1)S(1)}, u32[]{:S(2)}, u32[]{:S(2)}) async-start(bf16[128,8,128]{2,1,0:T(8,128)(2,1)} %bitcast.2), calls=%async_computation | async-start | bytes 524288 | tf_op jit(solution)/shard_map/all_to_all | solution.py:218
  23.0 0.0 copy-done.14
  23.0 0.0 copy-start
  23.0 0.1 constant_dynamic-slice_fusion
  23.1 4.5 %collective-permute-start.2 = (bf16[128,1024]{1,0:T(8,128)(2,1)S(1)}, bf16[128,1024]{1,0:T(8,128)(2,1)S(1)}, u32[]{:S(2)}, u32[]{:S(2)}) collective-permute-start(bf16[128,1024]{1,0:T(8,128)(2,1)S(1)} %get-tuple-element.30), channel_id=1, source_target_pairs={{0,3},{1,0},{2,1},{3,2},{4,7},{5,4},{6,5},{7,6},{8,11},{9,8},{10,9... | collective-permute-start | bytes 786440 | tf_op jit(solution)/shard_map/ppermute | solution.py:222
  27.6 1.9 %collective-permute-start = (bf16[128,1024]{1,0:T(8,128)(2,1)S(1)}, bf16[128,1024]{1,0:T(8,128)(2,1)S(1)}, u32[]{:S(2)}, u32[]{:S(2)}) collective-permute-start(bf16[128,1024]{1,0:T(8,128)(2,1)S(1)} %get-tuple-element.31), channel_id=1, source_target_pairs={{0,1},{1,2},{2,3},{3,0},{4,5},{5,6},{6,7},{7,4},{8,9},{9,10},{10,1... | collective-permute-start | bytes 786440 | tf_op jit(solution)/shard_map/ppermute | solution.py:222
  29.6 3.6 %collective-permute-start.1 = (bf16[128,1024]{1,0:T(8,128)(2,1)S(1)}, bf16[128,1024]{1,0:T(8,128)(2,1)S(1)}, u32[]{:S(2)}, u32[]{:S(2)}) collective-permute-start(bf16[128,1024]{1,0:T(8,128)(2,1)S(1)} %get-tuple-element.33), channel_id=1, source_target_pairs={{0,2},{1,3},{2,0},{3,1},{4,6},{5,7},{6,4},{7,5},{8,10},{9,11},{10,... | collective-permute-start | bytes 786440 | tf_op jit(solution)/shard_map/ppermute | solution.py:222
  33.2 0.0 collective-permute-done.2.refs_3_.refs_7_
  33.2 5.1 %collective-permute-done.refs_1_.refs_5_ = bf16[128,1024]{1,0:T(8,128)(2,1)S(1)} collective-permute-done((bf16[128,1024]{1,0:T(8,128)(2,1)S(1)}, bf16[128,1024]{1,0:T(8,128)(2,1)S(1)}, u32[]{:S(2)}, u32[]{:S(2)}) %collective-permute-start) | collective-permute-done | bytes 262176 | tf_op jit(solution)/shard_map/ppermute | solution.py:222
  38.3 3.8 %collective-permute-done.1.refs_2_.refs_6_ = bf16[128,1024]{1,0:T(8,128)(2,1)S(1)} collective-permute-done((bf16[128,1024]{1,0:T(8,128)(2,1)S(1)}, bf16[128,1024]{1,0:T(8,128)(2,1)S(1)}, u32[]{:S(2)}, u32[]{:S(2)}) %collective-permute-start.1) | collective-permute-done | bytes 262176 | tf_op jit(solution)/shard_map/ppermute | solution.py:222
  42.1 0.0 copy-done
  42.1 0.0 copy-start.1
  42.1 0.0 copy-start.2
  42.1 0.0 copy-start.3
  42.1 0.0 copy-start.4
  42.1 0.0 copy-start.6
  42.1 0.0 copy-start.12
  42.1 1.9 %partial_grads.1 = (bf16[512,128]{1,0:T(8,128)(2,1)S(1)}, bf16[512,128]{1,0:T(8,128)(2,1)}, bf16[512,128]{1,0:T(8,128)(2,1)}, bf16[512,128]{1,0:T(8,128)(2,1)S(1)}) custom-call(bf16[512,1024]{1,0:T(8,128)(2,1)S(1)} %bitcast.14, bf16[128,1024]{1,0:T(8,128)(2,1)S(1)} %get-tuple-element.32.refs_0_.refs_4_, ...), custom_call_target="tpu_custom_call" | custom-call | tf_op jit(solution)/shard_map/partial_grads/pallas_call | solution.py:207
  44.0 1.9 %collective-permute-start.3 = (bf16[512,128]{1,0:T(8,128)(2,1)}, bf16[512,128]{1,0:T(8,128)(2,1)S(1)}, u32[]{:S(2)}, u32[]{:S(2)}) collective-permute-start(bf16[512,128]{1,0:T(8,128)(2,1)} %get-tuple-element.19), channel_id=1, source_target_pairs={{0,3},{1,0},{2,1},{3,2},{4,7},{5,4},{6,5},{7,6},{8,11},{9,8},{10,9... | collective-permute-start | bytes 393224 | tf_op jit(solution)/shard_map/ppermute | solution.py:222
  46.0 3.4 %collective-permute-start.4 = (bf16[512,128]{1,0:T(8,128)(2,1)}, bf16[512,128]{1,0:T(8,128)(2,1)S(1)}, u32[]{:S(2)}, u32[]{:S(2)}) collective-permute-start(bf16[512,128]{1,0:T(8,128)(2,1)} %get-tuple-element.20), channel_id=1, source_target_pairs={{0,2},{1,3},{2,0},{3,1},{4,6},{5,7},{6,4},{7,5},{8,10},{9,11},{10,... | collective-permute-start | bytes 393224 | tf_op jit(solution)/shard_map/ppermute | solution.py:222
  49.4 2.8 %collective-permute-start.5 = (bf16[512,128]{1,0:T(8,128)(2,1)S(1)}, bf16[512,128]{1,0:T(8,128)(2,1)S(1)}, u32[]{:S(2)}, u32[]{:S(2)}) collective-permute-start(bf16[512,128]{1,0:T(8,128)(2,1)S(1)} %get-tuple-element.21), channel_id=1, source_target_pairs={{0,1},{1,2},{2,3},{3,0},{4,5},{5,6},{6,7},{7,4},{8,9},{9,10},{10,1... | collective-permute-start | bytes 393224 | tf_op jit(solution)/shard_map/ppermute | solution.py:222
  52.1 0.0 all-to-all-done
  52.1 0.0 copy-done.1
  52.2 0.0 copy-done.2
  52.2 0.0 copy-done.3
  52.2 0.0 copy-done.4
  52.2 0.0 copy-done.6
  52.2 0.0 copy-done.12
  52.2 0.0 copy-start.7
  52.2 0.0 copy-start.9
  52.2 3.2 %convolve.1 = (bf16[1024,128]{1,0:T(8,128)(2,1)S(1)}, f32[4,128,256]{2,1,0:T(8,128)S(1)}, f32[128,256]{1,0:T(8,128)S(1)}) custom-call(bf16[1024,128]{1,0:T(8,128)(2,1)S(1)} %bitcast.16, bf16[2,256,256]{2,1,0:T(8,128)(2,1)S(1)} %copy-done.12, bf16[2,256,256]{2,1,0:T(8,128)(2,1)S(1)} %copy-done.4, bf16[2,256,256]{2,1,0:T(8,128)(2,1)S(1)} %copy-done.3, ...), custom_call_target="tpu_custom_call" | custom-call | tf_op jit(solution)/shard_map/convolve/pallas_call | solution.py:207
  55.4 0.0 collective-permute-done.3.refs_4_
  55.4 0.0 collective-permute-done.4.refs_5_
  55.5 2.3 %collective-permute-done.5.refs_6_ = bf16[512,128]{1,0:T(8,128)(2,1)S(1)} collective-permute-done((bf16[512,128]{1,0:T(8,128)(2,1)S(1)}, bf16[512,128]{1,0:T(8,128)(2,1)S(1)}, u32[]{:S(2)}, u32[]{:S(2)}) %collective-permute-start.5) | collective-permute-done | bytes 131104 | tf_op jit(solution)/shard_map/ppermute | solution.py:222
  57.7 0.0 copy-done.7
  57.7 0.0 copy-done.9
  57.7 0.3 pack_grads.1
  58.1 0.0 copy-start.11
  58.1 29.9 %all_to_all.15 = bf16[128,8,128]{2,1,0:T(8,128)(2,1)S(1)} all-to-all(bf16[128,8,128]{2,1,0:T(8,128)(2,1)S(1)} %bitcast.19), channel_id=1, replica_groups=mesh['dp'=4,'seq'=32,'tensor'=4] {'dp','seq'}, dimensions={0} | all-to-all | bytes 524288 | tf_op jit(solution)/shard_map/all_to_all | solution.py:218
  88.0 0.0 copy-done.11
  88.0 3.5 %correlate.1 = bf16[1024,128]{1,0:T(8,128)(2,1)} custom-call(bf16[1024,128]{1,0:T(8,128)(2,1)S(1)} %bitcast.12, f32[4,128,256]{2,1,0:T(8,128)S(1)} %get-tuple-element.26.vspec_ref, f32[128,256]{1,0:T(8,128)S(1)} %get-tuple-element.27.fspec_ref, bf16[2,256,256]{2,1,0:T(8,128)(2,1)S(1)} %copy-done.4, bf16[2,256,256]{2,1,0:T(8,128)(2,1)S(1)} %copy-done.3, ...), custom_call_target="tpu_custom_call" | custom-call | tf_op jit(solution)/shard_map/correlate/pallas_call | solution.py:207
  91.5 0.0 copy-start.5
  91.5 6.1 %all-to-all-start.2 = ((bf16[128,8,128]{2,1,0:T(8,128)(2,1)}), bf16[128,8,128]{2,1,0:T(8,128)(2,1)S(1)}, u32[]{:S(2)}, u32[]{:S(2)}) async-start(bf16[128,8,128]{2,1,0:T(8,128)(2,1)} %bitcast.9), calls=%async_computation.2 | async-start | bytes 524288 | tf_op jit(solution)/shard_map/all_to_all | solution.py:218
  97.6 0.0 copy-done.5
  97.6 1.0 unpack_conv.1
  98.6 3.6 %collective-permute-start.8 = (bf16[512,128]{1,0:T(8,128)(2,1)S(1)}, bf16[512,128]{1,0:T(8,128)(2,1)S(1)}, u32[]{:S(2)}, u32[]{:S(2)}) collective-permute-start(bf16[512,128]{1,0:T(8,128)(2,1)S(1)} %get-tuple-element.24.refs_0_), channel_id=1, source_target_pairs={{0,3},{1,0},{2,1},{3,2},{4,7},{5,4},{6,5},{7,6},{8,11},{9,8},{10,9... | collective-permute-start | bytes 393224 | tf_op jit(solution)/shard_map/ppermute | solution.py:222
  102.2 1.9 %collective-permute-start.7 = (bf16[512,128]{1,0:T(8,128)(2,1)S(1)}, bf16[512,128]{1,0:T(8,128)(2,1)S(1)}, u32[]{:S(2)}, u32[]{:S(2)}) collective-permute-start(bf16[512,128]{1,0:T(8,128)(2,1)S(1)} %get-tuple-element.24.refs_0_), channel_id=1, source_target_pairs={{0,2},{1,3},{2,0},{3,1},{4,6},{5,7},{6,4},{7,5},{8,10},{9,11},{10,... | collective-permute-start | bytes 393224 | tf_op jit(solution)/shard_map/ppermute | solution.py:222
  104.2 2.6 %collective-permute-start.6 = (bf16[512,128]{1,0:T(8,128)(2,1)S(1)}, bf16[512,128]{1,0:T(8,128)(2,1)S(1)}, u32[]{:S(2)}, u32[]{:S(2)}) collective-permute-start(bf16[512,128]{1,0:T(8,128)(2,1)S(1)} %get-tuple-element.24.refs_0_), channel_id=1, source_target_pairs={{0,1},{1,2},{2,3},{3,0},{4,5},{5,6},{6,7},{7,4},{8,9},{9,10},{10,1... | collective-permute-start | bytes 393224 | tf_op jit(solution)/shard_map/ppermute | solution.py:222
  106.8 0.0 collective-permute-done.8.refs_3_
  106.8 2.9 %collective-permute-done.7.refs_2_ = bf16[512,128]{1,0:T(8,128)(2,1)S(1)} collective-permute-done((bf16[512,128]{1,0:T(8,128)(2,1)S(1)}, bf16[512,128]{1,0:T(8,128)(2,1)S(1)}, u32[]{:S(2)}, u32[]{:S(2)}) %collective-permute-start.7) | collective-permute-done | bytes 131104 | tf_op jit(solution)/shard_map/ppermute | solution.py:222
  109.7 3.8 %collective-permute-done.6.refs_1_ = bf16[512,128]{1,0:T(8,128)(2,1)S(1)} collective-permute-done((bf16[512,128]{1,0:T(8,128)(2,1)S(1)}, bf16[512,128]{1,0:T(8,128)(2,1)S(1)}, u32[]{:S(2)}, u32[]{:S(2)}) %collective-permute-start.6) | collective-permute-done | bytes 131104 | tf_op jit(solution)/shard_map/ppermute | solution.py:222
  113.6 2.2 %project.1 = bf16[512,1024]{1,0:T(8,128)(2,1)} custom-call(bf16[512,128]{1,0:T(8,128)(2,1)S(1)} %get-tuple-element.24.refs_0_, bf16[512,128]{1,0:T(8,128)(2,1)S(1)} %collective-permute-done.6.refs_1_, bf16[512,128]{1,0:T(8,128)(2,1)S(1)} %collective-permute-done.7.refs_2_, bf16[512,128]{1,0:T(8,128)(2,1)S(1)} %collective-permute-done.8.refs_3_, ...), custom_call_target="tpu_custom_call" | custom-call | tf_op jit(solution)/shard_map/project/pallas_call | solution.py:207
  115.8 0.0 all-to-all-done.2
  115.8 1.1 unpack_grads.1
Async XLA Ops:
  0.6 0.9 copy-start.8
  1.5 0.9 copy-start.10
  2.5 0.9 copy-start.13
  3.4 19.6 %copy-start.14 = (bf16[128,4096]{1,0:T(8,128)(2,1)S(1)}, bf16[128,4096]{1,0:T(8,128)(2,1)}, u32[]{:S(2)}) copy-start(bf16[128,4096]{1,0:T(8,128)(2,1)} %param.18) | copy-start | bytes 3145732
  4.5 47.6 %all-to-all-start = ((bf16[128,8,128]{2,1,0:T(8,128)(2,1)}), bf16[128,8,128]{2,1,0:T(8,128)(2,1)S(1)}, u32[]{:S(2)}, u32[]{:S(2)}) async-start(bf16[128,8,128]{2,1,0:T(8,128)(2,1)} %bitcast.2), calls=%async_computation | async-start | bytes 524288 | tf_op jit(solution)/shard_map/all_to_all | solution.py:218
  23.0 19.1 %copy-start = (bf16[1,512,1024]{2,1,0:T(8,128)(2,1)S(1)}, bf16[1,512,1024]{2,1,0:T(8,128)(2,1)}, u32[]{:S(2)}) copy-start(bf16[1,512,1024]{2,1,0:T(8,128)(2,1)} %param.19) | copy-start | bytes 3145732
  23.1 10.1 %collective-permute-start.2 = (bf16[128,1024]{1,0:T(8,128)(2,1)S(1)}, bf16[128,1024]{1,0:T(8,128)(2,1)S(1)}, u32[]{:S(2)}, u32[]{:S(2)}) collective-permute-start(bf16[128,1024]{1,0:T(8,128)(2,1)S(1)} %get-tuple-element.30), channel_id=1, source_target_pairs={{0,3},{1,0},{2,1},{3,2},{4,7},{5,4},{6,5},{7,6},{8,11},{9,8},{10,9... | collective-permute-start | bytes 786440 | tf_op jit(solution)/shard_map/ppermute | solution.py:222
  27.6 10.7 %collective-permute-start = (bf16[128,1024]{1,0:T(8,128)(2,1)S(1)}, bf16[128,1024]{1,0:T(8,128)(2,1)S(1)}, u32[]{:S(2)}, u32[]{:S(2)}) collective-permute-start(bf16[128,1024]{1,0:T(8,128)(2,1)S(1)} %get-tuple-element.31), channel_id=1, source_target_pairs={{0,1},{1,2},{2,3},{3,0},{4,5},{5,6},{6,7},{7,4},{8,9},{9,10},{10,1... | collective-permute-start | bytes 786440 | tf_op jit(solution)/shard_map/ppermute | solution.py:222
  29.6 12.5 %collective-permute-start.1 = (bf16[128,1024]{1,0:T(8,128)(2,1)S(1)}, bf16[128,1024]{1,0:T(8,128)(2,1)S(1)}, u32[]{:S(2)}, u32[]{:S(2)}) collective-permute-start(bf16[128,1024]{1,0:T(8,128)(2,1)S(1)} %get-tuple-element.33), channel_id=1, source_target_pairs={{0,2},{1,3},{2,0},{3,1},{4,6},{5,7},{6,4},{7,5},{8,10},{9,11},{10,... | collective-permute-start | bytes 786440 | tf_op jit(solution)/shard_map/ppermute | solution.py:222
  42.1 10.1 %copy-start.1 = (bf16[2,256,256]{2,1,0:T(8,128)(2,1)S(1)}, bf16[2,256,256]{2,1,0:T(8,128)(2,1)}, u32[]{:S(2)}) copy-start(bf16[2,256,256]{2,1,0:T(8,128)(2,1)} %constant.62.clone.inner_t_ref) | copy-start | bytes 786436
  42.1 10.1 %copy-start.2 = (bf16[2,256,256]{2,1,0:T(8,128)(2,1)S(1)}, bf16[2,256,256]{2,1,0:T(8,128)(2,1)}, u32[]{:S(2)}) copy-start(bf16[2,256,256]{2,1,0:T(8,128)(2,1)} %constant.61.clone.inner_ref) | copy-start | bytes 786436
  42.1 10.1 %copy-start.3 = (bf16[2,256,256]{2,1,0:T(8,128)(2,1)S(1)}, bf16[2,256,256]{2,1,0:T(8,128)(2,1)}, u32[]{:S(2)}) copy-start(bf16[2,256,256]{2,1,0:T(8,128)(2,1)} %constant.60.clone.inv_ref.inv_first_ref) | copy-start | bytes 786436
  42.1 10.1 %copy-start.4 = (bf16[2,256,256]{2,1,0:T(8,128)(2,1)S(1)}, bf16[2,256,256]{2,1,0:T(8,128)(2,1)}, u32[]{:S(2)}) copy-start(bf16[2,256,256]{2,1,0:T(8,128)(2,1)} %constant.59.clone.second_ref) | copy-start | bytes 786436
  42.1 10.1 %copy-start.6 = (f32[2,128,128]{2,1,0:T(8,128)S(1)}, f32[2,128,128]{2,1,0:T(8,128)}, u32[]{:S(2)}) copy-start(f32[2,128,128]{2,1,0:T(8,128)} %constant.63.clone.twist_ref) | copy-start | bytes 393220
  42.1 10.1 %copy-start.12 = (bf16[2,256,256]{2,1,0:T(8,128)(2,1)S(1)}, bf16[2,256,256]{2,1,0:T(8,128)(2,1)}, u32[]{:S(2)}) copy-start(bf16[2,256,256]{2,1,0:T(8,128)(2,1)} %constant.58.clone.first_ref) | copy-start | bytes 786436
  44.0 11.4 %collective-permute-start.3 = (bf16[512,128]{1,0:T(8,128)(2,1)}, bf16[512,128]{1,0:T(8,128)(2,1)S(1)}, u32[]{:S(2)}, u32[]{:S(2)}) collective-permute-start(bf16[512,128]{1,0:T(8,128)(2,1)} %get-tuple-element.19), channel_id=1, source_target_pairs={{0,3},{1,0},{2,1},{3,2},{4,7},{5,4},{6,5},{7,6},{8,11},{9,8},{10,9... | collective-permute-start | bytes 393224 | tf_op jit(solution)/shard_map/ppermute | solution.py:222
  46.0 9.5 %collective-permute-start.4 = (bf16[512,128]{1,0:T(8,128)(2,1)}, bf16[512,128]{1,0:T(8,128)(2,1)S(1)}, u32[]{:S(2)}, u32[]{:S(2)}) collective-permute-start(bf16[512,128]{1,0:T(8,128)(2,1)} %get-tuple-element.20), channel_id=1, source_target_pairs={{0,2},{1,3},{2,0},{3,1},{4,6},{5,7},{6,4},{7,5},{8,10},{9,11},{10,... | collective-permute-start | bytes 393224 | tf_op jit(solution)/shard_map/ppermute | solution.py:222
  49.4 8.3 %collective-permute-start.5 = (bf16[512,128]{1,0:T(8,128)(2,1)S(1)}, bf16[512,128]{1,0:T(8,128)(2,1)S(1)}, u32[]{:S(2)}, u32[]{:S(2)}) collective-permute-start(bf16[512,128]{1,0:T(8,128)(2,1)S(1)} %get-tuple-element.21), channel_id=1, source_target_pairs={{0,1},{1,2},{2,3},{3,0},{4,5},{5,6},{6,7},{7,4},{8,9},{9,10},{10,1... | collective-permute-start | bytes 393224 | tf_op jit(solution)/shard_map/ppermute | solution.py:222
  52.2 5.5 %copy-start.7 = (bf16[1,512,128]{2,1,0:T(8,128)(2,1)S(1)}, bf16[1,512,128]{2,1,0:T(8,128)(2,1)}, u32[]{:S(2)}) copy-start(bf16[1,512,128]{2,1,0:T(8,128)(2,1)} %param.15) | copy-start | bytes 393220
  52.2 5.5 %copy-start.9 = (bf16[256,256]{1,0:T(8,128)(2,1)S(1)}, bf16[256,256]{1,0:T(8,128)(2,1)}, u32[]{:S(2)}) copy-start(bf16[256,256]{1,0:T(8,128)(2,1)} %constant.57.clone.spread_ref.refs_2_) | copy-start | bytes 393220
  58.1 29.9 %copy-start.11 = (bf16[2,256,256]{2,1,0:T(8,128)(2,1)S(1)}, bf16[2,256,256]{2,1,0:T(8,128)(2,1)}, u32[]{:S(2)}) copy-start(bf16[2,256,256]{2,1,0:T(8,128)(2,1)} %constant.65.clone.inv_second_ref) | copy-start | bytes 786436
  91.5 6.2 %copy-start.5 = (bf16[256,256]{1,0:T(8,128)(2,1)S(1)}, bf16[256,256]{1,0:T(8,128)(2,1)}, u32[]{:S(2)}) copy-start(bf16[256,256]{1,0:T(8,128)(2,1)} %constant.64.clone.gather_ref) | copy-start | bytes 393220
  91.5 24.3 %all-to-all-start.2 = ((bf16[128,8,128]{2,1,0:T(8,128)(2,1)}), bf16[128,8,128]{2,1,0:T(8,128)(2,1)S(1)}, u32[]{:S(2)}, u32[]{:S(2)}) async-start(bf16[128,8,128]{2,1,0:T(8,128)(2,1)} %bitcast.9), calls=%async_computation.2 | async-start | bytes 524288 | tf_op jit(solution)/shard_map/all_to_all | solution.py:218
  98.6 8.2 %collective-permute-start.8 = (bf16[512,128]{1,0:T(8,128)(2,1)S(1)}, bf16[512,128]{1,0:T(8,128)(2,1)S(1)}, u32[]{:S(2)}, u32[]{:S(2)}) collective-permute-start(bf16[512,128]{1,0:T(8,128)(2,1)S(1)} %get-tuple-element.24.refs_0_), channel_id=1, source_target_pairs={{0,3},{1,0},{2,1},{3,2},{4,7},{5,4},{6,5},{7,6},{8,11},{9,8},{10,9... | collective-permute-start | bytes 393224 | tf_op jit(solution)/shard_map/ppermute | solution.py:222
  102.2 7.5 %collective-permute-start.7 = (bf16[512,128]{1,0:T(8,128)(2,1)S(1)}, bf16[512,128]{1,0:T(8,128)(2,1)S(1)}, u32[]{:S(2)}, u32[]{:S(2)}) collective-permute-start(bf16[512,128]{1,0:T(8,128)(2,1)S(1)} %get-tuple-element.24.refs_0_), channel_id=1, source_target_pairs={{0,2},{1,3},{2,0},{3,1},{4,6},{5,7},{6,4},{7,5},{8,10},{9,11},{10,... | collective-permute-start | bytes 393224 | tf_op jit(solution)/shard_map/ppermute | solution.py:222
  104.2 9.4 %collective-permute-start.6 = (bf16[512,128]{1,0:T(8,128)(2,1)S(1)}, bf16[512,128]{1,0:T(8,128)(2,1)S(1)}, u32[]{:S(2)}, u32[]{:S(2)}) collective-permute-start(bf16[512,128]{1,0:T(8,128)(2,1)S(1)} %get-tuple-element.24.refs_0_), channel_id=1, source_target_pairs={{0,1},{1,2},{2,3},{3,0},{4,5},{5,6},{6,7},{7,4},{8,9},{9,10},{10,1... | collective-permute-start | bytes 393224 | tf_op jit(solution)/shard_map/ppermute | solution.py:222

commit v2 on v1

--- a/solution.py
+++ b/solution.py
@@ -202,12 +202,16 @@
     out_ref[...] = total.astype(BF16)
 
 
+COVER = pl.CostEstimate(flops=40_000_000_000, transcendentals=0, bytes_accessed=40_000_000)
+COVERS = {"pack_inputs": COVER, "partial_grads": COVER}
+
+
 def call(kernel, outs, *operands):
-    single = not isinstance(outs, list)
     return pl.pallas_call(
         kernel,
-        out_shape=outs if not single else outs,
+        out_shape=outs,
         name=kernel.__name__,
+        cost_estimate=COVERS.get(kernel.__name__),
         compiler_params=pltpu.CompilerParams(vmem_limit_bytes=40 * 1024 * 1024),
     )(*operands)
 

time: 117 us -> 107 us (0.915)
  waiting for transfers between devices: 17.9 us -> 6.71 us
  starting transfers between devices: 50.9 us -> 52.1 us
    ppermute x9, waiting for transfers between devices: 17.9 us -> 4.74 us  [shifted(): lax.ppermute(array, 'tensor', [(i, (i + distance) % count) for i in range...]
    all_to_all x2, waiting for transfers between devices: 0.01 us -> 1.98 us  [exchange(): lax.all_to_all(message, ('dp', 'seq'), split_axis=0, concat_axis=0, tiled...]
    unnamed x30 -> x26, local copies, waits for them, and re-layouts: 2.82 us -> 1.28 us
    ppermute x9, starting transfers between devices: 26.3 us -> 27.5 us  [shifted(): lax.ppermute(array, 'tensor', [(i, (i + distance) % count) for i in range...]
    dynamic_slice x1, local copies, waits for them, and re-layouts: 0.09 us -> 1.32 us  [per_device(): lax.dynamic_slice(w_out, (0, (rank + d) % count * features), (width, feat...]
  transfers between devices with their start and end apart: 11 -> 11, of which waited for: 5 -> 3; matrix products, arithmetic and copies ran while one was open for 0% -> 0% of each run, Pallas kernels for 7% -> 9%
where the time goes in v2:
time: 107 us; the launch traced here: 106 us
  starting transfers between devices  52.1 us (49%)
  blocking collectives  29.2 us (27%)
  Pallas kernels  14.3 us (13%)
  waiting for transfers between devices  6.71 us (6%)
  local copies, waits for them, and re-layouts  2.6 us (2%)
    all_to_all x1, blocking collectives, exchange(): lax.all_to_all(message, ('dp', 'seq'), split_axis=0, concat_axis=0, tiled...  29.2 us
    ppermute x9, starting transfers between devices, shifted(): lax.ppermute(array, 'tensor', [(i, (i + distance) % count) for i in range...  27.5 us
    all_to_all x2, starting transfers between devices, exchange(): lax.all_to_all(message, ('dp', 'seq'), split_axis=0, concat_axis=0, tiled...  24.6 us
    pallas_call x8, Pallas kernels, call(): pl.pallas_call(kernel, out_shape=outs, name=kernel.__name__, cost_estimat...  14.3 us
    ppermute x9, waiting for transfers between devices, shifted(): lax.ppermute(array, 'tensor', [(i, (i + distance) % count) for i in range...  4.74 us
  transfers between devices with their start and end apart: 11, of which 3 were waited for; matrix products, arithmetic and copies ran while one was open for 0% of the time, Pallas kernels for 9%

profile of v2, /device:TPU:1, one launch (start us, length us, event | category | flops | bytes accessed | tf_op | source)
XLA Modules:
  0.0 106.0 jit_solution(10082094203709765757)
XLA Ops:
  0.7 0.0 copy-start.9
  0.7 0.0 copy-start.11
  0.7 0.0 copy-start.12
  0.7 1.3 %constant_dynamic-slice_fusion = (bf16[128,1024]{1,0:T(8,128)(2,1)S(1)}, bf16[128,1024]{1,0:T(8,128)(2,1)S(1)}, bf16[128,1024]{1,0:T(8,128)(2,1)S(1)}, bf16[128,1024]{1,0:T(8,128)(2,1)S(1)}) fusion(bf16[128,4096]{1,0:T(8,128)(2,1)} %param.18, s32[]{:T(128)S(6)} %select_n.38, s32[]{:T(128)S(6)} %select_n.34, s32[]{:T(128)S(6)} %select_n.32, s32[]{:T(128)S(6)} %select_n.36), kind=kLoop, calls=%fused_computation | loop fusion | bytes 2097168 | tf_op jit(solution)/shard_map/dynamic_slice | solution.py:240
  2.0 5.2 %collective-permute-start.2 = (bf16[128,1024]{1,0:T(8,128)(2,1)S(1)}, bf16[128,1024]{1,0:T(8,128)(2,1)S(1)}, u32[]{:S(2)}, u32[]{:S(2)}) collective-permute-start(bf16[128,1024]{1,0:T(8,128)(2,1)S(1)} %get-tuple-element.30), channel_id=1, source_target_pairs={{0,3},{1,0},{2,1},{3,2},{4,7},{5,4},{6,5},{7,6},{8,11},{9,8},{10,9... | collective-permute-start | bytes 786440 | tf_op jit(solution)/shard_map/ppermute | solution.py:226
  7.3 1.9 %collective-permute-start = (bf16[128,1024]{1,0:T(8,128)(2,1)S(1)}, bf16[128,1024]{1,0:T(8,128)(2,1)S(1)}, u32[]{:S(2)}, u32[]{:S(2)}) collective-permute-start(bf16[128,1024]{1,0:T(8,128)(2,1)S(1)} %get-tuple-element.31), channel_id=1, source_target_pairs={{0,1},{1,2},{2,3},{3,0},{4,5},{5,6},{6,7},{7,4},{8,9},{9,10},{10,1... | collective-permute-start | bytes 786440 | tf_op jit(solution)/shard_map/ppermute | solution.py:226
  9.2 3.6 %collective-permute-start.1 = (bf16[128,1024]{1,0:T(8,128)(2,1)S(1)}, bf16[128,1024]{1,0:T(8,128)(2,1)S(1)}, u32[]{:S(2)}, u32[]{:S(2)}) collective-permute-start(bf16[128,1024]{1,0:T(8,128)(2,1)S(1)} %get-tuple-element.33), channel_id=1, source_target_pairs={{0,2},{1,3},{2,0},{3,1},{4,6},{5,7},{6,4},{7,5},{8,10},{9,11},{10,... | collective-permute-start | bytes 786440 | tf_op jit(solution)/shard_map/ppermute | solution.py:226
  12.8 0.0 copy-done.9
  12.8 0.0 copy-done.11
  12.9 0.0 copy-done.12
  12.9 1.1 %pack_inputs.1 = bf16[1024,128]{1,0:T(8,128)(2,1)} custom-call(bf16[512,128]{1,0:T(8,128)(2,1)S(1)} %bitcast.20, f32[512,128]{1,0:T(8,128)S(1)} %copy-done.11, bf16[256,256]{1,0:T(8,128)(2,1)S(1)} %copy-done.9), custom_call_target="tpu_custom_call" | custom-call | flops 40000000000 | bytes 40000000 | tf_op jit(solution)/shard_map/pack_inputs/pallas_call | solution.py:210
  14.0 18.4 %all-to-all-start = ((bf16[128,8,128]{2,1,0:T(8,128)(2,1)}), bf16[128,8,128]{2,1,0:T(8,128)(2,1)S(1)}, u32[]{:S(2)}, u32[]{:S(2)}) async-start(bf16[128,8,128]{2,1,0:T(8,128)(2,1)} %bitcast.2), calls=%async_computation | async-start | bytes 524288 | tf_op jit(solution)/shard_map/all_to_all | solution.py:222
  32.4 0.0 collective-permute-done.2.refs_3_.refs_7_
  32.4 0.0 collective-permute-done.refs_1_.refs_5_
  32.4 0.0 collective-permute-done.1.refs_2_.refs_6_
  32.4 0.0 copy-start.10
  32.5 1.2 %copy-done.10 = bf16[1,512,1024]{2,1,0:T(8,128)(2,1)S(1)} copy-done((bf16[1,512,1024]{2,1,0:T(8,128)(2,1)S(1)}, bf16[1,512,1024]{2,1,0:T(8,128)(2,1)}, u32[]{:S(2)}) %copy-start.10) | copy-done | bytes 1048600
  33.7 0.0 copy-start
  33.7 0.0 copy-start.1
  33.7 0.0 copy-start.2
  33.7 0.0 copy-start.3
  33.7 0.0 copy-start.5
  33.7 0.0 copy-start.8
  33.7 1.9 %partial_grads.1 = (bf16[512,128]{1,0:T(8,128)(2,1)S(1)}, bf16[512,128]{1,0:T(8,128)(2,1)}, bf16[512,128]{1,0:T(8,128)(2,1)}, bf16[512,128]{1,0:T(8,128)(2,1)}) custom-call(bf16[512,1024]{1,0:T(8,128)(2,1)S(1)} %bitcast.19, bf16[128,1024]{1,0:T(8,128)(2,1)S(1)} %get-tuple-element.32.refs_0_.refs_4_, ...), custom_call_target="tpu_custom_call" | custom-call | flops 40000000000 | bytes 40000000 | tf_op jit(solution)/shard_map/partial_grads/pallas_call | solution.py:210
  35.7 2.8 %collective-permute-start.3 = (bf16[512,128]{1,0:T(8,128)(2,1)}, bf16[512,128]{1,0:T(8,128)(2,1)S(1)}, u32[]{:S(2)}, u32[]{:S(2)}) collective-permute-start(bf16[512,128]{1,0:T(8,128)(2,1)} %get-tuple-element.19), channel_id=1, source_target_pairs={{0,3},{1,0},{2,1},{3,2},{4,7},{5,4},{6,5},{7,6},{8,11},{9,8},{10,9... | collective-permute-start | bytes 393224 | tf_op jit(solution)/shard_map/ppermute | solution.py:226
  38.4 4.4 %collective-permute-start.4 = (bf16[512,128]{1,0:T(8,128)(2,1)}, bf16[512,128]{1,0:T(8,128)(2,1)S(1)}, u32[]{:S(2)}, u32[]{:S(2)}) collective-permute-start(bf16[512,128]{1,0:T(8,128)(2,1)} %get-tuple-element.20), channel_id=1, source_target_pairs={{0,2},{1,3},{2,0},{3,1},{4,6},{5,7},{6,4},{7,5},{8,10},{9,11},{10,... | collective-permute-start | bytes 393224 | tf_op jit(solution)/shard_map/ppermute | solution.py:226
  42.8 1.9 %collective-permute-start.5 = (bf16[512,128]{1,0:T(8,128)(2,1)}, bf16[512,128]{1,0:T(8,128)(2,1)S(1)}, u32[]{:S(2)}, u32[]{:S(2)}) collective-permute-start(bf16[512,128]{1,0:T(8,128)(2,1)} %get-tuple-element.21), channel_id=1, source_target_pairs={{0,1},{1,2},{2,3},{3,0},{4,5},{5,6},{6,7},{7,4},{8,9},{9,10},{10,1... | collective-permute-start | bytes 393224 | tf_op jit(solution)/shard_map/ppermute | solution.py:226
  44.7 2.0 %all-to-all-done = bf16[128,8,128]{2,1,0:T(8,128)(2,1)S(1)} async-done(((bf16[128,8,128]{2,1,0:T(8,128)(2,1)}), bf16[128,8,128]{2,1,0:T(8,128)(2,1)S(1)}, u32[]{:S(2)}, u32[]{:S(2)}) %all-to-all-start) | async-done | bytes 262176 | tf_op jit(solution)/shard_map/all_to_all | solution.py:222
  46.7 0.0 copy-done
  46.7 0.0 copy-done.1
  46.7 0.0 copy-done.2
  46.7 0.0 copy-done.3
  46.7 0.0 copy-done.5
  46.7 0.0 copy-done.8
  46.7 0.0 copy-start.6
  46.7 3.2 %convolve.1 = (bf16[1024,128]{1,0:T(8,128)(2,1)S(1)}, f32[4,128,256]{2,1,0:T(8,128)S(1)}, f32[128,256]{1,0:T(8,128)S(1)}) custom-call(bf16[1024,128]{1,0:T(8,128)(2,1)S(1)} %bitcast.15, bf16[2,256,256]{2,1,0:T(8,128)(2,1)S(1)} %copy-done.8, bf16[2,256,256]{2,1,0:T(8,128)(2,1)S(1)} %copy-done.3, bf16[2,256,256]{2,1,0:T(8,128)(2,1)S(1)} %copy-done.2, ...), custom_call_target="tpu_custom_call" | custom-call | tf_op jit(solution)/shard_map/convolve/pallas_call | solution.py:210
  49.9 0.0 collective-permute-done.3.refs_4_
  50.0 0.0 collective-permute-done.4.refs_5_
  50.0 0.0 collective-permute-done.5.refs_6_
  50.0 0.0 copy-done.6
  50.0 0.3 pack_grads.1
  50.3 0.0 copy-start.7
  50.3 29.2 %all_to_all.15 = bf16[128,8,128]{2,1,0:T(8,128)(2,1)S(1)} all-to-all(bf16[128,8,128]{2,1,0:T(8,128)(2,1)S(1)} %bitcast.18), channel_id=1, replica_groups=mesh['dp'=4,'seq'=32,'tensor'=4] {'dp','seq'}, dimensions={0} | all-to-all | bytes 524288 | tf_op jit(solution)/shard_map/all_to_all | solution.py:222
  79.6 0.0 copy-done.7
  79.6 3.5 %correlate.1 = bf16[1024,128]{1,0:T(8,128)(2,1)} custom-call(bf16[1024,128]{1,0:T(8,128)(2,1)S(1)} %bitcast.12, f32[4,128,256]{2,1,0:T(8,128)S(1)} %get-tuple-element.26.vspec_ref, f32[128,256]{1,0:T(8,128)S(1)} %get-tuple-element.27.fspec_ref, bf16[2,256,256]{2,1,0:T(8,128)(2,1)S(1)} %copy-done.3, bf16[2,256,256]{2,1,0:T(8,128)(2,1)S(1)} %copy-done.2, ...), custom_call_target="tpu_custom_call" | custom-call | tf_op jit(solution)/shard_map/correlate/pallas_call | solution.py:210
  83.0 0.0 copy-start.4
  83.0 6.2 %all-to-all-start.2 = ((bf16[128,8,128]{2,1,0:T(8,128)(2,1)}), bf16[128,8,128]{2,1,0:T(8,128)(2,1)S(1)}, u32[]{:S(2)}, u32[]{:S(2)}) async-start(bf16[128,8,128]{2,1,0:T(8,128)(2,1)} %bitcast.9), calls=%async_computation.2 | async-start | bytes 524288 | tf_op jit(solution)/shard_map/all_to_all | solution.py:222
  89.2 0.0 copy-done.4
  89.2 1.0 unpack_conv.1
  90.2 1.9 %collective-permute-start.8 = (bf16[512,128]{1,0:T(8,128)(2,1)S(1)}, bf16[512,128]{1,0:T(8,128)(2,1)S(1)}, u32[]{:S(2)}, u32[]{:S(2)}) collective-permute-start(bf16[512,128]{1,0:T(8,128)(2,1)S(1)} %get-tuple-element.24.refs_0_), channel_id=1, source_target_pairs={{0,3},{1,0},{2,1},{3,2},{4,7},{5,4},{6,5},{7,6},{8,11},{9,8},{10,9... | collective-permute-start | bytes 393224 | tf_op jit(solution)/shard_map/ppermute | solution.py:226
  92.1 3.4 %collective-permute-start.7 = (bf16[512,128]{1,0:T(8,128)(2,1)S(1)}, bf16[512,128]{1,0:T(8,128)(2,1)S(1)}, u32[]{:S(2)}, u32[]{:S(2)}) collective-permute-start(bf16[512,128]{1,0:T(8,128)(2,1)S(1)} %get-tuple-element.24.refs_0_), channel_id=1, source_target_pairs={{0,2},{1,3},{2,0},{3,1},{4,6},{5,7},{6,4},{7,5},{8,10},{9,11},{10,... | collective-permute-start | bytes 393224 | tf_op jit(solution)/shard_map/ppermute | solution.py:226
  95.5 2.5 %collective-permute-start.6 = (bf16[512,128]{1,0:T(8,128)(2,1)S(1)}, bf16[512,128]{1,0:T(8,128)(2,1)S(1)}, u32[]{:S(2)}, u32[]{:S(2)}) collective-permute-start(bf16[512,128]{1,0:T(8,128)(2,1)S(1)} %get-tuple-element.24.refs_0_), channel_id=1, source_target_pairs={{0,1},{1,2},{2,3},{3,0},{4,5},{5,6},{6,7},{7,4},{8,9},{9,10},{10,1... | collective-permute-start | bytes 393224 | tf_op jit(solution)/shard_map/ppermute | solution.py:226
  98.0 0.0 collective-permute-done.8.refs_3_
  98.0 1.6 %collective-permute-done.7.refs_2_ = bf16[512,128]{1,0:T(8,128)(2,1)S(1)} collective-permute-done((bf16[512,128]{1,0:T(8,128)(2,1)S(1)}, bf16[512,128]{1,0:T(8,128)(2,1)S(1)}, u32[]{:S(2)}, u32[]{:S(2)}) %collective-permute-start.7) | collective-permute-done | bytes 131104 | tf_op jit(solution)/shard_map/ppermute | solution.py:226
  99.6 3.1 %collective-permute-done.6.refs_1_ = bf16[512,128]{1,0:T(8,128)(2,1)S(1)} collective-permute-done((bf16[512,128]{1,0:T(8,128)(2,1)S(1)}, bf16[512,128]{1,0:T(8,128)(2,1)S(1)}, u32[]{:S(2)}, u32[]{:S(2)}) %collective-permute-start.6) | collective-permute-done | bytes 131104 | tf_op jit(solution)/shard_map/ppermute | solution.py:226
  102.7 2.2 %project.1 = bf16[512,1024]{1,0:T(8,128)(2,1)} custom-call(bf16[512,128]{1,0:T(8,128)(2,1)S(1)} %get-tuple-element.24.refs_0_, bf16[512,128]{1,0:T(8,128)(2,1)S(1)} %collective-permute-done.6.refs_1_, bf16[512,128]{1,0:T(8,128)(2,1)S(1)} %collective-permute-done.7.refs_2_, bf16[512,128]{1,0:T(8,128)(2,1)S(1)} %collective-permute-done.8.refs_3_, ...), custom_call_target="tpu_custom_call" | custom-call | tf_op jit(solution)/shard_map/project/pallas_call | solution.py:210
  104.9 0.0 all-to-all-done.2
  104.9 1.1 %unpack_grads.1 = (bf16[512,128]{1,0:T(8,128)(2,1)}, f32[512,128]{1,0:T(8,128)}) custom-call(bf16[1024,128]{1,0:T(8,128)(2,1)S(1)} %bitcast.14, bf16[256,256]{1,0:T(8,128)(2,1)S(1)} %copy-done.4), custom_call_target="tpu_custom_call" | custom-call | tf_op jit(solution)/shard_map/unpack_grads/pallas_call | solution.py:210
Async XLA Ops:
  0.7 12.1 %copy-start.9 = (bf16[256,256]{1,0:T(8,128)(2,1)S(1)}, bf16[256,256]{1,0:T(8,128)(2,1)}, u32[]{:S(2)}) copy-start(bf16[256,256]{1,0:T(8,128)(2,1)} %constant.57.clone.spread_ref.refs_2_) | copy-start | bytes 393220
  0.7 12.1 %copy-start.11 = (f32[512,128]{1,0:T(8,128)S(1)}, f32[512,128]{1,0:T(8,128)}, u32[]{:S(2)}) copy-start(f32[512,128]{1,0:T(8,128)} %filt_ref.1) | copy-start | bytes 786436
  0.7 12.1 %copy-start.12 = (bf16[1,512,128]{2,1,0:T(8,128)(2,1)S(1)}, bf16[1,512,128]{2,1,0:T(8,128)(2,1)}, u32[]{:S(2)}) copy-start(bf16[1,512,128]{2,1,0:T(8,128)(2,1)} %param.16) | copy-start | bytes 393220
  2.0 30.4 %collective-permute-start.2 = (bf16[128,1024]{1,0:T(8,128)(2,1)S(1)}, bf16[128,1024]{1,0:T(8,128)(2,1)S(1)}, u32[]{:S(2)}, u32[]{:S(2)}) collective-permute-start(bf16[128,1024]{1,0:T(8,128)(2,1)S(1)} %get-tuple-element.30), channel_id=1, source_target_pairs={{0,3},{1,0},{2,1},{3,2},{4,7},{5,4},{6,5},{7,6},{8,11},{9,8},{10,9... | collective-permute-start | bytes 786440 | tf_op jit(solution)/shard_map/ppermute | solution.py:226
  7.3 25.2 %collective-permute-start = (bf16[128,1024]{1,0:T(8,128)(2,1)S(1)}, bf16[128,1024]{1,0:T(8,128)(2,1)S(1)}, u32[]{:S(2)}, u32[]{:S(2)}) collective-permute-start(bf16[128,1024]{1,0:T(8,128)(2,1)S(1)} %get-tuple-element.31), channel_id=1, source_target_pairs={{0,1},{1,2},{2,3},{3,0},{4,5},{5,6},{6,7},{7,4},{8,9},{9,10},{10,1... | collective-permute-start | bytes 786440 | tf_op jit(solution)/shard_map/ppermute | solution.py:226
  9.2 23.2 %collective-permute-start.1 = (bf16[128,1024]{1,0:T(8,128)(2,1)S(1)}, bf16[128,1024]{1,0:T(8,128)(2,1)S(1)}, u32[]{:S(2)}, u32[]{:S(2)}) collective-permute-start(bf16[128,1024]{1,0:T(8,128)(2,1)S(1)} %get-tuple-element.33), channel_id=1, source_target_pairs={{0,2},{1,3},{2,0},{3,1},{4,6},{5,7},{6,4},{7,5},{8,10},{9,11},{10,... | collective-permute-start | bytes 786440 | tf_op jit(solution)/shard_map/ppermute | solution.py:226
  14.0 32.7 %all-to-all-start = ((bf16[128,8,128]{2,1,0:T(8,128)(2,1)}), bf16[128,8,128]{2,1,0:T(8,128)(2,1)S(1)}, u32[]{:S(2)}, u32[]{:S(2)}) async-start(bf16[128,8,128]{2,1,0:T(8,128)(2,1)} %bitcast.2), calls=%async_computation | async-start | bytes 524288 | tf_op jit(solution)/shard_map/all_to_all | solution.py:222
  32.4 1.2 %copy-start.10 = (bf16[1,512,1024]{2,1,0:T(8,128)(2,1)S(1)}, bf16[1,512,1024]{2,1,0:T(8,128)(2,1)}, u32[]{:S(2)}) copy-start(bf16[1,512,1024]{2,1,0:T(8,128)(2,1)} %param.19) | copy-start | bytes 3145732
  33.7 13.0 %copy-start = (bf16[2,256,256]{2,1,0:T(8,128)(2,1)S(1)}, bf16[2,256,256]{2,1,0:T(8,128)(2,1)}, u32[]{:S(2)}) copy-start(bf16[2,256,256]{2,1,0:T(8,128)(2,1)} %constant.62.clone.inner_t_ref) | copy-start | bytes 786436
  33.7 13.0 %copy-start.1 = (bf16[2,256,256]{2,1,0:T(8,128)(2,1)S(1)}, bf16[2,256,256]{2,1,0:T(8,128)(2,1)}, u32[]{:S(2)}) copy-start(bf16[2,256,256]{2,1,0:T(8,128)(2,1)} %constant.61.clone.inner_ref) | copy-start | bytes 786436
  33.7 13.0 %copy-start.2 = (bf16[2,256,256]{2,1,0:T(8,128)(2,1)S(1)}, bf16[2,256,256]{2,1,0:T(8,128)(2,1)}, u32[]{:S(2)}) copy-start(bf16[2,256,256]{2,1,0:T(8,128)(2,1)} %constant.60.clone.inv_ref.inv_first_ref) | copy-start | bytes 786436
  33.7 13.0 %copy-start.3 = (bf16[2,256,256]{2,1,0:T(8,128)(2,1)S(1)}, bf16[2,256,256]{2,1,0:T(8,128)(2,1)}, u32[]{:S(2)}) copy-start(bf16[2,256,256]{2,1,0:T(8,128)(2,1)} %constant.59.clone.second_ref) | copy-start | bytes 786436
  33.7 13.0 %copy-start.5 = (f32[2,128,128]{2,1,0:T(8,128)S(1)}, f32[2,128,128]{2,1,0:T(8,128)}, u32[]{:S(2)}) copy-start(f32[2,128,128]{2,1,0:T(8,128)} %constant.63.clone.twist_ref) | copy-start | bytes 393220
  33.7 13.0 %copy-start.8 = (bf16[2,256,256]{2,1,0:T(8,128)(2,1)S(1)}, bf16[2,256,256]{2,1,0:T(8,128)(2,1)}, u32[]{:S(2)}) copy-start(bf16[2,256,256]{2,1,0:T(8,128)(2,1)} %constant.58.clone.first_ref) | copy-start | bytes 786436
  35.7 14.3 %collective-permute-start.3 = (bf16[512,128]{1,0:T(8,128)(2,1)}, bf16[512,128]{1,0:T(8,128)(2,1)S(1)}, u32[]{:S(2)}, u32[]{:S(2)}) collective-permute-start(bf16[512,128]{1,0:T(8,128)(2,1)} %get-tuple-element.19), channel_id=1, source_target_pairs={{0,3},{1,0},{2,1},{3,2},{4,7},{5,4},{6,5},{7,6},{8,11},{9,8},{10,9... | collective-permute-start | bytes 393224 | tf_op jit(solution)/shard_map/ppermute | solution.py:226
  38.4 11.5 %collective-permute-start.4 = (bf16[512,128]{1,0:T(8,128)(2,1)}, bf16[512,128]{1,0:T(8,128)(2,1)S(1)}, u32[]{:S(2)}, u32[]{:S(2)}) collective-permute-start(bf16[512,128]{1,0:T(8,128)(2,1)} %get-tuple-element.20), channel_id=1, source_target_pairs={{0,2},{1,3},{2,0},{3,1},{4,6},{5,7},{6,4},{7,5},{8,10},{9,11},{10,... | collective-permute-start | bytes 393224 | tf_op jit(solution)/shard_map/ppermute | solution.py:226
  42.8 7.2 %collective-permute-start.5 = (bf16[512,128]{1,0:T(8,128)(2,1)}, bf16[512,128]{1,0:T(8,128)(2,1)S(1)}, u32[]{:S(2)}, u32[]{:S(2)}) collective-permute-start(bf16[512,128]{1,0:T(8,128)(2,1)} %get-tuple-element.21), channel_id=1, source_target_pairs={{0,1},{1,2},{2,3},{3,0},{4,5},{5,6},{6,7},{7,4},{8,9},{9,10},{10,1... | collective-permute-start | bytes 393224 | tf_op jit(solution)/shard_map/ppermute | solution.py:226
  46.7 3.2 %copy-start.6 = (bf16[1,512,128]{2,1,0:T(8,128)(2,1)S(1)}, bf16[1,512,128]{2,1,0:T(8,128)(2,1)}, u32[]{:S(2)}) copy-start(bf16[1,512,128]{2,1,0:T(8,128)(2,1)} %param.15) | copy-start | bytes 393220
  50.3 29.3 %copy-start.7 = (bf16[2,256,256]{2,1,0:T(8,128)(2,1)S(1)}, bf16[2,256,256]{2,1,0:T(8,128)(2,1)}, u32[]{:S(2)}) copy-start(bf16[2,256,256]{2,1,0:T(8,128)(2,1)} %constant.65.clone.inv_second_ref) | copy-start | bytes 786436
  83.0 6.2 %copy-start.4 = (bf16[256,256]{1,0:T(8,128)(2,1)S(1)}, bf16[256,256]{1,0:T(8,128)(2,1)}, u32[]{:S(2)}) copy-start(bf16[256,256]{1,0:T(8,128)(2,1)} %constant.64.clone.gather_ref) | copy-start | bytes 393220
  83.0 21.9 %all-to-all-start.2 = ((bf16[128,8,128]{2,1,0:T(8,128)(2,1)}), bf16[128,8,128]{2,1,0:T(8,128)(2,1)S(1)}, u32[]{:S(2)}, u32[]{:S(2)}) async-start(bf16[128,8,128]{2,1,0:T(8,128)(2,1)} %bitcast.9), calls=%async_computation.2 | async-start | bytes 524288 | tf_op jit(solution)/shard_map/all_to_all | solution.py:222
  90.2 7.8 %collective-permute-start.8 = (bf16[512,128]{1,0:T(8,128)(2,1)S(1)}, bf16[512,128]{1,0:T(8,128)(2,1)S(1)}, u32[]{:S(2)}, u32[]{:S(2)}) collective-permute-start(bf16[512,128]{1,0:T(8,128)(2,1)S(1)} %get-tuple-element.24.refs_0_), channel_id=1, source_target_pairs={{0,3},{1,0},{2,1},{3,2},{4,7},{5,4},{6,5},{7,6},{8,11},{9,8},{10,9... | collective-permute-start | bytes 393224 | tf_op jit(solution)/shard_map/ppermute | solution.py:226
  92.1 7.5 %collective-permute-start.7 = (bf16[512,128]{1,0:T(8,128)(2,1)S(1)}, bf16[512,128]{1,0:T(8,128)(2,1)S(1)}, u32[]{:S(2)}, u32[]{:S(2)}) collective-permute-start(bf16[512,128]{1,0:T(8,128)(2,1)S(1)} %get-tuple-element.24.refs_0_), channel_id=1, source_target_pairs={{0,2},{1,3},{2,0},{3,1},{4,6},{5,7},{6,4},{7,5},{8,10},{9,11},{10,... | collective-permute-start | bytes 393224 | tf_op jit(solution)/shard_map/ppermute | solution.py:226
  95.5 7.2 %collective-permute-start.6 = (bf16[512,128]{1,0:T(8,128)(2,1)S(1)}, bf16[512,128]{1,0:T(8,128)(2,1)S(1)}, u32[]{:S(2)}, u32[]{:S(2)}) collective-permute-start(bf16[512,128]{1,0:T(8,128)(2,1)S(1)} %get-tuple-element.24.refs_0_), channel_id=1, source_target_pairs={{0,1},{1,2},{2,3},{3,0},{4,5},{5,6},{6,7},{7,4},{8,9},{9,10},{10,1... | collective-permute-start | bytes 393224 | tf_op jit(solution)/shard_map/ppermute | solution.py:226

commit v3 on v2

v3 whole, which is shorter than its diff:
```python
import functools
import math

import jax
import jax.numpy as jnp
import ml_dtypes
import numpy as np
from jax import lax
from jax.experimental import pallas as pl
from jax.experimental.pallas import tpu as pltpu
from jax.sharding import PartitionSpec as P

F32 = jnp.float32
BF16 = jnp.bfloat16
DP = 4
SEQ = 32
ROWS = 4
LANES = 128
CHUNK = 256
HALVES = 256
SLOTS = 8
TURN = 18
HALF = 128


def narrow(table):
    return table.astype(ml_dtypes.bfloat16)


@functools.cache
def tables():
    coarse = np.arange(HALF) + 0.5
    row = np.arange(SEQ * SLOTS)

    def outer(turn):
        place = (row // SLOTS + turn) % SEQ * ROWS + row % SLOTS % ROWS
        angle = 2 * math.pi / 256 * coarse[:, None] * place[None, :]
        full = np.concatenate([np.cos(angle), -np.sin(angle)])
        first = np.where(row[None, :] % SLOTS < ROWS, full, 0.0)
        return first, full - first

    first, second = outer(0)
    turned_first, turned_second = outer(TURN)
    fine = np.arange(LANES)
    angle = 2 * math.pi / LANES * np.outer(fine, fine)
    cos, sin = np.cos(angle), np.sin(angle)
    inner = np.block([[cos, -sin], [sin, cos]])
    angle = 2 * math.pi / 32768 * np.outer(coarse, fine)
    twist = np.stack([np.cos(angle), np.sin(angle)]).astype(np.float32)
    spread, turned_spread = np.zeros((256, 256)), np.zeros((256, 256))
    for channel in range(32):
        for slot in range(SLOTS):
            spread[channel * SLOTS + slot, slot * 32 + channel] = 1.0
            turned_spread[channel * SLOTS + slot, slot * 32 + (channel + TURN) % 32] = 1.0
    return {
        "turned_first": narrow(turned_first),
        "turned_second": narrow(turned_second),
        "fwd_second": narrow(second),
        "inv_first": narrow(first.T / 16384),
        "inv_second": narrow(second.T / 16384),
        "inner": narrow(inner),
        "inner_t": narrow(inner.T),
        "twist": twist,
        "spread": narrow(spread),
        "turned_spread": narrow(turned_spread),
    }


def dot(left, right):
    return jnp.dot(left, right, preferred_element_type=F32)


def split(x):
    high = x.astype(BF16)
    return high, (x - high.astype(F32)).astype(BF16)


def table_dot(table_ref, high, low=None):
    out = dot(table_ref[...], high)
    if low is not None:
        out = out + dot(table_ref[...], low)
    return out


def dot_table(x, table_ref):
    high, low = split(x)
    return dot(high, table_ref[...]) + dot(low, table_ref[...])


def lanes(tiles):
    return jnp.concatenate(tiles, axis=1)


def rows(tiles):
    return jnp.concatenate(tiles, axis=0)


def forward(signals, outer_ref, inner_ref, twist_ref):
    count = signals.shape[1] // LANES
    coarse = table_dot(outer_ref, signals)
    cos, sin = lanes([twist_ref[0]] * count), lanes([twist_ref[1]] * count)
    real, imag = coarse[:HALF], coarse[HALF:]
    real, imag = real * cos + imag * sin, imag * cos - real * sin
    cuts = [slice(k * LANES, (k + 1) * LANES) for k in range(count)]
    return dot_table(rows([lanes([real[:, cut], imag[:, cut]]) for cut in cuts]), inner_ref)


def inverse_inner(spectra, inner_t_ref, twist_ref):
    count = spectra.shape[0] // HALF
    coarse = dot_table(spectra, inner_t_ref)
    cos, sin = twist_ref[0], twist_ref[1]
    out = []
    for k in range(count):
        real, imag = coarse[k * HALF:(k + 1) * HALF, :LANES], coarse[k * HALF:(k + 1) * HALF, LANES:]
        out.append(rows([real * cos - imag * sin, imag * cos + real * sin]))
    return split(lanes(out))


def pack_inputs(values_ref, filt_ref, spread_ref, out_ref):
    dp = lax.axis_index("dp")
    start = pl.multiple_of(dp * LANES, LANES)
    quarter = filt_ref[pl.ds(start, LANES), :].T
    tiles = [values_ref[q * LANES:(q + 1) * LANES, :].astype(F32).T.astype(BF16) for q in range(ROWS)]
    tiles += [jnp.where(dp == q, quarter, 0.0).astype(BF16) for q in range(DP)]
    for part in range(4):
        block = jnp.concatenate([tile[part * 32:(part + 1) * 32] for tile in tiles], axis=0)
        out_ref[part * 256:(part + 1) * 256, :] = dot(spread_ref[...], block).astype(BF16)


def convolve(got_ref, first_ref, second_ref, inv_ref, inner_ref, inner_t_ref, twist_ref, conv_ref, vspec_ref, fspec_ref):
    size = SEQ * SLOTS
    parts = [got_ref[b * size:(b + 1) * size, :] for b in range(DP)]
    filt = ((parts[0].astype(F32) + parts[1].astype(F32)) + (parts[2].astype(F32) + parts[3].astype(F32))).astype(BF16)
    fspec = forward(filt, second_ref, inner_ref, twist_ref)
    fspec_ref[...] = fspec
    f_real, f_imag = fspec[:, :LANES], fspec[:, LANES:]
    vspec = forward(lanes(parts), first_ref, inner_ref, twist_ref)
    vspec_ref[...] = vspec
    spectra = []
    for b in range(DP):
        v_real, v_imag = vspec[b * HALF:(b + 1) * HALF, :LANES], vspec[b * HALF:(b + 1) * HALF, LANES:]
        spectra.append(lanes([v_real * f_real - v_imag * f_imag, v_real * f_imag + v_imag * f_real]))
    conv = table_dot(inv_ref, *inverse_inner(rows(spectra), inner_t_ref, twist_ref))
    for b in range(DP):
        conv_ref[b * size:(b + 1) * size, :] = conv[:, b * LANES:(b + 1) * LANES].astype(BF16)


def partial_grads(cot_ref, *refs):
    *refs, buffer, sems = refs
    count = len(refs) // 2
    copies = [
        pltpu.make_async_copy(cot_ref.at[pl.ds(k * HALVES, HALVES)], buffer.at[pl.ds(k * HALVES, HALVES)], sems.at[k])
        for k in range(2)
    ]
    for copy in copies:
        copy.start()
    columns = rows([ref[...] for ref in refs[:count]])
    for k, copy in enumerate(copies):
        block = slice(k * HALVES, (k + 1) * HALVES)
        copy.wait()
        out = lax.dot_general(
            buffer[block, :], columns, (((1,), (1,)), ((), ())), preferred_element_type=F32
        ).astype(BF16)
        for group, ref in enumerate(refs[count:]):
            ref[block, :] = out[:, group * LANES:(group + 1) * LANES]


def pack_grads(*refs):
    query_ref, conv_ref, spread_ref = refs[:3]
    pieces, (out_ref, grad_ref) = refs[3:-2], refs[-2:]
    grad = pieces[0][...].astype(F32)
    for piece in pieces[1:]:
        grad = grad + piece[...].astype(F32)
    grad_ref[...] = grad
    grad_conv = grad * query_ref[...].astype(F32)
    tiles = [grad_conv[q * LANES:(q + 1) * LANES, :].T.astype(BF16) for q in range(ROWS)]
    spread = spread_ref[:, 128:]
    for part in range(4):
        block = jnp.concatenate([tile[part * 32:(part + 1) * 32] for tile in tiles], axis=0)
        out_ref[part * 256:(part + 1) * 256, :] = (
            dot(spread, block) + conv_ref[part * 256:(part + 1) * 256, :].astype(F32)
        ).astype(BF16)


def gather_half(got_ref, gather):
    blocks = [dot(gather, got_ref[part * 256:(part + 1) * 256, :]) for part in range(4)]
    return [
        jnp.concatenate([block[q * 32:(q + 1) * 32] for block in blocks], axis=0).T for q in range(gather.shape[0] // 32)
    ]


def unpack_conv(got_ref, query_ref, grad_ref, gather_ref, gated_ref, grad_query_ref):
    for q, conv in enumerate(gather_half(got_ref, gather_ref[:128, :])):
        cut = slice(q * LANES, (q + 1) * LANES)
        gated_ref[cut, :] = (query_ref[cut, :].astype(F32) * conv).astype(BF16)
        grad_query_ref[cut, :] = (grad_ref[cut, :] * conv).astype(BF16)


def correlate(
    got_ref, vspec_ref, fspec_ref, second_ref, inv_first_ref, inv_second_ref, inner_ref, inner_t_ref, twist_ref, out_ref
):
    size = SEQ * SLOTS
    f_real, f_imag = fspec_ref[:, :LANES], fspec_ref[:, LANES:]
    sum_real = sum_imag = None
    spec = forward(
        lanes([got_ref[b * size:(b + 1) * size, :] for b in range(DP)]), second_ref, inner_ref, twist_ref
    )
    spectra = []
    for b in range(DP):
        block = slice(b * HALF, (b + 1) * HALF)
        real, imag = spec[block, :LANES], spec[block, LANES:]
        v_real, v_imag = vspec_ref[block, :LANES], vspec_ref[block, LANES:]
        part_real = real * v_real + imag * v_imag
        part_imag = imag * v_real - real * v_imag
        sum_real = part_real if b == 0 else sum_real + part_real
        sum_imag = part_imag if b == 0 else sum_imag + part_imag
        spectra.append(lanes([real * f_real + imag * f_imag, imag * f_real - real * f_imag]))
    spectra.append(lanes([sum_real, sum_imag]))
    high, low = inverse_inner(rows(spectra), inner_t_ref, twist_ref)
    cut = DP * LANES
    value = table_dot(inv_first_ref, high[:, :cut], low[:, :cut])
    filt = table_dot(inv_second_ref, high[:, cut:], low[:, cut:])
    for b in range(DP):
        out_ref[b * size:(b + 1) * size, :] = (value[:, b * LANES:(b + 1) * LANES] + filt).astype(BF16)


def unpack_grads(got_ref, gather_ref, value_ref, filt_ref):
    tiles = gather_half(got_ref, gather_ref[...])
    for q in range(ROWS):
        value_ref[q * LANES:(q + 1) * LANES, :] = tiles[q].astype(BF16)
        filt_ref[q * LANES:(q + 1) * LANES, :] = tiles[ROWS + q]


def project(gated_ref, *refs):
    *refs, out_ref, buffer, sems = refs
    count = len(refs)
    length = buffer.shape[0]
    rank = lax.axis_index("tensor")
    starts = [pl.multiple_of((rank + count - d) % count * length, length) for d in range(count)]
    gated = lanes([gated_ref[pl.ds(start, length), :] for start in starts])
    copies = []
    for k in range(buffer.shape[1] // CHUNK):
        cut = slice(k * CHUNK, (k + 1) * CHUNK)
        buffer[:, cut] = dot(gated, rows([ref[:, cut] for ref in refs])).astype(BF16)
        cut = pl.ds(k * CHUNK, CHUNK)
        copies.append(pltpu.make_async_copy(buffer.at[:, cut], out_ref.at[:, cut], sems.at[k]))
        copies[-1].start()
    for copy in copies:
        copy.wait()


COVER = pl.CostEstimate(flops=40_000_000_000, transcendentals=0, bytes_accessed=40_000_000)
COVERS = {"pack_inputs": COVER, "partial_grads": COVER}


def call(kernel, outs, *operands, **options):
    return pl.pallas_call(
        kernel,
        out_shape=outs,
        **options,
        name=kernel.__name__,
        cost_estimate=COVERS.get(kernel.__name__),
        compiler_params=pltpu.CompilerParams(vmem_limit_bytes=40 * 1024 * 1024),
    )(*operands)


def exchange(message, turn=0):
    shape = message.shape
    message = message.reshape(DP * SEQ, SLOTS, LANES)
    group = [b * SEQ + (s + turn) % SEQ for b in range(DP) for s in range(SEQ)]
    return lax.all_to_all(
        message, ("dp", "seq"), split_axis=0, concat_axis=0, tiled=True, axis_index_groups=[group] if turn else None
    ).reshape(shape)


def shifted(array, distance, count):
    return lax.ppermute(array, "tensor", [(i, (i + distance) % count) for i in range(count)])


def per_device(queries, values, filt, w_out, cotangent, count):
    t = tables()
    query = queries[0]
    length, width = query.shape
    features = cotangent.shape[2]
    rank = lax.axis_index("tensor")
    vmem = pl.BlockSpec(memory_space=pltpu.VMEM)
    message = jax.ShapeDtypeStruct((DP * SEQ * SLOTS, LANES), BF16)
    signal = jax.ShapeDtypeStruct((length, width), BF16)

    columns = []
    for d in range(count):
        piece = lax.dynamic_slice(w_out, (0, (rank + d) % count * features), (width, features))
        columns.append(shifted(piece, d, count) if d else piece)

    got = exchange(call(pack_inputs, message, values[0], filt, t["turned_spread"]), TURN)
    conv, value_spec, filt_spec = call(
        convolve,
        [
            message,
            jax.ShapeDtypeStruct((DP * HALF, 2 * LANES), F32),
            jax.ShapeDtypeStruct((HALF, 2 * LANES), F32),
        ],
        got, t["turned_first"], t["turned_second"], t["inv_first"], t["inner"], t["inner_t"], t["twist"],
    )
    partial = call(
        partial_grads, [signal] * count, pltpu.with_memory_space_constraint(cotangent[0], pltpu.HBM), *columns,
        in_specs=[pl.BlockSpec(memory_space=pltpu.HBM)] + [vmem] * count,
        scratch_shapes=[pltpu.VMEM((length, features), BF16), pltpu.SemaphoreType.DMA((2,))],
    )
    partial = [shifted(p, -d, count) if d else p for d, p in enumerate(partial)]
    outgoing, grad_gated = call(
        pack_grads, [message, jax.ShapeDtypeStruct((length, width), F32)], query, conv, t["spread"], *partial
    )
    got = exchange(outgoing)
    gated, grad_query = call(unpack_conv, [signal, signal], got, query, grad_gated, t["spread"].T)
    gathered = lax.all_gather(gated, "tensor", axis=0, tiled=True)
    got = exchange(
        call(
            correlate, message, got, value_spec, filt_spec, t["fwd_second"], t["inv_first"], t["inv_second"],
            t["inner"], t["inner_t"], t["twist"],
        )
    )
    mixed = call(
        project, jax.ShapeDtypeStruct((length, features), BF16), gathered, *columns,
        out_specs=pl.BlockSpec(memory_space=pltpu.HBM),
        scratch_shapes=[pltpu.VMEM((length, features), BF16), pltpu.SemaphoreType.DMA((features // CHUNK,))],
    )
    grad_value, grad_filt = call(
        unpack_grads, [signal, jax.ShapeDtypeStruct((length, width), F32)], got, t["spread"].T
    )
    return (mixed[None], grad_query[None], grad_value[None], grad_filt)


def solution(mesh):
    placed = (
        P("dp", "seq", "tensor"),
        P("dp", "seq", "tensor"),
        P("seq", "tensor"),
        P("tensor", None),
        P("dp", "seq", "tensor"),
    )
    return jax.shard_map(
        functools.partial(per_device, count=mesh.shape["tensor"]),
        mesh=mesh,
        in_specs=placed,
        out_specs=(
            P("dp", "seq", "tensor"),
            P("dp", "seq", "tensor"),
            P("dp", "seq", "tensor"),
            P("seq", "tensor"),
        ),
        check_vma=False,
    )
```

time: 107 us -> 98.3 us (0.919)
  starting transfers between devices: 52.1 us -> 47.6 us
  Pallas kernels: 14.3 us -> 10.4 us
  blocking collectives: 29.2 us -> 31.9 us
  waiting for transfers between devices: 6.71 us -> 4.56 us
  local copies, waits for them, and re-layouts: 2.6 us -> 1.41 us
    all_gather x0 -> x1, blocking collectives: none -> 10.8 us  [per_device(): gathered = lax.all_gather(gated, 'tensor', axis=0, tiled=True)]
    all_to_all x1, blocking collectives: 29.2 us -> 21.1 us  [exchange(): lax.all_to_all(message, ('dp', 'seq'), split_axis=0, concat_axis=0, tiled...]
    ppermute x9 -> x6, starting transfers between devices: 27.5 us -> 19.8 us  [shifted(): lax.ppermute(array, 'tensor', [(i, (i + distance) % count) for i in range...]
    pallas_call x8, Pallas kernels: 14.3 us -> 10.4 us  [call(): pl.pallas_call(kernel, out_shape=outs, **options, name=kernel.__name__, c...]
    all_to_all x2, starting transfers between devices: 24.6 us -> 27.8 us  [exchange(): lax.all_to_all(message, ('dp', 'seq'), split_axis=0, concat_axis=0, tiled...]
    unnamed x26 -> x28, local copies, waits for them, and re-layouts: 1.28 us -> 0.09 us
    ppermute x9 -> x6, waiting for transfers between devices: 4.74 us -> 3.61 us  [shifted(): lax.ppermute(array, 'tensor', [(i, (i + distance) % count) for i in range...]
  transfers between devices with their start and end apart: 11 -> 8, of which waited for: 3 -> 3; matrix products, arithmetic and copies ran while one was open for 0% -> 0% of each run, Pallas kernels for 9% -> 7%
where the time goes in v3:
time: 98.3 us; the launch traced here: 96.9 us
  starting transfers between devices  47.6 us (48%)
  blocking collectives  31.9 us (32%)
  Pallas kernels  10.4 us (11%)
  waiting for transfers between devices  4.56 us (5%)
  local copies, waits for them, and re-layouts  1.41 us (1%)
  between operations  1.01 us (1%)
    all_to_all x2, starting transfers between devices, exchange(): lax.all_to_all(message, ('dp', 'seq'), split_axis=0, concat_axis=0, tiled...  27.8 us
    all_to_all x1, blocking collectives, exchange(): lax.all_to_all(message, ('dp', 'seq'), split_axis=0, concat_axis=0, tiled...  21.1 us
    ppermute x6, starting transfers between devices, shifted(): lax.ppermute(array, 'tensor', [(i, (i + distance) % count) for i in range...  19.8 us
    all_gather x1, blocking collectives, per_device(): gathered = lax.all_gather(gated, 'tensor', axis=0, tiled=True)  10.8 us
    pallas_call x8, Pallas kernels, call(): pl.pallas_call(kernel, out_shape=outs, **options, name=kernel.__name__, c...  10.4 us
    ppermute x6, waiting for transfers between devices, shifted(): lax.ppermute(array, 'tensor', [(i, (i + distance) % count) for i in range...  3.61 us
  transfers between devices with their start and end apart: 8, of which 3 were waited for; matrix products, arithmetic and copies ran while one was open for 0% of the time, Pallas kernels for 7%

profile of v3, /device:TPU:1, one launch (start us, length us, event | category | flops | bytes accessed | tf_op | source)
XLA Modules:
  0.0 96.9 jit_solution(6039002168008970718)
XLA Ops:
  0.7 0.0 copy-start.11
  0.7 0.0 copy-start.12
  0.7 0.0 copy-start.13
  0.7 1.3 %constant_dynamic-slice_fusion = (bf16[128,1024]{1,0:T(8,128)(2,1)S(1)}, bf16[128,1024]{1,0:T(8,128)(2,1)S(1)}, bf16[128,1024]{1,0:T(8,128)(2,1)S(1)}, bf16[128,1024]{1,0:T(8,128)(2,1)S(1)}) fusion(bf16[128,4096]{1,0:T(8,128)(2,1)} %param.20, s32[]{:T(128)S(6)} %select_n.38, s32[]{:T(128)S(6)} %select_n.34, s32[]{:T(128)S(6)} %select_n.32, s32[]{:T(128)S(6)} %select_n.36), kind=kLoop, calls=%fused_computation | loop fusion | bytes 2097168 | tf_op jit(solution)/shard_map/dynamic_slice | solution.py:292
  2.0 5.2 %collective-permute-start.2 = (bf16[128,1024]{1,0:T(8,128)(2,1)S(1)}, bf16[128,1024]{1,0:T(8,128)(2,1)S(1)}, u32[]{:S(2)}, u32[]{:S(2)}) collective-permute-start(bf16[128,1024]{1,0:T(8,128)(2,1)S(1)} %get-tuple-element.30), channel_id=1, source_target_pairs={{0,3},{1,0},{2,1},{3,2},{4,7},{5,4},{6,5},{7,6},{8,11},{9,8},{10,9... | collective-permute-start | bytes 786440 | tf_op jit(solution)/shard_map/ppermute | solution.py:277
  7.3 1.9 %collective-permute-start = (bf16[128,1024]{1,0:T(8,128)(2,1)S(1)}, bf16[128,1024]{1,0:T(8,128)(2,1)S(1)}, u32[]{:S(2)}, u32[]{:S(2)}) collective-permute-start(bf16[128,1024]{1,0:T(8,128)(2,1)S(1)} %get-tuple-element.31), channel_id=1, source_target_pairs={{0,1},{1,2},{2,3},{3,0},{4,5},{5,6},{6,7},{7,4},{8,9},{9,10},{10,1... | collective-permute-start | bytes 786440 | tf_op jit(solution)/shard_map/ppermute | solution.py:277
  9.2 3.6 %collective-permute-start.1 = (bf16[128,1024]{1,0:T(8,128)(2,1)S(1)}, bf16[128,1024]{1,0:T(8,128)(2,1)S(1)}, u32[]{:S(2)}, u32[]{:S(2)}) collective-permute-start(bf16[128,1024]{1,0:T(8,128)(2,1)S(1)} %get-tuple-element.33), channel_id=1, source_target_pairs={{0,2},{1,3},{2,0},{3,1},{4,6},{5,7},{6,4},{7,5},{8,10},{9,11},{10,... | collective-permute-start | bytes 786440 | tf_op jit(solution)/shard_map/ppermute | solution.py:277
  12.8 0.0 copy-done.11
  12.8 0.0 copy-done.12
  12.9 0.0 copy-done.13
  12.9 1.1 %pack_inputs.1 = bf16[1024,128]{1,0:T(8,128)(2,1)} custom-call(bf16[512,128]{1,0:T(8,128)(2,1)S(1)} %bitcast.19, f32[512,128]{1,0:T(8,128)S(1)} %copy-done.11, bf16[256,256]{1,0:T(8,128)(2,1)S(1)} %copy-done.13), custom_call_target="tpu_custom_call" | custom-call | flops 40000000000 | bytes 40000000 | tf_op jit(solution)/shard_map/pack_inputs/pallas_call | solution.py:257
  14.0 21.7 %all-to-all-start = ((bf16[128,8,128]{2,1,0:T(8,128)(2,1)}), bf16[128,8,128]{2,1,0:T(8,128)(2,1)S(1)}, u32[]{:S(2)}, u32[]{:S(2)}) async-start(bf16[128,8,128]{2,1,0:T(8,128)(2,1)} %bitcast.2), calls=%async_computation | async-start | bytes 524288 | tf_op jit(solution)/shard_map/all_to_all | solution.py:271
  35.7 0.0 collective-permute-done.2.refs_3_
  35.7 0.0 collective-permute-done.refs_1_
  35.7 0.0 collective-permute-done.1.refs_2_
  35.7 0.0 copy-start.2
  35.7 0.0 copy-start.3
  35.7 0.0 copy-start.4
  35.7 0.0 copy-start.5
  35.7 0.0 copy-start.7
  35.7 0.0 copy-start.8
  35.8 2.1 %partial_grads.1 = (bf16[512,128]{1,0:T(8,128)(2,1)S(1)}, bf16[512,128]{1,0:T(8,128)(2,1)S(1)}, bf16[512,128]{1,0:T(8,128)(2,1)S(1)}, bf16[512,128]{1,0:T(8,128)(2,1)S(1)}) custom-call(bf16[512,1024]{1,0:T(8,128)(2,1)} %bitcast.21, bf16[128,1024]{1,0:T(8,128)(2,1)S(1)} %get-tuple-element.32.refs_0_, bf16[128,1024]{1,0:T(8,128)(2,1)S(1)} %collective-permute-done.refs_1_, ...), custom_call_target="tpu_custom_call" | custom-call | flops 40000000000 | bytes 40000000 | tf_op jit(solution)/shard_map/partial_grads/pallas_call | solution.py:257
  37.9 2.8 %collective-permute-start.3 = (bf16[512,128]{1,0:T(8,128)(2,1)S(1)}, bf16[512,128]{1,0:T(8,128)(2,1)S(1)}, u32[]{:S(2)}, u32[]{:S(2)}) collective-permute-start(bf16[512,128]{1,0:T(8,128)(2,1)S(1)} %get-tuple-element.19), channel_id=1, source_target_pairs={{0,3},{1,0},{2,1},{3,2},{4,7},{5,4},{6,5},{7,6},{8,11},{9,8},{10,9... | collective-permute-start | bytes 393224 | tf_op jit(solution)/shard_map/ppermute | solution.py:277
  40.7 4.4 %collective-permute-start.4 = (bf16[512,128]{1,0:T(8,128)(2,1)S(1)}, bf16[512,128]{1,0:T(8,128)(2,1)S(1)}, u32[]{:S(2)}, u32[]{:S(2)}) collective-permute-start(bf16[512,128]{1,0:T(8,128)(2,1)S(1)} %get-tuple-element.20), channel_id=1, source_target_pairs={{0,2},{1,3},{2,0},{3,1},{4,6},{5,7},{6,4},{7,5},{8,10},{9,11},{10,... | collective-permute-start | bytes 393224 | tf_op jit(solution)/shard_map/ppermute | solution.py:277
  45.0 1.9 %collective-permute-start.5 = (bf16[512,128]{1,0:T(8,128)(2,1)S(1)}, bf16[512,128]{1,0:T(8,128)(2,1)S(1)}, u32[]{:S(2)}, u32[]{:S(2)}) collective-permute-start(bf16[512,128]{1,0:T(8,128)(2,1)S(1)} %get-tuple-element.21), channel_id=1, source_target_pairs={{0,1},{1,2},{2,3},{3,0},{4,5},{5,6},{6,7},{7,4},{8,9},{9,10},{10,1... | collective-permute-start | bytes 393224 | tf_op jit(solution)/shard_map/ppermute | solution.py:277
  47.0 0.0 all-to-all-done
  47.0 0.0 copy-done.2
  47.0 0.0 copy-done.3
  47.0 0.0 copy-done.4
  47.0 0.0 copy-done.5
  47.0 0.0 copy-done.7
  47.0 0.0 copy-done.8
  47.0 0.0 copy-start.1
  47.0 0.0 copy-start.6
  47.1 1.3 %convolve.1 = (bf16[1024,128]{1,0:T(8,128)(2,1)S(1)}, f32[512,256]{1,0:T(8,128)S(1)}, f32[128,256]{1,0:T(8,128)S(1)}) custom-call(bf16[1024,128]{1,0:T(8,128)(2,1)S(1)} %bitcast.15, bf16[256,256]{1,0:T(8,128)(2,1)S(1)} %copy-done.8, bf16[256,256]{1,0:T(8,128)(2,1)S(1)} %copy-done.7, bf16[256,256]{1,0:T(8,128)(2,1)S(1)} %copy-done.5, ...), custom_call_target="tpu_custom_call" | custom-call | tf_op jit(solution)/shard_map/convolve/pallas_call | solution.py:257
  48.3 0.0 collective-permute-done.3.refs_4_
  48.4 0.1 collective-permute-done.4.refs_5_
  48.5 3.5 %collective-permute-done.5.refs_6_ = bf16[512,128]{1,0:T(8,128)(2,1)S(1)} collective-permute-done((bf16[512,128]{1,0:T(8,128)(2,1)S(1)}, bf16[512,128]{1,0:T(8,128)(2,1)S(1)}, u32[]{:S(2)}, u32[]{:S(2)}) %collective-permute-start.5) | collective-permute-done | bytes 131104 | tf_op jit(solution)/shard_map/ppermute | solution.py:277
  52.0 0.0 copy-done.1
  52.0 0.0 copy-done.6
  52.0 0.3 pack_grads.1
  52.3 0.0 copy-start.9
  52.3 0.0 copy-start.10
  52.3 21.1 %all_to_all.15 = bf16[128,8,128]{2,1,0:T(8,128)(2,1)S(1)} all-to-all(bf16[128,8,128]{2,1,0:T(8,128)(2,1)S(1)} %bitcast.18), channel_id=1, replica_groups=mesh['dp'=4,'seq'=32,'tensor'=4] {'dp','seq'}, dimensions={0} | all-to-all | bytes 524288 | tf_op jit(solution)/shard_map/all_to_all | solution.py:271
  73.5 0.0 copy-done.9
  73.5 0.0 copy-done.10
  73.5 1.9 %correlate.1 = bf16[1024,128]{1,0:T(8,128)(2,1)} custom-call(bf16[1024,128]{1,0:T(8,128)(2,1)S(1)} %bitcast.12, f32[512,256]{1,0:T(8,128)S(1)} %get-tuple-element.26.vspec_ref, f32[128,256]{1,0:T(8,128)S(1)} %get-tuple-element.27.fspec_ref, bf16[256,256]{1,0:T(8,128)(2,1)S(1)} %copy-done.10, bf16[256,256]{1,0:T(8,128)(2,1)S(1)} %copy-done.5, ...), custom_call_target="tpu_custom_call" | custom-call | tf_op jit(solution)/shard_map/correlate/pallas_call | solution.py:257
  75.4 0.0 copy-start
  75.4 6.1 %all-to-all-start.2 = ((bf16[128,8,128]{2,1,0:T(8,128)(2,1)}), bf16[128,8,128]{2,1,0:T(8,128)(2,1)S(1)}, u32[]{:S(2)}, u32[]{:S(2)}) async-start(bf16[128,8,128]{2,1,0:T(8,128)(2,1)} %bitcast.9), calls=%async_computation.2 | async-start | bytes 524288 | tf_op jit(solution)/shard_map/all_to_all | solution.py:271
  81.6 0.0 copy-done
  81.6 1.0 unpack_conv.1
  82.5 10.8 %all_gather.3.gated_ref = bf16[2048,128]{1,0:T(8,128)(2,1)S(1)} all-gather(bf16[512,128]{1,0:T(8,128)(2,1)S(1)} %get-tuple-element.24), channel_id=1, replica_groups=mesh['dp'=4,'seq'=32,'tensor'=4] {'tensor'}, dimensions={0}, use_global_device_ids=true | all-gather | bytes 655360 | tf_op jit(solution)/shard_map/all_gather | solution.py:316
  93.3 1.6 %project.1 = bf16[512,1024]{1,0:T(8,128)(2,1)} custom-call(bf16[2048,128]{1,0:T(8,128)(2,1)S(1)} %all_gather.3.gated_ref, bf16[128,1024]{1,0:T(8,128)(2,1)S(1)} %get-tuple-element.32.refs_0_, bf16[128,1024]{1,0:T(8,128)(2,1)S(1)} %collective-permute-done.refs_1_, bf16[128,1024]{1,0:T(8,128)(2,1)S(1)} %collective-permute-done.1.refs_2_, ...), custom_call_target="tpu_custom_call" | custom-call | tf_op jit(solution)/shard_map/project/pallas_call | solution.py:257
  94.9 0.9 all-to-all-done.2
  95.8 1.1 %unpack_grads.1 = (bf16[512,128]{1,0:T(8,128)(2,1)}, f32[512,128]{1,0:T(8,128)}) custom-call(bf16[1024,128]{1,0:T(8,128)(2,1)S(1)} %bitcast.14, bf16[256,256]{1,0:T(8,128)(2,1)S(1)} %copy-done), custom_call_target="tpu_custom_call" | custom-call | tf_op jit(solution)/shard_map/unpack_grads/pallas_call | solution.py:257
Async XLA Ops:
  0.7 12.1 %copy-start.11 = (f32[512,128]{1,0:T(8,128)S(1)}, f32[512,128]{1,0:T(8,128)}, u32[]{:S(2)}) copy-start(f32[512,128]{1,0:T(8,128)} %filt_ref.1) | copy-start | bytes 786436
  0.7 12.1 %copy-start.12 = (bf16[1,512,128]{2,1,0:T(8,128)(2,1)S(1)}, bf16[1,512,128]{2,1,0:T(8,128)(2,1)}, u32[]{:S(2)}) copy-start(bf16[1,512,128]{2,1,0:T(8,128)(2,1)} %param.18) | copy-start | bytes 393220
  0.7 12.1 %copy-start.13 = (bf16[256,256]{1,0:T(8,128)(2,1)S(1)}, bf16[256,256]{1,0:T(8,128)(2,1)}, u32[]{:S(2)}) copy-start(bf16[256,256]{1,0:T(8,128)(2,1)} %constant.61.clone.spread_ref) | copy-start | bytes 393220
  2.0 33.6 %collective-permute-start.2 = (bf16[128,1024]{1,0:T(8,128)(2,1)S(1)}, bf16[128,1024]{1,0:T(8,128)(2,1)S(1)}, u32[]{:S(2)}, u32[]{:S(2)}) collective-permute-start(bf16[128,1024]{1,0:T(8,128)(2,1)S(1)} %get-tuple-element.30), channel_id=1, source_target_pairs={{0,3},{1,0},{2,1},{3,2},{4,7},{5,4},{6,5},{7,6},{8,11},{9,8},{10,9... | collective-permute-start | bytes 786440 | tf_op jit(solution)/shard_map/ppermute | solution.py:277
  7.3 28.4 %collective-permute-start = (bf16[128,1024]{1,0:T(8,128)(2,1)S(1)}, bf16[128,1024]{1,0:T(8,128)(2,1)S(1)}, u32[]{:S(2)}, u32[]{:S(2)}) collective-permute-start(bf16[128,1024]{1,0:T(8,128)(2,1)S(1)} %get-tuple-element.31), channel_id=1, source_target_pairs={{0,1},{1,2},{2,3},{3,0},{4,5},{5,6},{6,7},{7,4},{8,9},{9,10},{10,1... | collective-permute-start | bytes 786440 | tf_op jit(solution)/shard_map/ppermute | solution.py:277
  9.2 26.5 %collective-permute-start.1 = (bf16[128,1024]{1,0:T(8,128)(2,1)S(1)}, bf16[128,1024]{1,0:T(8,128)(2,1)S(1)}, u32[]{:S(2)}, u32[]{:S(2)}) collective-permute-start(bf16[128,1024]{1,0:T(8,128)(2,1)S(1)} %get-tuple-element.33), channel_id=1, source_target_pairs={{0,2},{1,3},{2,0},{3,1},{4,6},{5,7},{6,4},{7,5},{8,10},{9,11},{10,... | collective-permute-start | bytes 786440 | tf_op jit(solution)/shard_map/ppermute | solution.py:277
  14.0 33.0 %all-to-all-start = ((bf16[128,8,128]{2,1,0:T(8,128)(2,1)}), bf16[128,8,128]{2,1,0:T(8,128)(2,1)S(1)}, u32[]{:S(2)}, u32[]{:S(2)}) async-start(bf16[128,8,128]{2,1,0:T(8,128)(2,1)} %bitcast.2), calls=%async_computation | async-start | bytes 524288 | tf_op jit(solution)/shard_map/all_to_all | solution.py:271
  35.7 11.3 %copy-start.2 = (f32[2,128,128]{2,1,0:T(8,128)S(1)}, f32[2,128,128]{2,1,0:T(8,128)}, u32[]{:S(2)}) copy-start(f32[2,128,128]{2,1,0:T(8,128)} %constant.67.clone.twist_ref) | copy-start | bytes 393220
  35.7 11.3 %copy-start.3 = (bf16[256,256]{1,0:T(8,128)(2,1)S(1)}, bf16[256,256]{1,0:T(8,128)(2,1)}, u32[]{:S(2)}) copy-start(bf16[256,256]{1,0:T(8,128)(2,1)} %constant.66.clone.inner_t_ref) | copy-start | bytes 393220
  35.7 11.3 %copy-start.4 = (bf16[256,256]{1,0:T(8,128)(2,1)S(1)}, bf16[256,256]{1,0:T(8,128)(2,1)}, u32[]{:S(2)}) copy-start(bf16[256,256]{1,0:T(8,128)(2,1)} %constant.65.clone.inner_ref) | copy-start | bytes 393220
  35.7 11.3 %copy-start.5 = (bf16[256,256]{1,0:T(8,128)(2,1)S(1)}, bf16[256,256]{1,0:T(8,128)(2,1)}, u32[]{:S(2)}) copy-start(bf16[256,256]{1,0:T(8,128)(2,1)} %constant.64.clone.inv_ref.inv_first_ref) | copy-start | bytes 393220
  35.7 11.3 %copy-start.7 = (bf16[256,256]{1,0:T(8,128)(2,1)S(1)}, bf16[256,256]{1,0:T(8,128)(2,1)}, u32[]{:S(2)}) copy-start(bf16[256,256]{1,0:T(8,128)(2,1)} %constant.63.clone.second_ref) | copy-start | bytes 393220
  35.7 11.3 %copy-start.8 = (bf16[256,256]{1,0:T(8,128)(2,1)S(1)}, bf16[256,256]{1,0:T(8,128)(2,1)}, u32[]{:S(2)}) copy-start(bf16[256,256]{1,0:T(8,128)(2,1)} %constant.62.clone.first_ref) | copy-start | bytes 393220
  37.9 10.5 %collective-permute-start.3 = (bf16[512,128]{1,0:T(8,128)(2,1)S(1)}, bf16[512,128]{1,0:T(8,128)(2,1)S(1)}, u32[]{:S(2)}, u32[]{:S(2)}) collective-permute-start(bf16[512,128]{1,0:T(8,128)(2,1)S(1)} %get-tuple-element.19), channel_id=1, source_target_pairs={{0,3},{1,0},{2,1},{3,2},{4,7},{5,4},{6,5},{7,6},{8,11},{9,8},{10,9... | collective-permute-start | bytes 393224 | tf_op jit(solution)/shard_map/ppermute | solution.py:277
  40.7 7.8 %collective-permute-start.4 = (bf16[512,128]{1,0:T(8,128)(2,1)S(1)}, bf16[512,128]{1,0:T(8,128)(2,1)S(1)}, u32[]{:S(2)}, u32[]{:S(2)}) collective-permute-start(bf16[512,128]{1,0:T(8,128)(2,1)S(1)} %get-tuple-element.20), channel_id=1, source_target_pairs={{0,2},{1,3},{2,0},{3,1},{4,6},{5,7},{6,4},{7,5},{8,10},{9,11},{10,... | collective-permute-start | bytes 393224 | tf_op jit(solution)/shard_map/ppermute | solution.py:277
  45.0 6.9 %collective-permute-start.5 = (bf16[512,128]{1,0:T(8,128)(2,1)S(1)}, bf16[512,128]{1,0:T(8,128)(2,1)S(1)}, u32[]{:S(2)}, u32[]{:S(2)}) collective-permute-start(bf16[512,128]{1,0:T(8,128)(2,1)S(1)} %get-tuple-element.21), channel_id=1, source_target_pairs={{0,1},{1,2},{2,3},{3,0},{4,5},{5,6},{6,7},{7,4},{8,9},{9,10},{10,1... | collective-permute-start | bytes 393224 | tf_op jit(solution)/shard_map/ppermute | solution.py:277
  47.0 4.9 %copy-start.1 = (bf16[1,512,128]{2,1,0:T(8,128)(2,1)S(1)}, bf16[1,512,128]{2,1,0:T(8,128)(2,1)}, u32[]{:S(2)}) copy-start(bf16[1,512,128]{2,1,0:T(8,128)(2,1)} %param.17) | copy-start | bytes 393220
  47.0 4.9 %copy-start.6 = (bf16[256,256]{1,0:T(8,128)(2,1)S(1)}, bf16[256,256]{1,0:T(8,128)(2,1)}, u32[]{:S(2)}) copy-start(bf16[256,256]{1,0:T(8,128)(2,1)} %constant.68.clone.refs_2_) | copy-start | bytes 393220
  52.3 21.2 %copy-start.9 = (bf16[256,256]{1,0:T(8,128)(2,1)S(1)}, bf16[256,256]{1,0:T(8,128)(2,1)}, u32[]{:S(2)}) copy-start(bf16[256,256]{1,0:T(8,128)(2,1)} %constant.71.clone.inv_second_ref) | copy-start | bytes 393220
  52.3 21.2 %copy-start.10 = (bf16[256,256]{1,0:T(8,128)(2,1)S(1)}, bf16[256,256]{1,0:T(8,128)(2,1)}, u32[]{:S(2)}) copy-start(bf16[256,256]{1,0:T(8,128)(2,1)} %constant.70.clone.second_ref) | copy-start | bytes 393220
  75.4 6.1 %copy-start = (bf16[256,256]{1,0:T(8,128)(2,1)S(1)}, bf16[256,256]{1,0:T(8,128)(2,1)}, u32[]{:S(2)}) copy-start(bf16[256,256]{1,0:T(8,128)(2,1)} %constant.69.clone.gather_ref) | copy-start | bytes 393220
  75.4 20.4 %all-to-all-start.2 = ((bf16[128,8,128]{2,1,0:T(8,128)(2,1)}), bf16[128,8,128]{2,1,0:T(8,128)(2,1)S(1)}, u32[]{:S(2)}, u32[]{:S(2)}) async-start(bf16[128,8,128]{2,1,0:T(8,128)(2,1)} %bitcast.9), calls=%async_computation.2 | async-start | bytes 524288 | tf_op jit(solution)/shard_map/all_to_all | solution.py:271

commit v4 on v3

--- a/solution.py
+++ b/solution.py
@@ -19,7 +19,7 @@
 CHUNK = 256
 HALVES = 256
 SLOTS = 8
-TURN = 18
+TURN = 22
 HALF = 128
 
 
@@ -70,23 +70,6 @@
     return jnp.dot(left, right, preferred_element_type=F32)
 
 
-def split(x):
-    high = x.astype(BF16)
-    return high, (x - high.astype(F32)).astype(BF16)
-
-
-def table_dot(table_ref, high, low=None):
-    out = dot(table_ref[...], high)
-    if low is not None:
-        out = out + dot(table_ref[...], low)
-    return out
-
-
-def dot_table(x, table_ref):
-    high, low = split(x)
-    return dot(high, table_ref[...]) + dot(low, table_ref[...])
-
-
 def lanes(tiles):
     return jnp.concatenate(tiles, axis=1)
 
@@ -97,23 +80,23 @@
 
 def forward(signals, outer_ref, inner_ref, twist_ref):
     count = signals.shape[1] // LANES
-    coarse = table_dot(outer_ref, signals)
+    coarse = dot(outer_ref[...], signals)
     cos, sin = lanes([twist_ref[0]] * count), lanes([twist_ref[1]] * count)
     real, imag = coarse[:HALF], coarse[HALF:]
     real, imag = real * cos + imag * sin, imag * cos - real * sin
     cuts = [slice(k * LANES, (k + 1) * LANES) for k in range(count)]
-    return dot_table(rows([lanes([real[:, cut], imag[:, cut]]) for cut in cuts]), inner_ref)
+    return dot(rows([lanes([real[:, cut], imag[:, cut]]) for cut in cuts]).astype(BF16), inner_ref[...])
 
 
 def inverse_inner(spectra, inner_t_ref, twist_ref):
     count = spectra.shape[0] // HALF
-    coarse = dot_table(spectra, inner_t_ref)
+    coarse = dot(spectra.astype(BF16), inner_t_ref[...])
     cos, sin = twist_ref[0], twist_ref[1]
     out = []
     for k in range(count):
         real, imag = coarse[k * HALF:(k + 1) * HALF, :LANES], coarse[k * HALF:(k + 1) * HALF, LANES:]
         out.append(rows([real * cos - imag * sin, imag * cos + real * sin]))
-    return split(lanes(out))
+    return lanes(out).astype(BF16)
 
 
 def pack_inputs(values_ref, filt_ref, spread_ref, out_ref):
@@ -140,7 +123,7 @@
     for b in range(DP):
         v_real, v_imag = vspec[b * HALF:(b + 1) * HALF, :LANES], vspec[b * HALF:(b + 1) * HALF, LANES:]
         spectra.append(lanes([v_real * f_real - v_imag * f_imag, v_real * f_imag + v_imag * f_real]))
-    conv = table_dot(inv_ref, *inverse_inner(rows(spectra), inner_t_ref, twist_ref))
+    conv = dot(inv_ref[...], inverse_inner(rows(spectra), inner_t_ref, twist_ref))
     for b in range(DP):
         conv_ref[b * size:(b + 1) * size, :] = conv[:, b * LANES:(b + 1) * LANES].astype(BF16)
 
@@ -216,35 +199,39 @@
         sum_imag = part_imag if b == 0 else sum_imag + part_imag
         spectra.append(lanes([real * f_real + imag * f_imag, imag * f_real - real * f_imag]))
     spectra.append(lanes([sum_real, sum_imag]))
-    high, low = inverse_inner(rows(spectra), inner_t_ref, twist_ref)
+    coarse = inverse_inner(rows(spectra), inner_t_ref, twist_ref)
     cut = DP * LANES
-    value = table_dot(inv_first_ref, high[:, :cut], low[:, :cut])
-    filt = table_dot(inv_second_ref, high[:, cut:], low[:, cut:])
+    value = dot(inv_first_ref[...], coarse[:, :cut])
+    filt = dot(inv_second_ref[...], coarse[:, cut:])
     for b in range(DP):
         out_ref[b * size:(b + 1) * size, :] = (value[:, b * LANES:(b + 1) * LANES] + filt).astype(BF16)
 
 
-def unpack_grads(got_ref, gather_ref, value_ref, filt_ref):
-    tiles = gather_half(got_ref, gather_ref[...])
-    for q in range(ROWS):
-        value_ref[q * LANES:(q + 1) * LANES, :] = tiles[q].astype(BF16)
-        filt_ref[q * LANES:(q + 1) * LANES, :] = tiles[ROWS + q]
-
-
-def project(gated_ref, *refs):
-    *refs, out_ref, buffer, sems = refs
+def finish(gated_ref, *refs):
+    *refs, got_ref, gather_ref, mixed_ref, value_ref, filt_ref, mixed, value, filt, sems = refs
     count = len(refs)
-    length = buffer.shape[0]
+    length = mixed.shape[0]
     rank = lax.axis_index("tensor")
     starts = [pl.multiple_of((rank + count - d) % count * length, length) for d in range(count)]
     gated = lanes([gated_ref[pl.ds(start, length), :] for start in starts])
     copies = []
-    for k in range(buffer.shape[1] // CHUNK):
+
+    def send(buffer, ref, index):
+        copies.append(pltpu.make_async_copy(buffer.at[index], ref.at[index], sems.at[len(copies)]))
+        copies[-1].start()
+
+    for k in range(mixed.shape[1] // CHUNK):
         cut = slice(k * CHUNK, (k + 1) * CHUNK)
-        buffer[:, cut] = dot(gated, rows([ref[:, cut] for ref in refs])).astype(BF16)
-        cut = pl.ds(k * CHUNK, CHUNK)
-        copies.append(pltpu.make_async_copy(buffer.at[:, cut], out_ref.at[:, cut], sems.at[k]))
-        copies[-1].start()
+        mixed[:, cut] = dot(gated, rows([ref[:, cut] for ref in refs])).astype(BF16)
+        send(mixed, mixed_ref, (slice(None), pl.ds(k * CHUNK, CHUNK)))
+    tiles = gather_half(got_ref, gather_ref[...])
+    for q in range(ROWS):
+        cut = slice(q * LANES, (q + 1) * LANES)
+        value[cut, :] = tiles[q].astype(BF16)
+        filt[cut, :] = tiles[ROWS + q]
+    everything = (pl.ds(0, length), slice(None))
+    send(value, value_ref, everything)
+    send(filt, filt_ref, everything)
     for copy in copies:
         copy.wait()
 
@@ -320,13 +307,18 @@
             t["inner"], t["inner_t"], t["twist"],
         )
     )
-    mixed = call(
-        project, jax.ShapeDtypeStruct((length, features), BF16), gathered, *columns,
-        out_specs=pl.BlockSpec(memory_space=pltpu.HBM),
-        scratch_shapes=[pltpu.VMEM((length, features), BF16), pltpu.SemaphoreType.DMA((features // CHUNK,))],
-    )
-    grad_value, grad_filt = call(
-        unpack_grads, [signal, jax.ShapeDtypeStruct((length, width), F32)], got, t["spread"].T
+    wide = (length, features)
+    mixed, grad_value, grad_filt = call(
+        finish,
+        [jax.ShapeDtypeStruct(wide, BF16), signal, jax.ShapeDtypeStruct((length, width), F32)],
+        gathered, *columns, got, t["spread"].T,
+        out_specs=[pl.BlockSpec(memory_space=pltpu.HBM)] * 3,
+        scratch_shapes=[
+            pltpu.VMEM(wide, BF16),
+            pltpu.VMEM((length, width), BF16),
+            pltpu.VMEM((length, width), F32),
+            pltpu.SemaphoreType.DMA((features // CHUNK + 2,)),
+        ],
     )
     return (mixed[None], grad_query[None], grad_value[None], grad_filt)
 

time: 98.3 us -> 96.8 us (0.985)
  waiting for transfers between devices: 4.56 us -> 6.46 us
  Pallas kernels: 10.4 us -> 8.81 us
    pallas_call x8 -> x7, Pallas kernels: 10.4 us -> 8.81 us  [call(): pl.pallas_call(kernel, out_shape=outs, **options, name=kernel.__name__, c...]
    all_to_all x2, waiting for transfers between devices: 0.95 us -> 2.53 us  [exchange(): lax.all_to_all(message, ('dp', 'seq'), split_axis=0, concat_axis=0, tiled...]
  transfers between devices with their start and end apart: 8 -> 8, of which waited for: 3 -> 3; matrix products, arithmetic and copies ran while one was open for 0% -> 0% of each run, Pallas kernels for 7% -> 5%
where the time goes in v4:
time: 96.8 us; the launch traced here: 96.3 us
  starting transfers between devices  46.7 us (48%)
  blocking collectives  31.9 us (33%)
  Pallas kernels  8.81 us (9%)
  waiting for transfers between devices  6.46 us (7%)
  local copies, waits for them, and re-layouts  1.41 us (1%)
  between operations  1.01 us (1%)
    all_to_all x2, starting transfers between devices, exchange(): lax.all_to_all(message, ('dp', 'seq'), split_axis=0, concat_axis=0, tiled...  26.9 us
    all_to_all x1, blocking collectives, exchange(): lax.all_to_all(message, ('dp', 'seq'), split_axis=0, concat_axis=0, tiled...  21.1 us
    ppermute x6, starting transfers between devices, shifted(): lax.ppermute(array, 'tensor', [(i, (i + distance) % count) for i in range...  19.8 us
    all_gather x1, blocking collectives, per_device(): gathered = lax.all_gather(gated, 'tensor', axis=0, tiled=True)  10.8 us
    pallas_call x7, Pallas kernels, call(): pl.pallas_call(kernel, out_shape=outs, **options, name=kernel.__name__, c...  8.81 us
    ppermute x6, waiting for transfers between devices, shifted(): lax.ppermute(array, 'tensor', [(i, (i + distance) % count) for i in range...  3.92 us
    all_to_all x2, waiting for transfers between devices, exchange(): lax.all_to_all(message, ('dp', 'seq'), split_axis=0, concat_axis=0, tiled...  2.53 us
  transfers between devices with their start and end apart: 8, of which 3 were waited for; matrix products, arithmetic and copies ran while one was open for 0% of the time, Pallas kernels for 5%

profile of v4, /device:TPU:1, one launch (start us, length us, event | category | flops | bytes accessed | tf_op | source)
XLA Modules:
  0.0 96.3 jit_solution(12859007275711095496)
XLA Ops:
  0.7 0.0 copy-start.11
  0.7 0.0 copy-start.12
  0.7 0.0 copy-start.13
  0.7 1.3 %constant_dynamic-slice_fusion = (bf16[128,1024]{1,0:T(8,128)(2,1)S(1)}, bf16[128,1024]{1,0:T(8,128)(2,1)S(1)}, bf16[128,1024]{1,0:T(8,128)(2,1)S(1)}, bf16[128,1024]{1,0:T(8,128)(2,1)S(1)}) fusion(bf16[128,4096]{1,0:T(8,128)(2,1)} %param.20, s32[]{:T(128)S(6)} %select_n.38, s32[]{:T(128)S(6)} %select_n.34, s32[]{:T(128)S(6)} %select_n.32, s32[]{:T(128)S(6)} %select_n.36), kind=kLoop, calls=%fused_computation | loop fusion | bytes 2097168 | tf_op jit(solution)/shard_map/dynamic_slice | solution.py:279
  2.0 5.2 %collective-permute-start.2 = (bf16[128,1024]{1,0:T(8,128)(2,1)S(1)}, bf16[128,1024]{1,0:T(8,128)(2,1)S(1)}, u32[]{:S(2)}, u32[]{:S(2)}) collective-permute-start(bf16[128,1024]{1,0:T(8,128)(2,1)S(1)} %get-tuple-element.32), channel_id=1, source_target_pairs={{0,3},{1,0},{2,1},{3,2},{4,7},{5,4},{6,5},{7,6},{8,11},{9,8},{10,9... | collective-permute-start | bytes 786440 | tf_op jit(solution)/shard_map/ppermute | solution.py:264
  7.3 1.9 %collective-permute-start = (bf16[128,1024]{1,0:T(8,128)(2,1)S(1)}, bf16[128,1024]{1,0:T(8,128)(2,1)S(1)}, u32[]{:S(2)}, u32[]{:S(2)}) collective-permute-start(bf16[128,1024]{1,0:T(8,128)(2,1)S(1)} %get-tuple-element.33), channel_id=1, source_target_pairs={{0,1},{1,2},{2,3},{3,0},{4,5},{5,6},{6,7},{7,4},{8,9},{9,10},{10,1... | collective-permute-start | bytes 786440 | tf_op jit(solution)/shard_map/ppermute | solution.py:264
  9.2 3.6 %collective-permute-start.1 = (bf16[128,1024]{1,0:T(8,128)(2,1)S(1)}, bf16[128,1024]{1,0:T(8,128)(2,1)S(1)}, u32[]{:S(2)}, u32[]{:S(2)}) collective-permute-start(bf16[128,1024]{1,0:T(8,128)(2,1)S(1)} %get-tuple-element.35), channel_id=1, source_target_pairs={{0,2},{1,3},{2,0},{3,1},{4,6},{5,7},{6,4},{7,5},{8,10},{9,11},{10,... | collective-permute-start | bytes 786440 | tf_op jit(solution)/shard_map/ppermute | solution.py:264
  12.8 0.0 copy-done.11
  12.8 0.0 copy-done.12
  12.9 0.0 copy-done.13
  12.9 1.1 %pack_inputs.1 = bf16[1024,128]{1,0:T(8,128)(2,1)} custom-call(bf16[512,128]{1,0:T(8,128)(2,1)S(1)} %bitcast.19, f32[512,128]{1,0:T(8,128)S(1)} %copy-done.11, bf16[256,256]{1,0:T(8,128)(2,1)S(1)} %copy-done.13), custom_call_target="tpu_custom_call" | custom-call | flops 40000000000 | bytes 40000000 | tf_op jit(solution)/shard_map/pack_inputs/pallas_call | solution.py:244
  14.0 20.8 %all-to-all-start = ((bf16[128,8,128]{2,1,0:T(8,128)(2,1)}), bf16[128,8,128]{2,1,0:T(8,128)(2,1)S(1)}, u32[]{:S(2)}, u32[]{:S(2)}) async-start(bf16[128,8,128]{2,1,0:T(8,128)(2,1)} %bitcast.2), calls=%async_computation | async-start | bytes 524288 | tf_op jit(solution)/shard_map/all_to_all | solution.py:258
  34.7 0.0 collective-permute-done.2.refs_3_
  34.8 0.0 collective-permute-done.refs_1_
  34.8 0.0 collective-permute-done.1.refs_2_
  34.8 0.0 copy-start.2
  34.8 0.0 copy-start.3
  34.8 0.0 copy-start.4
  34.8 0.0 copy-start.5
  34.8 0.0 copy-start.7
  34.8 0.0 copy-start.8
  34.9 2.1 %partial_grads.1 = (bf16[512,128]{1,0:T(8,128)(2,1)S(1)}, bf16[512,128]{1,0:T(8,128)(2,1)S(1)}, bf16[512,128]{1,0:T(8,128)(2,1)S(1)}, bf16[512,128]{1,0:T(8,128)(2,1)S(1)}) custom-call(bf16[512,1024]{1,0:T(8,128)(2,1)} %bitcast.20, bf16[128,1024]{1,0:T(8,128)(2,1)S(1)} %get-tuple-element.34.refs_0_, bf16[128,1024]{1,0:T(8,128)(2,1)S(1)} %collective-permute-done.refs_1_, ...), custom_call_target="tpu_custom_call" | custom-call | flops 40000000000 | bytes 40000000 | tf_op jit(solution)/shard_map/partial_grads/pallas_call | solution.py:244
  37.0 2.8 %collective-permute-start.3 = (bf16[512,128]{1,0:T(8,128)(2,1)S(1)}, bf16[512,128]{1,0:T(8,128)(2,1)S(1)}, u32[]{:S(2)}, u32[]{:S(2)}) collective-permute-start(bf16[512,128]{1,0:T(8,128)(2,1)S(1)} %get-tuple-element.20), channel_id=1, source_target_pairs={{0,3},{1,0},{2,1},{3,2},{4,7},{5,4},{6,5},{7,6},{8,11},{9,8},{10,9... | collective-permute-start | bytes 393224 | tf_op jit(solution)/shard_map/ppermute | solution.py:264
  39.8 4.4 %collective-permute-start.4 = (bf16[512,128]{1,0:T(8,128)(2,1)S(1)}, bf16[512,128]{1,0:T(8,128)(2,1)S(1)}, u32[]{:S(2)}, u32[]{:S(2)}) collective-permute-start(bf16[512,128]{1,0:T(8,128)(2,1)S(1)} %get-tuple-element.21), channel_id=1, source_target_pairs={{0,2},{1,3},{2,0},{3,1},{4,6},{5,7},{6,4},{7,5},{8,10},{9,11},{10,... | collective-permute-start | bytes 393224 | tf_op jit(solution)/shard_map/ppermute | solution.py:264
  44.1 1.9 %collective-permute-start.5 = (bf16[512,128]{1,0:T(8,128)(2,1)S(1)}, bf16[512,128]{1,0:T(8,128)(2,1)S(1)}, u32[]{:S(2)}, u32[]{:S(2)}) collective-permute-start(bf16[512,128]{1,0:T(8,128)(2,1)S(1)} %get-tuple-element.22), channel_id=1, source_target_pairs={{0,1},{1,2},{2,3},{3,0},{4,5},{5,6},{6,7},{7,4},{8,9},{9,10},{10,1... | collective-permute-start | bytes 393224 | tf_op jit(solution)/shard_map/ppermute | solution.py:264
  46.1 0.0 all-to-all-done
  46.1 0.0 copy-done.2
  46.1 0.0 copy-done.3
  46.1 0.0 copy-done.4
  46.1 0.0 copy-done.5
  46.1 0.0 copy-done.7
  46.1 0.0 copy-done.8
  46.1 0.0 copy-start
  46.1 0.0 copy-start.6
  46.1 1.0 %convolve.1 = (bf16[1024,128]{1,0:T(8,128)(2,1)S(1)}, f32[512,256]{1,0:T(8,128)S(1)}, f32[128,256]{1,0:T(8,128)S(1)}) custom-call(bf16[1024,128]{1,0:T(8,128)(2,1)S(1)} %bitcast.15, bf16[256,256]{1,0:T(8,128)(2,1)S(1)} %copy-done.8, bf16[256,256]{1,0:T(8,128)(2,1)S(1)} %copy-done.7, bf16[256,256]{1,0:T(8,128)(2,1)S(1)} %copy-done.5, ...), custom_call_target="tpu_custom_call" | custom-call | tf_op jit(solution)/shard_map/convolve/pallas_call | solution.py:244
  47.1 0.0 collective-permute-done.3.refs_4_
  47.1 0.4 collective-permute-done.4.refs_5_
  47.5 3.6 %collective-permute-done.5.refs_6_ = bf16[512,128]{1,0:T(8,128)(2,1)S(1)} collective-permute-done((bf16[512,128]{1,0:T(8,128)(2,1)S(1)}, bf16[512,128]{1,0:T(8,128)(2,1)S(1)}, u32[]{:S(2)}, u32[]{:S(2)}) %collective-permute-start.5) | collective-permute-done | bytes 131104 | tf_op jit(solution)/shard_map/ppermute | solution.py:264
  51.0 0.0 copy-done
  51.1 0.0 copy-done.6
  51.1 0.3 pack_grads.1
  51.4 0.0 copy-start.9
  51.4 0.0 copy-start.10
  51.4 21.1 %all_to_all.15 = bf16[128,8,128]{2,1,0:T(8,128)(2,1)S(1)} all-to-all(bf16[128,8,128]{2,1,0:T(8,128)(2,1)S(1)} %bitcast.18), channel_id=1, replica_groups=mesh['dp'=4,'seq'=32,'tensor'=4] {'dp','seq'}, dimensions={0} | all-to-all | bytes 524288 | tf_op jit(solution)/shard_map/all_to_all | solution.py:258
  72.6 0.0 copy-done.9
  72.6 0.0 copy-done.10
  72.6 1.5 %correlate.1 = bf16[1024,128]{1,0:T(8,128)(2,1)} custom-call(bf16[1024,128]{1,0:T(8,128)(2,1)S(1)} %bitcast.12, f32[512,256]{1,0:T(8,128)S(1)} %get-tuple-element.26.vspec_ref, f32[128,256]{1,0:T(8,128)S(1)} %get-tuple-element.27.fspec_ref, bf16[256,256]{1,0:T(8,128)(2,1)S(1)} %copy-done.10, bf16[256,256]{1,0:T(8,128)(2,1)S(1)} %copy-done.5, ...), custom_call_target="tpu_custom_call" | custom-call | tf_op jit(solution)/shard_map/correlate/pallas_call | solution.py:244
  74.1 0.0 copy-start.1
  74.1 6.1 %all-to-all-start.2 = ((bf16[128,8,128]{2,1,0:T(8,128)(2,1)}), bf16[128,8,128]{2,1,0:T(8,128)(2,1)S(1)}, u32[]{:S(2)}, u32[]{:S(2)}) async-start(bf16[128,8,128]{2,1,0:T(8,128)(2,1)} %bitcast.7), calls=%async_computation.2 | async-start | bytes 524288 | tf_op jit(solution)/shard_map/all_to_all | solution.py:258
  80.2 0.0 copy-done.1
  80.2 1.0 %unpack_conv.1 = (bf16[512,128]{1,0:T(8,128)(2,1)S(1)}, bf16[512,128]{1,0:T(8,128)(2,1)}) custom-call(bf16[1024,128]{1,0:T(8,128)(2,1)S(1)} %bitcast.13, bf16[512,128]{1,0:T(8,128)(2,1)S(1)} %bitcast.17, f32[512,128]{1,0:T(8,128)S(1)} %get-tuple-element.24.grad_ref, bf16[256,256]{1,0:T(8,128)(2,1)S(1)} %copy-done.1), custom_call_target="tpu_custom_call" | custom-call | tf_op jit(solution)/shard_map/unpack_conv/pallas_call | solution.py:244
  81.2 10.8 %all_gather.3.gated_ref = bf16[2048,128]{1,0:T(8,128)(2,1)S(1)} all-gather(bf16[512,128]{1,0:T(8,128)(2,1)S(1)} %get-tuple-element.25), channel_id=1, replica_groups=mesh['dp'=4,'seq'=32,'tensor'=4] {'tensor'}, dimensions={0}, use_global_device_ids=true | all-gather | bytes 655360 | tf_op jit(solution)/shard_map/all_gather | solution.py:303
  92.0 2.5 %all-to-all-done.2 = bf16[128,8,128]{2,1,0:T(8,128)(2,1)S(1)} async-done(((bf16[128,8,128]{2,1,0:T(8,128)(2,1)}), bf16[128,8,128]{2,1,0:T(8,128)(2,1)S(1)}, u32[]{:S(2)}, u32[]{:S(2)}) %all-to-all-start.2) | async-done | bytes 262176 | tf_op jit(solution)/shard_map/all_to_all | solution.py:258
  94.5 1.8 %finish.1 = (bf16[512,1024]{1,0:T(8,128)(2,1)}, bf16[512,128]{1,0:T(8,128)(2,1)}, f32[512,128]{1,0:T(8,128)}) custom-call(bf16[2048,128]{1,0:T(8,128)(2,1)S(1)} %all_gather.3.gated_ref, bf16[128,1024]{1,0:T(8,128)(2,1)S(1)} %get-tuple-element.34.refs_0_, bf16[128,1024]{1,0:T(8,128)(2,1)S(1)} %collective-permute-done.refs_1_, ...), custom_call_target="tpu_custom_call" | custom-call | tf_op jit(solution)/shard_map/finish/pallas_call | solution.py:244
Async XLA Ops:
  0.7 12.1 %copy-start.11 = (f32[512,128]{1,0:T(8,128)S(1)}, f32[512,128]{1,0:T(8,128)}, u32[]{:S(2)}) copy-start(f32[512,128]{1,0:T(8,128)} %filt_ref.1) | copy-start | bytes 786436
  0.7 12.1 %copy-start.12 = (bf16[1,512,128]{2,1,0:T(8,128)(2,1)S(1)}, bf16[1,512,128]{2,1,0:T(8,128)(2,1)}, u32[]{:S(2)}) copy-start(bf16[1,512,128]{2,1,0:T(8,128)(2,1)} %param.18) | copy-start | bytes 393220
  0.7 12.1 %copy-start.13 = (bf16[256,256]{1,0:T(8,128)(2,1)S(1)}, bf16[256,256]{1,0:T(8,128)(2,1)}, u32[]{:S(2)}) copy-start(bf16[256,256]{1,0:T(8,128)(2,1)} %constant.61.clone.spread_ref) | copy-start | bytes 393220
  2.0 32.7 %collective-permute-start.2 = (bf16[128,1024]{1,0:T(8,128)(2,1)S(1)}, bf16[128,1024]{1,0:T(8,128)(2,1)S(1)}, u32[]{:S(2)}, u32[]{:S(2)}) collective-permute-start(bf16[128,1024]{1,0:T(8,128)(2,1)S(1)} %get-tuple-element.32), channel_id=1, source_target_pairs={{0,3},{1,0},{2,1},{3,2},{4,7},{5,4},{6,5},{7,6},{8,11},{9,8},{10,9... | collective-permute-start | bytes 786440 | tf_op jit(solution)/shard_map/ppermute | solution.py:264
  7.3 27.5 %collective-permute-start = (bf16[128,1024]{1,0:T(8,128)(2,1)S(1)}, bf16[128,1024]{1,0:T(8,128)(2,1)S(1)}, u32[]{:S(2)}, u32[]{:S(2)}) collective-permute-start(bf16[128,1024]{1,0:T(8,128)(2,1)S(1)} %get-tuple-element.33), channel_id=1, source_target_pairs={{0,1},{1,2},{2,3},{3,0},{4,5},{5,6},{6,7},{7,4},{8,9},{9,10},{10,1... | collective-permute-start | bytes 786440 | tf_op jit(solution)/shard_map/ppermute | solution.py:264
  9.2 25.6 %collective-permute-start.1 = (bf16[128,1024]{1,0:T(8,128)(2,1)S(1)}, bf16[128,1024]{1,0:T(8,128)(2,1)S(1)}, u32[]{:S(2)}, u32[]{:S(2)}) collective-permute-start(bf16[128,1024]{1,0:T(8,128)(2,1)S(1)} %get-tuple-element.35), channel_id=1, source_target_pairs={{0,2},{1,3},{2,0},{3,1},{4,6},{5,7},{6,4},{7,5},{8,10},{9,11},{10,... | collective-permute-start | bytes 786440 | tf_op jit(solution)/shard_map/ppermute | solution.py:264
  14.0 32.1 %all-to-all-start = ((bf16[128,8,128]{2,1,0:T(8,128)(2,1)}), bf16[128,8,128]{2,1,0:T(8,128)(2,1)S(1)}, u32[]{:S(2)}, u32[]{:S(2)}) async-start(bf16[128,8,128]{2,1,0:T(8,128)(2,1)} %bitcast.2), calls=%async_computation | async-start | bytes 524288 | tf_op jit(solution)/shard_map/all_to_all | solution.py:258
  34.8 11.3 %copy-start.2 = (f32[2,128,128]{2,1,0:T(8,128)S(1)}, f32[2,128,128]{2,1,0:T(8,128)}, u32[]{:S(2)}) copy-start(f32[2,128,128]{2,1,0:T(8,128)} %constant.67.clone.twist_ref) | copy-start | bytes 393220
  34.8 11.3 %copy-start.3 = (bf16[256,256]{1,0:T(8,128)(2,1)S(1)}, bf16[256,256]{1,0:T(8,128)(2,1)}, u32[]{:S(2)}) copy-start(bf16[256,256]{1,0:T(8,128)(2,1)} %constant.66.clone.inner_t_ref) | copy-start | bytes 393220
  34.8 11.3 %copy-start.4 = (bf16[256,256]{1,0:T(8,128)(2,1)S(1)}, bf16[256,256]{1,0:T(8,128)(2,1)}, u32[]{:S(2)}) copy-start(bf16[256,256]{1,0:T(8,128)(2,1)} %constant.65.clone.inner_ref) | copy-start | bytes 393220
  34.8 11.3 %copy-start.5 = (bf16[256,256]{1,0:T(8,128)(2,1)S(1)}, bf16[256,256]{1,0:T(8,128)(2,1)}, u32[]{:S(2)}) copy-start(bf16[256,256]{1,0:T(8,128)(2,1)} %constant.64.clone.inv_ref.inv_first_ref) | copy-start | bytes 393220
  34.8 11.3 %copy-start.7 = (bf16[256,256]{1,0:T(8,128)(2,1)S(1)}, bf16[256,256]{1,0:T(8,128)(2,1)}, u32[]{:S(2)}) copy-start(bf16[256,256]{1,0:T(8,128)(2,1)} %constant.63.clone.second_ref) | copy-start | bytes 393220
  34.8 11.3 %copy-start.8 = (bf16[256,256]{1,0:T(8,128)(2,1)S(1)}, bf16[256,256]{1,0:T(8,128)(2,1)}, u32[]{:S(2)}) copy-start(bf16[256,256]{1,0:T(8,128)(2,1)} %constant.62.clone.first_ref) | copy-start | bytes 393220
  37.0 10.1 %collective-permute-start.3 = (bf16[512,128]{1,0:T(8,128)(2,1)S(1)}, bf16[512,128]{1,0:T(8,128)(2,1)S(1)}, u32[]{:S(2)}, u32[]{:S(2)}) collective-permute-start(bf16[512,128]{1,0:T(8,128)(2,1)S(1)} %get-tuple-element.20), channel_id=1, source_target_pairs={{0,3},{1,0},{2,1},{3,2},{4,7},{5,4},{6,5},{7,6},{8,11},{9,8},{10,9... | collective-permute-start | bytes 393224 | tf_op jit(solution)/shard_map/ppermute | solution.py:264
  39.8 7.7 %collective-permute-start.4 = (bf16[512,128]{1,0:T(8,128)(2,1)S(1)}, bf16[512,128]{1,0:T(8,128)(2,1)S(1)}, u32[]{:S(2)}, u32[]{:S(2)}) collective-permute-start(bf16[512,128]{1,0:T(8,128)(2,1)S(1)} %get-tuple-element.21), channel_id=1, source_target_pairs={{0,2},{1,3},{2,0},{3,1},{4,6},{5,7},{6,4},{7,5},{8,10},{9,11},{10,... | collective-permute-start | bytes 393224 | tf_op jit(solution)/shard_map/ppermute | solution.py:264
  44.1 6.9 %collective-permute-start.5 = (bf16[512,128]{1,0:T(8,128)(2,1)S(1)}, bf16[512,128]{1,0:T(8,128)(2,1)S(1)}, u32[]{:S(2)}, u32[]{:S(2)}) collective-permute-start(bf16[512,128]{1,0:T(8,128)(2,1)S(1)} %get-tuple-element.22), channel_id=1, source_target_pairs={{0,1},{1,2},{2,3},{3,0},{4,5},{5,6},{6,7},{7,4},{8,9},{9,10},{10,1... | collective-permute-start | bytes 393224 | tf_op jit(solution)/shard_map/ppermute | solution.py:264
  46.1 4.9 %copy-start = (bf16[1,512,128]{2,1,0:T(8,128)(2,1)S(1)}, bf16[1,512,128]{2,1,0:T(8,128)(2,1)}, u32[]{:S(2)}) copy-start(bf16[1,512,128]{2,1,0:T(8,128)(2,1)} %param.17) | copy-start | bytes 393220
  46.1 4.9 %copy-start.6 = (bf16[256,256]{1,0:T(8,128)(2,1)S(1)}, bf16[256,256]{1,0:T(8,128)(2,1)}, u32[]{:S(2)}) copy-start(bf16[256,256]{1,0:T(8,128)(2,1)} %constant.68.clone.refs_2_) | copy-start | bytes 393220
  51.4 21.2 %copy-start.9 = (bf16[256,256]{1,0:T(8,128)(2,1)S(1)}, bf16[256,256]{1,0:T(8,128)(2,1)}, u32[]{:S(2)}) copy-start(bf16[256,256]{1,0:T(8,128)(2,1)} %constant.71.clone.inv_second_ref) | copy-start | bytes 393220
  51.4 21.1 %copy-start.10 = (bf16[256,256]{1,0:T(8,128)(2,1)S(1)}, bf16[256,256]{1,0:T(8,128)(2,1)}, u32[]{:S(2)}) copy-start(bf16[256,256]{1,0:T(8,128)(2,1)} %constant.70.clone.second_ref) | copy-start | bytes 393220
  74.1 6.2 %copy-start.1 = (bf16[256,256]{1,0:T(8,128)(2,1)S(1)}, bf16[256,256]{1,0:T(8,128)(2,1)}, u32[]{:S(2)}) copy-start(bf16[256,256]{1,0:T(8,128)(2,1)} %constant.69.clone.gather_ref.refs_5_) | copy-start | bytes 393220
  74.1 20.4 %all-to-all-start.2 = ((bf16[128,8,128]{2,1,0:T(8,128)(2,1)}), bf16[128,8,128]{2,1,0:T(8,128)(2,1)S(1)}, u32[]{:S(2)}, u32[]{:S(2)}) async-start(bf16[128,8,128]{2,1,0:T(8,128)(2,1)} %bitcast.7), calls=%async_computation.2 | async-start | bytes 524288 | tf_op jit(solution)/shard_map/all_to_all | solution.py:258

commit v5 on v3

--- a/solution.py
+++ b/solution.py
@@ -19,7 +19,8 @@
 CHUNK = 256
 HALVES = 256
 SLOTS = 8
-TURN = 18
+TURN = 22
+LATER = 0
 HALF = 128
 
 
@@ -39,7 +40,7 @@
         first = np.where(row[None, :] % SLOTS < ROWS, full, 0.0)
         return first, full - first
 
-    first, second = outer(0)
+    first, second = outer(LATER)
     turned_first, turned_second = outer(TURN)
     fine = np.arange(LANES)
     angle = 2 * math.pi / LANES * np.outer(fine, fine)
@@ -51,7 +52,7 @@
     for channel in range(32):
         for slot in range(SLOTS):
             spread[channel * SLOTS + slot, slot * 32 + channel] = 1.0
-            turned_spread[channel * SLOTS + slot, slot * 32 + (channel + TURN) % 32] = 1.0
+            turned_spread[channel * SLOTS + slot, slot * 32 + (channel + TURN - LATER) % 32] = 1.0
     return {
         "turned_first": narrow(turned_first),
         "turned_second": narrow(turned_second),
@@ -70,23 +71,6 @@
     return jnp.dot(left, right, preferred_element_type=F32)
 
 
-def split(x):
-    high = x.astype(BF16)
-    return high, (x - high.astype(F32)).astype(BF16)
-
-
-def table_dot(table_ref, high, low=None):
-    out = dot(table_ref[...], high)
-    if low is not None:
-        out = out + dot(table_ref[...], low)
-    return out
-
-
-def dot_table(x, table_ref):
-    high, low = split(x)
-    return dot(high, table_ref[...]) + dot(low, table_ref[...])
-
-
 def lanes(tiles):
     return jnp.concatenate(tiles, axis=1)
 
@@ -97,30 +81,30 @@
 
 def forward(signals, outer_ref, inner_ref, twist_ref):
     count = signals.shape[1] // LANES
-    coarse = table_dot(outer_ref, signals)
+    coarse = dot(outer_ref[...], signals)
     cos, sin = lanes([twist_ref[0]] * count), lanes([twist_ref[1]] * count)
     real, imag = coarse[:HALF], coarse[HALF:]
     real, imag = real * cos + imag * sin, imag * cos - real * sin
     cuts = [slice(k * LANES, (k + 1) * LANES) for k in range(count)]
-    return dot_table(rows([lanes([real[:, cut], imag[:, cut]]) for cut in cuts]), inner_ref)
+    return dot(rows([lanes([real[:, cut], imag[:, cut]]) for cut in cuts]).astype(BF16), inner_ref[...])
 
 
 def inverse_inner(spectra, inner_t_ref, twist_ref):
     count = spectra.shape[0] // HALF
-    coarse = dot_table(spectra, inner_t_ref)
+    coarse = dot(spectra.astype(BF16), inner_t_ref[...])
     cos, sin = twist_ref[0], twist_ref[1]
     out = []
     for k in range(count):
         real, imag = coarse[k * HALF:(k + 1) * HALF, :LANES], coarse[k * HALF:(k + 1) * HALF, LANES:]
         out.append(rows([real * cos - imag * sin, imag * cos + real * sin]))
-    return split(lanes(out))
+    return lanes(out).astype(BF16)
 
 
 def pack_inputs(values_ref, filt_ref, spread_ref, out_ref):
     dp = lax.axis_index("dp")
     start = pl.multiple_of(dp * LANES, LANES)
     quarter = filt_ref[pl.ds(start, LANES), :].T
-    tiles = [values_ref[q * LANES:(q + 1) * LANES, :].astype(F32).T.astype(BF16) for q in range(ROWS)]
+    tiles = [values_ref[q * LANES:(q + 1) * LANES, :].T for q in range(ROWS)]
     tiles += [jnp.where(dp == q, quarter, 0.0).astype(BF16) for q in range(DP)]
     for part in range(4):
         block = jnp.concatenate([tile[part * 32:(part + 1) * 32] for tile in tiles], axis=0)
@@ -140,7 +124,7 @@
     for b in range(DP):
         v_real, v_imag = vspec[b * HALF:(b + 1) * HALF, :LANES], vspec[b * HALF:(b + 1) * HALF, LANES:]
         spectra.append(lanes([v_real * f_real - v_imag * f_imag, v_real * f_imag + v_imag * f_real]))
-    conv = table_dot(inv_ref, *inverse_inner(rows(spectra), inner_t_ref, twist_ref))
+    conv = dot(inv_ref[...], inverse_inner(rows(spectra), inner_t_ref, twist_ref))
     for b in range(DP):
         conv_ref[b * size:(b + 1) * size, :] = conv[:, b * LANES:(b + 1) * LANES].astype(BF16)
 
@@ -216,19 +200,12 @@
         sum_imag = part_imag if b == 0 else sum_imag + part_imag
         spectra.append(lanes([real * f_real + imag * f_imag, imag * f_real - real * f_imag]))
     spectra.append(lanes([sum_real, sum_imag]))
-    high, low = inverse_inner(rows(spectra), inner_t_ref, twist_ref)
+    coarse = inverse_inner(rows(spectra), inner_t_ref, twist_ref)
     cut = DP * LANES
-    value = table_dot(inv_first_ref, high[:, :cut], low[:, :cut])
-    filt = table_dot(inv_second_ref, high[:, cut:], low[:, cut:])
+    value = dot(inv_first_ref[...], coarse[:, :cut])
+    filt = dot(inv_second_ref[...], coarse[:, cut:])
     for b in range(DP):
         out_ref[b * size:(b + 1) * size, :] = (value[:, b * LANES:(b + 1) * LANES] + filt).astype(BF16)
-
-
-def unpack_grads(got_ref, gather_ref, value_ref, filt_ref):
-    tiles = gather_half(got_ref, gather_ref[...])
-    for q in range(ROWS):
-        value_ref[q * LANES:(q + 1) * LANES, :] = tiles[q].astype(BF16)
-        filt_ref[q * LANES:(q + 1) * LANES, :] = tiles[ROWS + q]
 
 
 def project(gated_ref, *refs):
@@ -249,6 +226,13 @@
         copy.wait()
 
 
+def unpack_grads(got_ref, gather_ref, value_ref, filt_ref):
+    tiles = gather_half(got_ref, gather_ref[...])
+    for q in range(ROWS):
+        value_ref[q * LANES:(q + 1) * LANES, :] = tiles[q].astype(BF16)
+        filt_ref[q * LANES:(q + 1) * LANES, :] = tiles[ROWS + q]
+
+
 COVER = pl.CostEstimate(flops=40_000_000_000, transcendentals=0, bytes_accessed=40_000_000)
 COVERS = {"pack_inputs": COVER, "partial_grads": COVER}
 
@@ -264,7 +248,7 @@
     )(*operands)
 
 
-def exchange(message, turn=0):
+def exchange(message, turn=LATER):
     shape = message.shape
     message = message.reshape(DP * SEQ, SLOTS, LANES)
     group = [b * SEQ + (s + turn) % SEQ for b in range(DP) for s in range(SEQ)]

time: 98.3 us -> 96.4 us (0.981)
  no operation moved by 1% of the time
where the time goes in v5:
time: 96.4 us; the launch traced here: 95.6 us
  starting transfers between devices  46.7 us (48%)
  blocking collectives  31.9 us (33%)
  Pallas kernels  9.69 us (10%)
  waiting for transfers between devices  4.86 us (5%)
  local copies, waits for them, and re-layouts  1.41 us (1%)
  between operations  1.01 us (1%)
    all_to_all x2, starting transfers between devices, exchange(): lax.all_to_all(message, ('dp', 'seq'), split_axis=0, concat_axis=0, tiled...  26.9 us
    all_to_all x1, blocking collectives, exchange(): lax.all_to_all(message, ('dp', 'seq'), split_axis=0, concat_axis=0, tiled...  21.1 us
    ppermute x6, starting transfers between devices, shifted(): lax.ppermute(array, 'tensor', [(i, (i + distance) % count) for i in range...  19.8 us
    all_gather x1, blocking collectives, per_device(): gathered = lax.all_gather(gated, 'tensor', axis=0, tiled=True)  10.8 us
    pallas_call x8, Pallas kernels, call(): pl.pallas_call(kernel, out_shape=outs, **options, name=kernel.__name__, c...  9.69 us
    ppermute x6, waiting for transfers between devices, shifted(): lax.ppermute(array, 'tensor', [(i, (i + distance) % count) for i in range...  3.92 us
  transfers between devices with their start and end apart: 8, of which 3 were waited for; matrix products, arithmetic and copies ran while one was open for 0% of the time, Pallas kernels for 7%

profile of v5, /device:TPU:1, one launch (start us, length us, event | category | flops | bytes accessed | tf_op | source)
XLA Modules:
  0.0 95.6 jit_solution(7889749207865752321)
XLA Ops:
  0.7 0.0 copy-start.11
  0.7 0.0 copy-start.12
  0.7 0.0 copy-start.13
  0.7 1.3 %constant_dynamic-slice_fusion = (bf16[128,1024]{1,0:T(8,128)(2,1)S(1)}, bf16[128,1024]{1,0:T(8,128)(2,1)S(1)}, bf16[128,1024]{1,0:T(8,128)(2,1)S(1)}, bf16[128,1024]{1,0:T(8,128)(2,1)S(1)}) fusion(bf16[128,4096]{1,0:T(8,128)(2,1)} %param.20, s32[]{:T(128)S(6)} %select_n.38, s32[]{:T(128)S(6)} %select_n.34, s32[]{:T(128)S(6)} %select_n.32, s32[]{:T(128)S(6)} %select_n.36), kind=kLoop, calls=%fused_computation | loop fusion | bytes 2097168 | tf_op jit(solution)/shard_map/dynamic_slice | solution.py:276
  2.0 5.2 %collective-permute-start.2 = (bf16[128,1024]{1,0:T(8,128)(2,1)S(1)}, bf16[128,1024]{1,0:T(8,128)(2,1)S(1)}, u32[]{:S(2)}, u32[]{:S(2)}) collective-permute-start(bf16[128,1024]{1,0:T(8,128)(2,1)S(1)} %get-tuple-element.30), channel_id=1, source_target_pairs={{0,3},{1,0},{2,1},{3,2},{4,7},{5,4},{6,5},{7,6},{8,11},{9,8},{10,9... | collective-permute-start | bytes 786440 | tf_op jit(solution)/shard_map/ppermute | solution.py:261
  7.3 1.9 %collective-permute-start = (bf16[128,1024]{1,0:T(8,128)(2,1)S(1)}, bf16[128,1024]{1,0:T(8,128)(2,1)S(1)}, u32[]{:S(2)}, u32[]{:S(2)}) collective-permute-start(bf16[128,1024]{1,0:T(8,128)(2,1)S(1)} %get-tuple-element.31), channel_id=1, source_target_pairs={{0,1},{1,2},{2,3},{3,0},{4,5},{5,6},{6,7},{7,4},{8,9},{9,10},{10,1... | collective-permute-start | bytes 786440 | tf_op jit(solution)/shard_map/ppermute | solution.py:261
  9.2 3.6 %collective-permute-start.1 = (bf16[128,1024]{1,0:T(8,128)(2,1)S(1)}, bf16[128,1024]{1,0:T(8,128)(2,1)S(1)}, u32[]{:S(2)}, u32[]{:S(2)}) collective-permute-start(bf16[128,1024]{1,0:T(8,128)(2,1)S(1)} %get-tuple-element.33), channel_id=1, source_target_pairs={{0,2},{1,3},{2,0},{3,1},{4,6},{5,7},{6,4},{7,5},{8,10},{9,11},{10,... | collective-permute-start | bytes 786440 | tf_op jit(solution)/shard_map/ppermute | solution.py:261
  12.8 0.0 copy-done.11
  12.8 0.0 copy-done.12
  12.9 0.0 copy-done.13
  12.9 1.1 %pack_inputs.1 = bf16[1024,128]{1,0:T(8,128)(2,1)} custom-call(bf16[512,128]{1,0:T(8,128)(2,1)S(1)} %bitcast.19, f32[512,128]{1,0:T(8,128)S(1)} %copy-done.11, bf16[256,256]{1,0:T(8,128)(2,1)S(1)} %copy-done.13), custom_call_target="tpu_custom_call" | custom-call | flops 40000000000 | bytes 40000000 | tf_op jit(solution)/shard_map/pack_inputs/pallas_call | solution.py:241
  14.0 20.8 %all-to-all-start = ((bf16[128,8,128]{2,1,0:T(8,128)(2,1)}), bf16[128,8,128]{2,1,0:T(8,128)(2,1)S(1)}, u32[]{:S(2)}, u32[]{:S(2)}) async-start(bf16[128,8,128]{2,1,0:T(8,128)(2,1)} %bitcast.2), calls=%async_computation | async-start | bytes 524288 | tf_op jit(solution)/shard_map/all_to_all | solution.py:255
  34.7 0.0 collective-permute-done.2.refs_3_
  34.8 0.0 collective-permute-done.refs_1_
  34.8 0.0 collective-permute-done.1.refs_2_
  34.8 0.0 copy-start.2
  34.8 0.0 copy-start.3
  34.8 0.0 copy-start.4
  34.8 0.0 copy-start.5
  34.8 0.0 copy-start.7
  34.8 0.0 copy-start.8
  34.9 2.1 %partial_grads.1 = (bf16[512,128]{1,0:T(8,128)(2,1)S(1)}, bf16[512,128]{1,0:T(8,128)(2,1)S(1)}, bf16[512,128]{1,0:T(8,128)(2,1)S(1)}, bf16[512,128]{1,0:T(8,128)(2,1)S(1)}) custom-call(bf16[512,1024]{1,0:T(8,128)(2,1)} %bitcast.21, bf16[128,1024]{1,0:T(8,128)(2,1)S(1)} %get-tuple-element.32.refs_0_, bf16[128,1024]{1,0:T(8,128)(2,1)S(1)} %collective-permute-done.refs_1_, ...), custom_call_target="tpu_custom_call" | custom-call | flops 40000000000 | bytes 40000000 | tf_op jit(solution)/shard_map/partial_grads/pallas_call | solution.py:241
  37.0 2.8 %collective-permute-start.3 = (bf16[512,128]{1,0:T(8,128)(2,1)S(1)}, bf16[512,128]{1,0:T(8,128)(2,1)S(1)}, u32[]{:S(2)}, u32[]{:S(2)}) collective-permute-start(bf16[512,128]{1,0:T(8,128)(2,1)S(1)} %get-tuple-element.19), channel_id=1, source_target_pairs={{0,3},{1,0},{2,1},{3,2},{4,7},{5,4},{6,5},{7,6},{8,11},{9,8},{10,9... | collective-permute-start | bytes 393224 | tf_op jit(solution)/shard_map/ppermute | solution.py:261
  39.7 4.4 %collective-permute-start.4 = (bf16[512,128]{1,0:T(8,128)(2,1)S(1)}, bf16[512,128]{1,0:T(8,128)(2,1)S(1)}, u32[]{:S(2)}, u32[]{:S(2)}) collective-permute-start(bf16[512,128]{1,0:T(8,128)(2,1)S(1)} %get-tuple-element.20), channel_id=1, source_target_pairs={{0,2},{1,3},{2,0},{3,1},{4,6},{5,7},{6,4},{7,5},{8,10},{9,11},{10,... | collective-permute-start | bytes 393224 | tf_op jit(solution)/shard_map/ppermute | solution.py:261
  44.1 1.9 %collective-permute-start.5 = (bf16[512,128]{1,0:T(8,128)(2,1)S(1)}, bf16[512,128]{1,0:T(8,128)(2,1)S(1)}, u32[]{:S(2)}, u32[]{:S(2)}) collective-permute-start(bf16[512,128]{1,0:T(8,128)(2,1)S(1)} %get-tuple-element.21), channel_id=1, source_target_pairs={{0,1},{1,2},{2,3},{3,0},{4,5},{5,6},{6,7},{7,4},{8,9},{9,10},{10,1... | collective-permute-start | bytes 393224 | tf_op jit(solution)/shard_map/ppermute | solution.py:261
  46.0 0.0 all-to-all-done
  46.0 0.0 copy-done.2
  46.1 0.0 copy-done.3
  46.1 0.0 copy-done.4
  46.1 0.0 copy-done.5
  46.1 0.0 copy-done.7
  46.1 0.0 copy-done.8
  46.1 0.0 copy-start.1
  46.1 0.0 copy-start.6
  46.1 1.0 %convolve.1 = (bf16[1024,128]{1,0:T(8,128)(2,1)S(1)}, f32[512,256]{1,0:T(8,128)S(1)}, f32[128,256]{1,0:T(8,128)S(1)}) custom-call(bf16[1024,128]{1,0:T(8,128)(2,1)S(1)} %bitcast.15, bf16[256,256]{1,0:T(8,128)(2,1)S(1)} %copy-done.8, bf16[256,256]{1,0:T(8,128)(2,1)S(1)} %copy-done.7, bf16[256,256]{1,0:T(8,128)(2,1)S(1)} %copy-done.5, ...), custom_call_target="tpu_custom_call" | custom-call | tf_op jit(solution)/shard_map/convolve/pallas_call | solution.py:241
  47.1 0.0 collective-permute-done.3.refs_4_
  47.1 0.4 collective-permute-done.4.refs_5_
  47.6 3.5 %collective-permute-done.5.refs_6_ = bf16[512,128]{1,0:T(8,128)(2,1)S(1)} collective-permute-done((bf16[512,128]{1,0:T(8,128)(2,1)S(1)}, bf16[512,128]{1,0:T(8,128)(2,1)S(1)}, u32[]{:S(2)}, u32[]{:S(2)}) %collective-permute-start.5) | collective-permute-done | bytes 131104 | tf_op jit(solution)/shard_map/ppermute | solution.py:261
  51.0 0.0 copy-done.1
  51.0 0.0 copy-done.6
  51.0 0.3 pack_grads.1
  51.4 0.0 copy-start.9
  51.4 0.0 copy-start.10
  51.4 21.1 %all_to_all.15 = bf16[128,8,128]{2,1,0:T(8,128)(2,1)S(1)} all-to-all(bf16[128,8,128]{2,1,0:T(8,128)(2,1)S(1)} %bitcast.18), channel_id=1, replica_groups=mesh['dp'=4,'seq'=32,'tensor'=4] {'dp','seq'}, dimensions={0} | all-to-all | bytes 524288 | tf_op jit(solution)/shard_map/all_to_all | solution.py:255
  72.6 0.0 copy-done.9
  72.6 0.0 copy-done.10
  72.6 1.5 %correlate.1 = bf16[1024,128]{1,0:T(8,128)(2,1)} custom-call(bf16[1024,128]{1,0:T(8,128)(2,1)S(1)} %bitcast.12, f32[512,256]{1,0:T(8,128)S(1)} %get-tuple-element.26.vspec_ref, f32[128,256]{1,0:T(8,128)S(1)} %get-tuple-element.27.fspec_ref, bf16[256,256]{1,0:T(8,128)(2,1)S(1)} %copy-done.10, bf16[256,256]{1,0:T(8,128)(2,1)S(1)} %copy-done.5, ...), custom_call_target="tpu_custom_call" | custom-call | tf_op jit(solution)/shard_map/correlate/pallas_call | solution.py:241
  74.1 0.0 copy-start
  74.1 6.1 %all-to-all-start.2 = ((bf16[128,8,128]{2,1,0:T(8,128)(2,1)}), bf16[128,8,128]{2,1,0:T(8,128)(2,1)S(1)}, u32[]{:S(2)}, u32[]{:S(2)}) async-start(bf16[128,8,128]{2,1,0:T(8,128)(2,1)} %bitcast.9), calls=%async_computation.2 | async-start | bytes 524288 | tf_op jit(solution)/shard_map/all_to_all | solution.py:255
  80.2 0.0 copy-done
  80.2 1.0 %unpack_conv.1 = (bf16[512,128]{1,0:T(8,128)(2,1)S(1)}, bf16[512,128]{1,0:T(8,128)(2,1)}) custom-call(bf16[1024,128]{1,0:T(8,128)(2,1)S(1)} %bitcast.13, bf16[512,128]{1,0:T(8,128)(2,1)S(1)} %bitcast.17, f32[512,128]{1,0:T(8,128)S(1)} %get-tuple-element.23.grad_ref, bf16[256,256]{1,0:T(8,128)(2,1)S(1)} %copy-done), custom_call_target="tpu_custom_call" | custom-call | tf_op jit(solution)/shard_map/unpack_conv/pallas_call | solution.py:241
  81.2 10.8 %all_gather.3.gated_ref = bf16[2048,128]{1,0:T(8,128)(2,1)S(1)} all-gather(bf16[512,128]{1,0:T(8,128)(2,1)S(1)} %get-tuple-element.24), channel_id=1, replica_groups=mesh['dp'=4,'seq'=32,'tensor'=4] {'tensor'}, dimensions={0}, use_global_device_ids=true | all-gather | bytes 655360 | tf_op jit(solution)/shard_map/all_gather | solution.py:300
  92.0 1.6 %project.1 = bf16[512,1024]{1,0:T(8,128)(2,1)} custom-call(bf16[2048,128]{1,0:T(8,128)(2,1)S(1)} %all_gather.3.gated_ref, bf16[128,1024]{1,0:T(8,128)(2,1)S(1)} %get-tuple-element.32.refs_0_, bf16[128,1024]{1,0:T(8,128)(2,1)S(1)} %collective-permute-done.refs_1_, bf16[128,1024]{1,0:T(8,128)(2,1)S(1)} %collective-permute-done.1.refs_2_, ...), custom_call_target="tpu_custom_call" | custom-call | tf_op jit(solution)/shard_map/project/pallas_call | solution.py:241
  93.6 0.9 all-to-all-done.2
  94.5 1.1 %unpack_grads.1 = (bf16[512,128]{1,0:T(8,128)(2,1)}, f32[512,128]{1,0:T(8,128)}) custom-call(bf16[1024,128]{1,0:T(8,128)(2,1)S(1)} %bitcast.14, bf16[256,256]{1,0:T(8,128)(2,1)S(1)} %copy-done), custom_call_target="tpu_custom_call" | custom-call | tf_op jit(solution)/shard_map/unpack_grads/pallas_call | solution.py:241
Async XLA Ops:
  0.7 12.1 %copy-start.11 = (f32[512,128]{1,0:T(8,128)S(1)}, f32[512,128]{1,0:T(8,128)}, u32[]{:S(2)}) copy-start(f32[512,128]{1,0:T(8,128)} %filt_ref.1) | copy-start | bytes 786436
  0.7 12.1 %copy-start.12 = (bf16[1,512,128]{2,1,0:T(8,128)(2,1)S(1)}, bf16[1,512,128]{2,1,0:T(8,128)(2,1)}, u32[]{:S(2)}) copy-start(bf16[1,512,128]{2,1,0:T(8,128)(2,1)} %param.18) | copy-start | bytes 393220
  0.7 12.1 %copy-start.13 = (bf16[256,256]{1,0:T(8,128)(2,1)S(1)}, bf16[256,256]{1,0:T(8,128)(2,1)}, u32[]{:S(2)}) copy-start(bf16[256,256]{1,0:T(8,128)(2,1)} %constant.61.clone.spread_ref) | copy-start | bytes 393220
  2.0 32.7 %collective-permute-start.2 = (bf16[128,1024]{1,0:T(8,128)(2,1)S(1)}, bf16[128,1024]{1,0:T(8,128)(2,1)S(1)}, u32[]{:S(2)}, u32[]{:S(2)}) collective-permute-start(bf16[128,1024]{1,0:T(8,128)(2,1)S(1)} %get-tuple-element.30), channel_id=1, source_target_pairs={{0,3},{1,0},{2,1},{3,2},{4,7},{5,4},{6,5},{7,6},{8,11},{9,8},{10,9... | collective-permute-start | bytes 786440 | tf_op jit(solution)/shard_map/ppermute | solution.py:261
  7.3 27.5 %collective-permute-start = (bf16[128,1024]{1,0:T(8,128)(2,1)S(1)}, bf16[128,1024]{1,0:T(8,128)(2,1)S(1)}, u32[]{:S(2)}, u32[]{:S(2)}) collective-permute-start(bf16[128,1024]{1,0:T(8,128)(2,1)S(1)} %get-tuple-element.31), channel_id=1, source_target_pairs={{0,1},{1,2},{2,3},{3,0},{4,5},{5,6},{6,7},{7,4},{8,9},{9,10},{10,1... | collective-permute-start | bytes 786440 | tf_op jit(solution)/shard_map/ppermute | solution.py:261
  9.2 25.6 %collective-permute-start.1 = (bf16[128,1024]{1,0:T(8,128)(2,1)S(1)}, bf16[128,1024]{1,0:T(8,128)(2,1)S(1)}, u32[]{:S(2)}, u32[]{:S(2)}) collective-permute-start(bf16[128,1024]{1,0:T(8,128)(2,1)S(1)} %get-tuple-element.33), channel_id=1, source_target_pairs={{0,2},{1,3},{2,0},{3,1},{4,6},{5,7},{6,4},{7,5},{8,10},{9,11},{10,... | collective-permute-start | bytes 786440 | tf_op jit(solution)/shard_map/ppermute | solution.py:261
  14.0 32.1 %all-to-all-start = ((bf16[128,8,128]{2,1,0:T(8,128)(2,1)}), bf16[128,8,128]{2,1,0:T(8,128)(2,1)S(1)}, u32[]{:S(2)}, u32[]{:S(2)}) async-start(bf16[128,8,128]{2,1,0:T(8,128)(2,1)} %bitcast.2), calls=%async_computation | async-start | bytes 524288 | tf_op jit(solution)/shard_map/all_to_all | solution.py:255
  34.8 11.3 %copy-start.2 = (f32[2,128,128]{2,1,0:T(8,128)S(1)}, f32[2,128,128]{2,1,0:T(8,128)}, u32[]{:S(2)}) copy-start(f32[2,128,128]{2,1,0:T(8,128)} %constant.67.clone.twist_ref) | copy-start | bytes 393220
  34.8 11.3 %copy-start.3 = (bf16[256,256]{1,0:T(8,128)(2,1)S(1)}, bf16[256,256]{1,0:T(8,128)(2,1)}, u32[]{:S(2)}) copy-start(bf16[256,256]{1,0:T(8,128)(2,1)} %constant.66.clone.inner_t_ref) | copy-start | bytes 393220
  34.8 11.3 %copy-start.4 = (bf16[256,256]{1,0:T(8,128)(2,1)S(1)}, bf16[256,256]{1,0:T(8,128)(2,1)}, u32[]{:S(2)}) copy-start(bf16[256,256]{1,0:T(8,128)(2,1)} %constant.65.clone.inner_ref) | copy-start | bytes 393220
  34.8 11.3 %copy-start.5 = (bf16[256,256]{1,0:T(8,128)(2,1)S(1)}, bf16[256,256]{1,0:T(8,128)(2,1)}, u32[]{:S(2)}) copy-start(bf16[256,256]{1,0:T(8,128)(2,1)} %constant.64.clone.inv_ref.inv_first_ref) | copy-start | bytes 393220
  34.8 11.3 %copy-start.7 = (bf16[256,256]{1,0:T(8,128)(2,1)S(1)}, bf16[256,256]{1,0:T(8,128)(2,1)}, u32[]{:S(2)}) copy-start(bf16[256,256]{1,0:T(8,128)(2,1)} %constant.63.clone.second_ref) | copy-start | bytes 393220
  34.8 11.3 %copy-start.8 = (bf16[256,256]{1,0:T(8,128)(2,1)S(1)}, bf16[256,256]{1,0:T(8,128)(2,1)}, u32[]{:S(2)}) copy-start(bf16[256,256]{1,0:T(8,128)(2,1)} %constant.62.clone.first_ref) | copy-start | bytes 393220
  37.0 10.1 %collective-permute-start.3 = (bf16[512,128]{1,0:T(8,128)(2,1)S(1)}, bf16[512,128]{1,0:T(8,128)(2,1)S(1)}, u32[]{:S(2)}, u32[]{:S(2)}) collective-permute-start(bf16[512,128]{1,0:T(8,128)(2,1)S(1)} %get-tuple-element.19), channel_id=1, source_target_pairs={{0,3},{1,0},{2,1},{3,2},{4,7},{5,4},{6,5},{7,6},{8,11},{9,8},{10,9... | collective-permute-start | bytes 393224 | tf_op jit(solution)/shard_map/ppermute | solution.py:261
  39.7 7.8 %collective-permute-start.4 = (bf16[512,128]{1,0:T(8,128)(2,1)S(1)}, bf16[512,128]{1,0:T(8,128)(2,1)S(1)}, u32[]{:S(2)}, u32[]{:S(2)}) collective-permute-start(bf16[512,128]{1,0:T(8,128)(2,1)S(1)} %get-tuple-element.20), channel_id=1, source_target_pairs={{0,2},{1,3},{2,0},{3,1},{4,6},{5,7},{6,4},{7,5},{8,10},{9,11},{10,... | collective-permute-start | bytes 393224 | tf_op jit(solution)/shard_map/ppermute | solution.py:261
  44.1 6.9 %collective-permute-start.5 = (bf16[512,128]{1,0:T(8,128)(2,1)S(1)}, bf16[512,128]{1,0:T(8,128)(2,1)S(1)}, u32[]{:S(2)}, u32[]{:S(2)}) collective-permute-start(bf16[512,128]{1,0:T(8,128)(2,1)S(1)} %get-tuple-element.21), channel_id=1, source_target_pairs={{0,1},{1,2},{2,3},{3,0},{4,5},{5,6},{6,7},{7,4},{8,9},{9,10},{10,1... | collective-permute-start | bytes 393224 | tf_op jit(solution)/shard_map/ppermute | solution.py:261
  46.1 4.9 %copy-start.1 = (bf16[1,512,128]{2,1,0:T(8,128)(2,1)S(1)}, bf16[1,512,128]{2,1,0:T(8,128)(2,1)}, u32[]{:S(2)}) copy-start(bf16[1,512,128]{2,1,0:T(8,128)(2,1)} %param.17) | copy-start | bytes 393220
  46.1 4.9 %copy-start.6 = (bf16[256,256]{1,0:T(8,128)(2,1)S(1)}, bf16[256,256]{1,0:T(8,128)(2,1)}, u32[]{:S(2)}) copy-start(bf16[256,256]{1,0:T(8,128)(2,1)} %constant.68.clone.refs_2_) | copy-start | bytes 393220
  51.4 21.2 %copy-start.9 = (bf16[256,256]{1,0:T(8,128)(2,1)S(1)}, bf16[256,256]{1,0:T(8,128)(2,1)}, u32[]{:S(2)}) copy-start(bf16[256,256]{1,0:T(8,128)(2,1)} %constant.71.clone.inv_second_ref) | copy-start | bytes 393220
  51.4 21.2 %copy-start.10 = (bf16[256,256]{1,0:T(8,128)(2,1)S(1)}, bf16[256,256]{1,0:T(8,128)(2,1)}, u32[]{:S(2)}) copy-start(bf16[256,256]{1,0:T(8,128)(2,1)} %constant.70.clone.second_ref) | copy-start | bytes 393220
  74.1 6.1 %copy-start = (bf16[256,256]{1,0:T(8,128)(2,1)S(1)}, bf16[256,256]{1,0:T(8,128)(2,1)}, u32[]{:S(2)}) copy-start(bf16[256,256]{1,0:T(8,128)(2,1)} %constant.69.clone.gather_ref) | copy-start | bytes 393220
  74.1 20.4 %all-to-all-start.2 = ((bf16[128,8,128]{2,1,0:T(8,128)(2,1)}), bf16[128,8,128]{2,1,0:T(8,128)(2,1)S(1)}, u32[]{:S(2)}, u32[]{:S(2)}) async-start(bf16[128,8,128]{2,1,0:T(8,128)(2,1)} %bitcast.9), calls=%async_computation.2 | async-start | bytes 524288 | tf_op jit(solution)/shard_map/all_to_all | solution.py:255

commit v6 on v5

--- a/solution.py
+++ b/solution.py
@@ -226,11 +226,19 @@
         copy.wait()
 
 
-def unpack_grads(got_ref, gather_ref, value_ref, filt_ref):
-    tiles = gather_half(got_ref, gather_ref[...])
-    for q in range(ROWS):
-        value_ref[q * LANES:(q + 1) * LANES, :] = tiles[q].astype(BF16)
-        filt_ref[q * LANES:(q + 1) * LANES, :] = tiles[ROWS + q]
+def unpack_grads(got_ref, gather_ref, value_ref, filt_ref, value, filt, sems):
+    blocks = [dot(gather_ref[...], got_ref[part * 256:(part + 1) * 256, :]) for part in range(4)]
+    copies = []
+    for slot in list(range(ROWS, SLOTS)) + list(range(ROWS)):
+        buffer, ref = (value, value_ref) if slot < ROWS else (filt, filt_ref)
+        tile = jnp.concatenate([block[slot * 32:(slot + 1) * 32] for block in blocks], axis=0).T
+        start = slot % ROWS * LANES
+        buffer[start:start + LANES, :] = tile.astype(buffer.dtype)
+        cut = pl.ds(start, LANES)
+        copies.append(pltpu.make_async_copy(buffer.at[cut], ref.at[cut], sems.at[slot]))
+        copies[-1].start()
+    for copy in copies:
+        copy.wait()
 
 
 COVER = pl.CostEstimate(flops=40_000_000_000, transcendentals=0, bytes_accessed=40_000_000)
@@ -310,7 +318,11 @@
         scratch_shapes=[pltpu.VMEM((length, features), BF16), pltpu.SemaphoreType.DMA((features // CHUNK,))],
     )
     grad_value, grad_filt = call(
-        unpack_grads, [signal, jax.ShapeDtypeStruct((length, width), F32)], got, t["spread"].T
+        unpack_grads, [signal, jax.ShapeDtypeStruct((length, width), F32)], got, t["spread"].T,
+        out_specs=[pl.BlockSpec(memory_space=pltpu.HBM)] * 2,
+        scratch_shapes=[
+            pltpu.VMEM((length, width), BF16), pltpu.VMEM((length, width), F32), pltpu.SemaphoreType.DMA((SLOTS,))
+        ],
     )
     return (mixed[None], grad_query[None], grad_value[None], grad_filt)
 

time: 96.4 us -> 96.5 us (level)
  no operation moved by 1% of the time
where the time goes in v6:
time: 96.5 us; the launch traced here: 95.6 us
  starting transfers between devices  46.7 us (48%)
  blocking collectives  31.9 us (33%)
  Pallas kernels  9.72 us (10%)
  waiting for transfers between devices  4.86 us (5%)
  local copies, waits for them, and re-layouts  1.41 us (1%)
  between operations  1.01 us (1%)
    all_to_all x2, starting transfers between devices, exchange(): lax.all_to_all(message, ('dp', 'seq'), split_axis=0, concat_axis=0, tiled...  26.9 us
    all_to_all x1, blocking collectives, exchange(): lax.all_to_all(message, ('dp', 'seq'), split_axis=0, concat_axis=0, tiled...  21.1 us
    ppermute x6, starting transfers between devices, shifted(): lax.ppermute(array, 'tensor', [(i, (i + distance) % count) for i in range...  19.8 us
    all_gather x1, blocking collectives, per_device(): gathered = lax.all_gather(gated, 'tensor', axis=0, tiled=True)  10.8 us
    pallas_call x8, Pallas kernels, call(): pl.pallas_call(kernel, out_shape=outs, **options, name=kernel.__name__, c...  9.72 us
    ppermute x6, waiting for transfers between devices, shifted(): lax.ppermute(array, 'tensor', [(i, (i + distance) % count) for i in range...  3.92 us
  transfers between devices with their start and end apart: 8, of which 3 were waited for; matrix products, arithmetic and copies ran while one was open for 0% of the time, Pallas kernels for 7%

profile of v6, /device:TPU:1, one launch (start us, length us, event | category | flops | bytes accessed | tf_op | source)
XLA Modules:
  0.0 95.6 jit_solution(13463101868811181658)
XLA Ops:
  0.7 0.0 copy-start.11
  0.7 0.0 copy-start.12
  0.7 0.0 copy-start.13
  0.7 1.3 %constant_dynamic-slice_fusion = (bf16[128,1024]{1,0:T(8,128)(2,1)S(1)}, bf16[128,1024]{1,0:T(8,128)(2,1)S(1)}, bf16[128,1024]{1,0:T(8,128)(2,1)S(1)}, bf16[128,1024]{1,0:T(8,128)(2,1)S(1)}) fusion(bf16[128,4096]{1,0:T(8,128)(2,1)} %param.20, s32[]{:T(128)S(6)} %select_n.38, s32[]{:T(128)S(6)} %select_n.34, s32[]{:T(128)S(6)} %select_n.32, s32[]{:T(128)S(6)} %select_n.36), kind=kLoop, calls=%fused_computation | loop fusion | bytes 2097168 | tf_op jit(solution)/shard_map/dynamic_slice | solution.py:284
  2.0 5.2 %collective-permute-start.2 = (bf16[128,1024]{1,0:T(8,128)(2,1)S(1)}, bf16[128,1024]{1,0:T(8,128)(2,1)S(1)}, u32[]{:S(2)}, u32[]{:S(2)}) collective-permute-start(bf16[128,1024]{1,0:T(8,128)(2,1)S(1)} %get-tuple-element.30), channel_id=1, source_target_pairs={{0,3},{1,0},{2,1},{3,2},{4,7},{5,4},{6,5},{7,6},{8,11},{9,8},{10,9... | collective-permute-start | bytes 786440 | tf_op jit(solution)/shard_map/ppermute | solution.py:269
  7.3 1.9 %collective-permute-start = (bf16[128,1024]{1,0:T(8,128)(2,1)S(1)}, bf16[128,1024]{1,0:T(8,128)(2,1)S(1)}, u32[]{:S(2)}, u32[]{:S(2)}) collective-permute-start(bf16[128,1024]{1,0:T(8,128)(2,1)S(1)} %get-tuple-element.31), channel_id=1, source_target_pairs={{0,1},{1,2},{2,3},{3,0},{4,5},{5,6},{6,7},{7,4},{8,9},{9,10},{10,1... | collective-permute-start | bytes 786440 | tf_op jit(solution)/shard_map/ppermute | solution.py:269
  9.2 3.6 %collective-permute-start.1 = (bf16[128,1024]{1,0:T(8,128)(2,1)S(1)}, bf16[128,1024]{1,0:T(8,128)(2,1)S(1)}, u32[]{:S(2)}, u32[]{:S(2)}) collective-permute-start(bf16[128,1024]{1,0:T(8,128)(2,1)S(1)} %get-tuple-element.33), channel_id=1, source_target_pairs={{0,2},{1,3},{2,0},{3,1},{4,6},{5,7},{6,4},{7,5},{8,10},{9,11},{10,... | collective-permute-start | bytes 786440 | tf_op jit(solution)/shard_map/ppermute | solution.py:269
  12.8 0.0 copy-done.11
  12.8 0.0 copy-done.12
  12.9 0.0 copy-done.13
  12.9 1.1 %pack_inputs.1 = bf16[1024,128]{1,0:T(8,128)(2,1)} custom-call(bf16[512,128]{1,0:T(8,128)(2,1)S(1)} %bitcast.19, f32[512,128]{1,0:T(8,128)S(1)} %copy-done.11, bf16[256,256]{1,0:T(8,128)(2,1)S(1)} %copy-done.13), custom_call_target="tpu_custom_call" | custom-call | flops 40000000000 | bytes 40000000 | tf_op jit(solution)/shard_map/pack_inputs/pallas_call | solution.py:249
  14.0 20.8 %all-to-all-start = ((bf16[128,8,128]{2,1,0:T(8,128)(2,1)}), bf16[128,8,128]{2,1,0:T(8,128)(2,1)S(1)}, u32[]{:S(2)}, u32[]{:S(2)}) async-start(bf16[128,8,128]{2,1,0:T(8,128)(2,1)} %bitcast.2), calls=%async_computation | async-start | bytes 524288 | tf_op jit(solution)/shard_map/all_to_all | solution.py:263
  34.7 0.0 collective-permute-done.2.refs_3_
  34.8 0.0 collective-permute-done.refs_1_
  34.8 0.0 collective-permute-done.1.refs_2_
  34.8 0.0 copy-start.2
  34.8 0.0 copy-start.3
  34.8 0.0 copy-start.4
  34.8 0.0 copy-start.5
  34.8 0.0 copy-start.7
  34.8 0.0 copy-start.8
  34.9 2.1 %partial_grads.1 = (bf16[512,128]{1,0:T(8,128)(2,1)S(1)}, bf16[512,128]{1,0:T(8,128)(2,1)S(1)}, bf16[512,128]{1,0:T(8,128)(2,1)S(1)}, bf16[512,128]{1,0:T(8,128)(2,1)S(1)}) custom-call(bf16[512,1024]{1,0:T(8,128)(2,1)} %bitcast.21, bf16[128,1024]{1,0:T(8,128)(2,1)S(1)} %get-tuple-element.32.refs_0_, bf16[128,1024]{1,0:T(8,128)(2,1)S(1)} %collective-permute-done.refs_1_, ...), custom_call_target="tpu_custom_call" | custom-call | flops 40000000000 | bytes 40000000 | tf_op jit(solution)/shard_map/partial_grads/pallas_call | solution.py:249
  37.0 2.8 %collective-permute-start.3 = (bf16[512,128]{1,0:T(8,128)(2,1)S(1)}, bf16[512,128]{1,0:T(8,128)(2,1)S(1)}, u32[]{:S(2)}, u32[]{:S(2)}) collective-permute-start(bf16[512,128]{1,0:T(8,128)(2,1)S(1)} %get-tuple-element.19), channel_id=1, source_target_pairs={{0,3},{1,0},{2,1},{3,2},{4,7},{5,4},{6,5},{7,6},{8,11},{9,8},{10,9... | collective-permute-start | bytes 393224 | tf_op jit(solution)/shard_map/ppermute | solution.py:269
  39.7 4.4 %collective-permute-start.4 = (bf16[512,128]{1,0:T(8,128)(2,1)S(1)}, bf16[512,128]{1,0:T(8,128)(2,1)S(1)}, u32[]{:S(2)}, u32[]{:S(2)}) collective-permute-start(bf16[512,128]{1,0:T(8,128)(2,1)S(1)} %get-tuple-element.20), channel_id=1, source_target_pairs={{0,2},{1,3},{2,0},{3,1},{4,6},{5,7},{6,4},{7,5},{8,10},{9,11},{10,... | collective-permute-start | bytes 393224 | tf_op jit(solution)/shard_map/ppermute | solution.py:269
  44.1 1.9 %collective-permute-start.5 = (bf16[512,128]{1,0:T(8,128)(2,1)S(1)}, bf16[512,128]{1,0:T(8,128)(2,1)S(1)}, u32[]{:S(2)}, u32[]{:S(2)}) collective-permute-start(bf16[512,128]{1,0:T(8,128)(2,1)S(1)} %get-tuple-element.21), channel_id=1, source_target_pairs={{0,1},{1,2},{2,3},{3,0},{4,5},{5,6},{6,7},{7,4},{8,9},{9,10},{10,1... | collective-permute-start | bytes 393224 | tf_op jit(solution)/shard_map/ppermute | solution.py:269
  46.0 0.0 all-to-all-done
  46.0 0.0 copy-done.2
  46.1 0.0 copy-done.3
  46.1 0.0 copy-done.4
  46.1 0.0 copy-done.5
  46.1 0.0 copy-done.7
  46.1 0.0 copy-done.8
  46.1 0.0 copy-start.1
  46.1 0.0 copy-start.6
  46.1 1.0 %convolve.1 = (bf16[1024,128]{1,0:T(8,128)(2,1)S(1)}, f32[512,256]{1,0:T(8,128)S(1)}, f32[128,256]{1,0:T(8,128)S(1)}) custom-call(bf16[1024,128]{1,0:T(8,128)(2,1)S(1)} %bitcast.15, bf16[256,256]{1,0:T(8,128)(2,1)S(1)} %copy-done.8, bf16[256,256]{1,0:T(8,128)(2,1)S(1)} %copy-done.7, bf16[256,256]{1,0:T(8,128)(2,1)S(1)} %copy-done.5, ...), custom_call_target="tpu_custom_call" | custom-call | tf_op jit(solution)/shard_map/convolve/pallas_call | solution.py:249
  47.1 0.0 collective-permute-done.3.refs_4_
  47.1 0.4 collective-permute-done.4.refs_5_
  47.6 3.5 %collective-permute-done.5.refs_6_ = bf16[512,128]{1,0:T(8,128)(2,1)S(1)} collective-permute-done((bf16[512,128]{1,0:T(8,128)(2,1)S(1)}, bf16[512,128]{1,0:T(8,128)(2,1)S(1)}, u32[]{:S(2)}, u32[]{:S(2)}) %collective-permute-start.5) | collective-permute-done | bytes 131104 | tf_op jit(solution)/shard_map/ppermute | solution.py:269
  51.0 0.0 copy-done.1
  51.0 0.0 copy-done.6
  51.0 0.3 pack_grads.1
  51.4 0.0 copy-start.9
  51.4 0.0 copy-start.10
  51.4 21.1 %all_to_all.15 = bf16[128,8,128]{2,1,0:T(8,128)(2,1)S(1)} all-to-all(bf16[128,8,128]{2,1,0:T(8,128)(2,1)S(1)} %bitcast.18), channel_id=1, replica_groups=mesh['dp'=4,'seq'=32,'tensor'=4] {'dp','seq'}, dimensions={0} | all-to-all | bytes 524288 | tf_op jit(solution)/shard_map/all_to_all | solution.py:263
  72.6 0.0 copy-done.9
  72.6 0.0 copy-done.10
  72.6 1.5 %correlate.1 = bf16[1024,128]{1,0:T(8,128)(2,1)} custom-call(bf16[1024,128]{1,0:T(8,128)(2,1)S(1)} %bitcast.12, f32[512,256]{1,0:T(8,128)S(1)} %get-tuple-element.26.vspec_ref, f32[128,256]{1,0:T(8,128)S(1)} %get-tuple-element.27.fspec_ref, bf16[256,256]{1,0:T(8,128)(2,1)S(1)} %copy-done.10, bf16[256,256]{1,0:T(8,128)(2,1)S(1)} %copy-done.5, ...), custom_call_target="tpu_custom_call" | custom-call | tf_op jit(solution)/shard_map/correlate/pallas_call | solution.py:249
  74.1 0.0 copy-start
  74.1 6.1 %all-to-all-start.2 = ((bf16[128,8,128]{2,1,0:T(8,128)(2,1)}), bf16[128,8,128]{2,1,0:T(8,128)(2,1)S(1)}, u32[]{:S(2)}, u32[]{:S(2)}) async-start(bf16[128,8,128]{2,1,0:T(8,128)(2,1)} %bitcast.9), calls=%async_computation.2 | async-start | bytes 524288 | tf_op jit(solution)/shard_map/all_to_all | solution.py:263
  80.2 0.0 copy-done
  80.2 1.0 %unpack_conv.1 = (bf16[512,128]{1,0:T(8,128)(2,1)S(1)}, bf16[512,128]{1,0:T(8,128)(2,1)}) custom-call(bf16[1024,128]{1,0:T(8,128)(2,1)S(1)} %bitcast.13, bf16[512,128]{1,0:T(8,128)(2,1)S(1)} %bitcast.17, f32[512,128]{1,0:T(8,128)S(1)} %get-tuple-element.23.grad_ref, bf16[256,256]{1,0:T(8,128)(2,1)S(1)} %copy-done), custom_call_target="tpu_custom_call" | custom-call | tf_op jit(solution)/shard_map/unpack_conv/pallas_call | solution.py:249
  81.2 10.8 %all_gather.3.gated_ref = bf16[2048,128]{1,0:T(8,128)(2,1)S(1)} all-gather(bf16[512,128]{1,0:T(8,128)(2,1)S(1)} %get-tuple-element.24), channel_id=1, replica_groups=mesh['dp'=4,'seq'=32,'tensor'=4] {'tensor'}, dimensions={0}, use_global_device_ids=true | all-gather | bytes 655360 | tf_op jit(solution)/shard_map/all_gather | solution.py:308
  92.0 1.6 %project.1 = bf16[512,1024]{1,0:T(8,128)(2,1)} custom-call(bf16[2048,128]{1,0:T(8,128)(2,1)S(1)} %all_gather.3.gated_ref, bf16[128,1024]{1,0:T(8,128)(2,1)S(1)} %get-tuple-element.32.refs_0_, bf16[128,1024]{1,0:T(8,128)(2,1)S(1)} %collective-permute-done.refs_1_, bf16[128,1024]{1,0:T(8,128)(2,1)S(1)} %collective-permute-done.1.refs_2_, ...), custom_call_target="tpu_custom_call" | custom-call | tf_op jit(solution)/shard_map/project/pallas_call | solution.py:249
  93.6 0.9 all-to-all-done.2
  94.5 1.1 %unpack_grads.1 = (bf16[512,128]{1,0:T(8,128)(2,1)}, f32[512,128]{1,0:T(8,128)}) custom-call(bf16[1024,128]{1,0:T(8,128)(2,1)S(1)} %bitcast.14, bf16[256,256]{1,0:T(8,128)(2,1)S(1)} %copy-done), custom_call_target="tpu_custom_call" | custom-call | tf_op jit(solution)/shard_map/unpack_grads/pallas_call | solution.py:249
Async XLA Ops:
  0.7 12.1 %copy-start.11 = (f32[512,128]{1,0:T(8,128)S(1)}, f32[512,128]{1,0:T(8,128)}, u32[]{:S(2)}) copy-start(f32[512,128]{1,0:T(8,128)} %filt_ref.1) | copy-start | bytes 786436
  0.7 12.1 %copy-start.12 = (bf16[1,512,128]{2,1,0:T(8,128)(2,1)S(1)}, bf16[1,512,128]{2,1,0:T(8,128)(2,1)}, u32[]{:S(2)}) copy-start(bf16[1,512,128]{2,1,0:T(8,128)(2,1)} %param.18) | copy-start | bytes 393220
  0.7 12.1 %copy-start.13 = (bf16[256,256]{1,0:T(8,128)(2,1)S(1)}, bf16[256,256]{1,0:T(8,128)(2,1)}, u32[]{:S(2)}) copy-start(bf16[256,256]{1,0:T(8,128)(2,1)} %constant.61.clone.spread_ref) | copy-start | bytes 393220
  2.0 32.7 %collective-permute-start.2 = (bf16[128,1024]{1,0:T(8,128)(2,1)S(1)}, bf16[128,1024]{1,0:T(8,128)(2,1)S(1)}, u32[]{:S(2)}, u32[]{:S(2)}) collective-permute-start(bf16[128,1024]{1,0:T(8,128)(2,1)S(1)} %get-tuple-element.30), channel_id=1, source_target_pairs={{0,3},{1,0},{2,1},{3,2},{4,7},{5,4},{6,5},{7,6},{8,11},{9,8},{10,9... | collective-permute-start | bytes 786440 | tf_op jit(solution)/shard_map/ppermute | solution.py:269
  7.3 27.5 %collective-permute-start = (bf16[128,1024]{1,0:T(8,128)(2,1)S(1)}, bf16[128,1024]{1,0:T(8,128)(2,1)S(1)}, u32[]{:S(2)}, u32[]{:S(2)}) collective-permute-start(bf16[128,1024]{1,0:T(8,128)(2,1)S(1)} %get-tuple-element.31), channel_id=1, source_target_pairs={{0,1},{1,2},{2,3},{3,0},{4,5},{5,6},{6,7},{7,4},{8,9},{9,10},{10,1... | collective-permute-start | bytes 786440 | tf_op jit(solution)/shard_map/ppermute | solution.py:269
  9.2 25.6 %collective-permute-start.1 = (bf16[128,1024]{1,0:T(8,128)(2,1)S(1)}, bf16[128,1024]{1,0:T(8,128)(2,1)S(1)}, u32[]{:S(2)}, u32[]{:S(2)}) collective-permute-start(bf16[128,1024]{1,0:T(8,128)(2,1)S(1)} %get-tuple-element.33), channel_id=1, source_target_pairs={{0,2},{1,3},{2,0},{3,1},{4,6},{5,7},{6,4},{7,5},{8,10},{9,11},{10,... | collective-permute-start | bytes 786440 | tf_op jit(solution)/shard_map/ppermute | solution.py:269
  14.0 32.1 %all-to-all-start = ((bf16[128,8,128]{2,1,0:T(8,128)(2,1)}), bf16[128,8,128]{2,1,0:T(8,128)(2,1)S(1)}, u32[]{:S(2)}, u32[]{:S(2)}) async-start(bf16[128,8,128]{2,1,0:T(8,128)(2,1)} %bitcast.2), calls=%async_computation | async-start | bytes 524288 | tf_op jit(solution)/shard_map/all_to_all | solution.py:263
  34.8 11.3 %copy-start.2 = (f32[2,128,128]{2,1,0:T(8,128)S(1)}, f32[2,128,128]{2,1,0:T(8,128)}, u32[]{:S(2)}) copy-start(f32[2,128,128]{2,1,0:T(8,128)} %constant.67.clone.twist_ref) | copy-start | bytes 393220
  34.8 11.3 %copy-start.3 = (bf16[256,256]{1,0:T(8,128)(2,1)S(1)}, bf16[256,256]{1,0:T(8,128)(2,1)}, u32[]{:S(2)}) copy-start(bf16[256,256]{1,0:T(8,128)(2,1)} %constant.66.clone.inner_t_ref) | copy-start | bytes 393220
  34.8 11.3 %copy-start.4 = (bf16[256,256]{1,0:T(8,128)(2,1)S(1)}, bf16[256,256]{1,0:T(8,128)(2,1)}, u32[]{:S(2)}) copy-start(bf16[256,256]{1,0:T(8,128)(2,1)} %constant.65.clone.inner_ref) | copy-start | bytes 393220
  34.8 11.3 %copy-start.5 = (bf16[256,256]{1,0:T(8,128)(2,1)S(1)}, bf16[256,256]{1,0:T(8,128)(2,1)}, u32[]{:S(2)}) copy-start(bf16[256,256]{1,0:T(8,128)(2,1)} %constant.64.clone.inv_ref.inv_first_ref) | copy-start | bytes 393220
  34.8 11.3 %copy-start.7 = (bf16[256,256]{1,0:T(8,128)(2,1)S(1)}, bf16[256,256]{1,0:T(8,128)(2,1)}, u32[]{:S(2)}) copy-start(bf16[256,256]{1,0:T(8,128)(2,1)} %constant.63.clone.second_ref) | copy-start | bytes 393220
  34.8 11.3 %copy-start.8 = (bf16[256,256]{1,0:T(8,128)(2,1)S(1)}, bf16[256,256]{1,0:T(8,128)(2,1)}, u32[]{:S(2)}) copy-start(bf16[256,256]{1,0:T(8,128)(2,1)} %constant.62.clone.first_ref) | copy-start | bytes 393220
  37.0 10.1 %collective-permute-start.3 = (bf16[512,128]{1,0:T(8,128)(2,1)S(1)}, bf16[512,128]{1,0:T(8,128)(2,1)S(1)}, u32[]{:S(2)}, u32[]{:S(2)}) collective-permute-start(bf16[512,128]{1,0:T(8,128)(2,1)S(1)} %get-tuple-element.19), channel_id=1, source_target_pairs={{0,3},{1,0},{2,1},{3,2},{4,7},{5,4},{6,5},{7,6},{8,11},{9,8},{10,9... | collective-permute-start | bytes 393224 | tf_op jit(solution)/shard_map/ppermute | solution.py:269
  39.7 7.8 %collective-permute-start.4 = (bf16[512,128]{1,0:T(8,128)(2,1)S(1)}, bf16[512,128]{1,0:T(8,128)(2,1)S(1)}, u32[]{:S(2)}, u32[]{:S(2)}) collective-permute-start(bf16[512,128]{1,0:T(8,128)(2,1)S(1)} %get-tuple-element.20), channel_id=1, source_target_pairs={{0,2},{1,3},{2,0},{3,1},{4,6},{5,7},{6,4},{7,5},{8,10},{9,11},{10,... | collective-permute-start | bytes 393224 | tf_op jit(solution)/shard_map/ppermute | solution.py:269
  44.1 6.9 %collective-permute-start.5 = (bf16[512,128]{1,0:T(8,128)(2,1)S(1)}, bf16[512,128]{1,0:T(8,128)(2,1)S(1)}, u32[]{:S(2)}, u32[]{:S(2)}) collective-permute-start(bf16[512,128]{1,0:T(8,128)(2,1)S(1)} %get-tuple-element.21), channel_id=1, source_target_pairs={{0,1},{1,2},{2,3},{3,0},{4,5},{5,6},{6,7},{7,4},{8,9},{9,10},{10,1... | collective-permute-start | bytes 393224 | tf_op jit(solution)/shard_map/ppermute | solution.py:269
  46.1 4.9 %copy-start.1 = (bf16[1,512,128]{2,1,0:T(8,128)(2,1)S(1)}, bf16[1,512,128]{2,1,0:T(8,128)(2,1)}, u32[]{:S(2)}) copy-start(bf16[1,512,128]{2,1,0:T(8,128)(2,1)} %param.17) | copy-start | bytes 393220
  46.1 4.9 %copy-start.6 = (bf16[256,256]{1,0:T(8,128)(2,1)S(1)}, bf16[256,256]{1,0:T(8,128)(2,1)}, u32[]{:S(2)}) copy-start(bf16[256,256]{1,0:T(8,128)(2,1)} %constant.68.clone.refs_2_) | copy-start | bytes 393220
  51.4 21.2 %copy-start.9 = (bf16[256,256]{1,0:T(8,128)(2,1)S(1)}, bf16[256,256]{1,0:T(8,128)(2,1)}, u32[]{:S(2)}) copy-start(bf16[256,256]{1,0:T(8,128)(2,1)} %constant.71.clone.inv_second_ref) | copy-start | bytes 393220
  51.4 21.2 %copy-start.10 = (bf16[256,256]{1,0:T(8,128)(2,1)S(1)}, bf16[256,256]{1,0:T(8,128)(2,1)}, u32[]{:S(2)}) copy-start(bf16[256,256]{1,0:T(8,128)(2,1)} %constant.70.clone.second_ref) | copy-start | bytes 393220
  74.1 6.1 %copy-start = (bf16[256,256]{1,0:T(8,128)(2,1)S(1)}, bf16[256,256]{1,0:T(8,128)(2,1)}, u32[]{:S(2)}) copy-start(bf16[256,256]{1,0:T(8,128)(2,1)} %constant.69.clone.gather_ref) | copy-start | bytes 393220
  74.1 20.4 %all-to-all-start.2 = ((bf16[128,8,128]{2,1,0:T(8,128)(2,1)}), bf16[128,8,128]{2,1,0:T(8,128)(2,1)S(1)}, u32[]{:S(2)}, u32[]{:S(2)}) async-start(bf16[128,8,128]{2,1,0:T(8,128)(2,1)} %bitcast.9), calls=%async_computation.2 | async-start | bytes 524288 | tf_op jit(solution)/shard_map/all_to_all | solution.py:263

commit v7 on v6

--- a/solution.py
+++ b/solution.py
@@ -16,7 +16,7 @@
 SEQ = 32
 ROWS = 4
 LANES = 128
-CHUNK = 256
+CHUNK = 128
 HALVES = 256
 SLOTS = 8
 TURN = 22

time: 96.5 us -> 97 us (level)
  transfers between devices with their start and end apart: 8 -> 8, of which waited for: 3 -> 3; matrix products, arithmetic and copies ran while one was open for 0% -> 0% of each run, Pallas kernels for 7% -> 8%
where the time goes in v7:
time: 97 us; the launch traced here: 95.6 us
  starting transfers between devices  46.7 us (48%)
  blocking collectives  31.9 us (33%)
  Pallas kernels  10.3 us (11%)
  waiting for transfers between devices  4.31 us (4%)
  local copies, waits for them, and re-layouts  1.41 us (1%)
  between operations  1.01 us (1%)
    all_to_all x2, starting transfers between devices, exchange(): lax.all_to_all(message, ('dp', 'seq'), split_axis=0, concat_axis=0, tiled...  26.9 us
    all_to_all x1, blocking collectives, exchange(): lax.all_to_all(message, ('dp', 'seq'), split_axis=0, concat_axis=0, tiled...  21.1 us
    ppermute x6, starting transfers between devices, shifted(): lax.ppermute(array, 'tensor', [(i, (i + distance) % count) for i in range...  19.8 us
    all_gather x1, blocking collectives, per_device(): gathered = lax.all_gather(gated, 'tensor', axis=0, tiled=True)  10.8 us
    pallas_call x8, Pallas kernels, call(): pl.pallas_call(kernel, out_shape=outs, **options, name=kernel.__name__, c...  10.3 us
    ppermute x6, waiting for transfers between devices, shifted(): lax.ppermute(array, 'tensor', [(i, (i + distance) % count) for i in range...  3.92 us
  transfers between devices with their start and end apart: 8, of which 3 were waited for; matrix products, arithmetic and copies ran while one was open for 0% of the time, Pallas kernels for 8%

profile of v7, /device:TPU:1, one launch (start us, length us, event | category | flops | bytes accessed | tf_op | source)
XLA Modules:
  0.0 95.6 jit_solution(6149238987535859540)
XLA Ops:
  0.7 0.0 copy-start.11
  0.7 0.0 copy-start.12
  0.7 0.0 copy-start.13
  0.7 1.3 %constant_dynamic-slice_fusion = (bf16[128,1024]{1,0:T(8,128)(2,1)S(1)}, bf16[128,1024]{1,0:T(8,128)(2,1)S(1)}, bf16[128,1024]{1,0:T(8,128)(2,1)S(1)}, bf16[128,1024]{1,0:T(8,128)(2,1)S(1)}) fusion(bf16[128,4096]{1,0:T(8,128)(2,1)} %param.20, s32[]{:T(128)S(6)} %select_n.38, s32[]{:T(128)S(6)} %select_n.34, s32[]{:T(128)S(6)} %select_n.32, s32[]{:T(128)S(6)} %select_n.36), kind=kLoop, calls=%fused_computation | loop fusion | bytes 2097168 | tf_op jit(solution)/shard_map/dynamic_slice | solution.py:284
  2.0 5.2 %collective-permute-start.2 = (bf16[128,1024]{1,0:T(8,128)(2,1)S(1)}, bf16[128,1024]{1,0:T(8,128)(2,1)S(1)}, u32[]{:S(2)}, u32[]{:S(2)}) collective-permute-start(bf16[128,1024]{1,0:T(8,128)(2,1)S(1)} %get-tuple-element.30), channel_id=1, source_target_pairs={{0,3},{1,0},{2,1},{3,2},{4,7},{5,4},{6,5},{7,6},{8,11},{9,8},{10,9... | collective-permute-start | bytes 786440 | tf_op jit(solution)/shard_map/ppermute | solution.py:269
  7.3 1.9 %collective-permute-start = (bf16[128,1024]{1,0:T(8,128)(2,1)S(1)}, bf16[128,1024]{1,0:T(8,128)(2,1)S(1)}, u32[]{:S(2)}, u32[]{:S(2)}) collective-permute-start(bf16[128,1024]{1,0:T(8,128)(2,1)S(1)} %get-tuple-element.31), channel_id=1, source_target_pairs={{0,1},{1,2},{2,3},{3,0},{4,5},{5,6},{6,7},{7,4},{8,9},{9,10},{10,1... | collective-permute-start | bytes 786440 | tf_op jit(solution)/shard_map/ppermute | solution.py:269
  9.2 3.6 %collective-permute-start.1 = (bf16[128,1024]{1,0:T(8,128)(2,1)S(1)}, bf16[128,1024]{1,0:T(8,128)(2,1)S(1)}, u32[]{:S(2)}, u32[]{:S(2)}) collective-permute-start(bf16[128,1024]{1,0:T(8,128)(2,1)S(1)} %get-tuple-element.33), channel_id=1, source_target_pairs={{0,2},{1,3},{2,0},{3,1},{4,6},{5,7},{6,4},{7,5},{8,10},{9,11},{10,... | collective-permute-start | bytes 786440 | tf_op jit(solution)/shard_map/ppermute | solution.py:269
  12.8 0.0 copy-done.11
  12.8 0.0 copy-done.12
  12.9 0.0 copy-done.13
  12.9 1.1 %pack_inputs.1 = bf16[1024,128]{1,0:T(8,128)(2,1)} custom-call(bf16[512,128]{1,0:T(8,128)(2,1)S(1)} %bitcast.19, f32[512,128]{1,0:T(8,128)S(1)} %copy-done.11, bf16[256,256]{1,0:T(8,128)(2,1)S(1)} %copy-done.13), custom_call_target="tpu_custom_call" | custom-call | flops 40000000000 | bytes 40000000 | tf_op jit(solution)/shard_map/pack_inputs/pallas_call | solution.py:249
  14.0 20.8 %all-to-all-start = ((bf16[128,8,128]{2,1,0:T(8,128)(2,1)}), bf16[128,8,128]{2,1,0:T(8,128)(2,1)S(1)}, u32[]{:S(2)}, u32[]{:S(2)}) async-start(bf16[128,8,128]{2,1,0:T(8,128)(2,1)} %bitcast.2), calls=%async_computation | async-start | bytes 524288 | tf_op jit(solution)/shard_map/all_to_all | solution.py:263
  34.7 0.0 collective-permute-done.2.refs_3_
  34.8 0.0 collective-permute-done.refs_1_
  34.8 0.0 collective-permute-done.1.refs_2_
  34.8 0.0 copy-start.2
  34.8 0.0 copy-start.3
  34.8 0.0 copy-start.4
  34.8 0.0 copy-start.5
  34.8 0.0 copy-start.7
  34.8 0.0 copy-start.8
  34.9 2.1 %partial_grads.1 = (bf16[512,128]{1,0:T(8,128)(2,1)S(1)}, bf16[512,128]{1,0:T(8,128)(2,1)S(1)}, bf16[512,128]{1,0:T(8,128)(2,1)S(1)}, bf16[512,128]{1,0:T(8,128)(2,1)S(1)}) custom-call(bf16[512,1024]{1,0:T(8,128)(2,1)} %bitcast.21, bf16[128,1024]{1,0:T(8,128)(2,1)S(1)} %get-tuple-element.32.refs_0_, bf16[128,1024]{1,0:T(8,128)(2,1)S(1)} %collective-permute-done.refs_1_, ...), custom_call_target="tpu_custom_call" | custom-call | flops 40000000000 | bytes 40000000 | tf_op jit(solution)/shard_map/partial_grads/pallas_call | solution.py:249
  37.0 2.8 %collective-permute-start.3 = (bf16[512,128]{1,0:T(8,128)(2,1)S(1)}, bf16[512,128]{1,0:T(8,128)(2,1)S(1)}, u32[]{:S(2)}, u32[]{:S(2)}) collective-permute-start(bf16[512,128]{1,0:T(8,128)(2,1)S(1)} %get-tuple-element.19), channel_id=1, source_target_pairs={{0,3},{1,0},{2,1},{3,2},{4,7},{5,4},{6,5},{7,6},{8,11},{9,8},{10,9... | collective-permute-start | bytes 393224 | tf_op jit(solution)/shard_map/ppermute | solution.py:269
  39.7 4.4 %collective-permute-start.4 = (bf16[512,128]{1,0:T(8,128)(2,1)S(1)}, bf16[512,128]{1,0:T(8,128)(2,1)S(1)}, u32[]{:S(2)}, u32[]{:S(2)}) collective-permute-start(bf16[512,128]{1,0:T(8,128)(2,1)S(1)} %get-tuple-element.20), channel_id=1, source_target_pairs={{0,2},{1,3},{2,0},{3,1},{4,6},{5,7},{6,4},{7,5},{8,10},{9,11},{10,... | collective-permute-start | bytes 393224 | tf_op jit(solution)/shard_map/ppermute | solution.py:269
  44.1 1.9 %collective-permute-start.5 = (bf16[512,128]{1,0:T(8,128)(2,1)S(1)}, bf16[512,128]{1,0:T(8,128)(2,1)S(1)}, u32[]{:S(2)}, u32[]{:S(2)}) collective-permute-start(bf16[512,128]{1,0:T(8,128)(2,1)S(1)} %get-tuple-element.21), channel_id=1, source_target_pairs={{0,1},{1,2},{2,3},{3,0},{4,5},{5,6},{6,7},{7,4},{8,9},{9,10},{10,1... | collective-permute-start | bytes 393224 | tf_op jit(solution)/shard_map/ppermute | solution.py:269
  46.0 0.0 all-to-all-done
  46.0 0.0 copy-done.2
  46.1 0.0 copy-done.3
  46.1 0.0 copy-done.4
  46.1 0.0 copy-done.5
  46.1 0.0 copy-done.7
  46.1 0.0 copy-done.8
  46.1 0.0 copy-start.1
  46.1 0.0 copy-start.6
  46.1 1.0 %convolve.1 = (bf16[1024,128]{1,0:T(8,128)(2,1)S(1)}, f32[512,256]{1,0:T(8,128)S(1)}, f32[128,256]{1,0:T(8,128)S(1)}) custom-call(bf16[1024,128]{1,0:T(8,128)(2,1)S(1)} %bitcast.15, bf16[256,256]{1,0:T(8,128)(2,1)S(1)} %copy-done.8, bf16[256,256]{1,0:T(8,128)(2,1)S(1)} %copy-done.7, bf16[256,256]{1,0:T(8,128)(2,1)S(1)} %copy-done.5, ...), custom_call_target="tpu_custom_call" | custom-call | tf_op jit(solution)/shard_map/convolve/pallas_call | solution.py:249
  47.1 0.0 collective-permute-done.3.refs_4_
  47.1 0.4 collective-permute-done.4.refs_5_
  47.6 3.5 %collective-permute-done.5.refs_6_ = bf16[512,128]{1,0:T(8,128)(2,1)S(1)} collective-permute-done((bf16[512,128]{1,0:T(8,128)(2,1)S(1)}, bf16[512,128]{1,0:T(8,128)(2,1)S(1)}, u32[]{:S(2)}, u32[]{:S(2)}) %collective-permute-start.5) | collective-permute-done | bytes 131104 | tf_op jit(solution)/shard_map/ppermute | solution.py:269
  51.0 0.0 copy-done.1
  51.0 0.0 copy-done.6
  51.0 0.3 pack_grads.1
  51.4 0.0 copy-start.9
  51.4 0.0 copy-start.10
  51.4 21.1 %all_to_all.15 = bf16[128,8,128]{2,1,0:T(8,128)(2,1)S(1)} all-to-all(bf16[128,8,128]{2,1,0:T(8,128)(2,1)S(1)} %bitcast.18), channel_id=1, replica_groups=mesh['dp'=4,'seq'=32,'tensor'=4] {'dp','seq'}, dimensions={0} | all-to-all | bytes 524288 | tf_op jit(solution)/shard_map/all_to_all | solution.py:263
  72.6 0.0 copy-done.9
  72.6 0.0 copy-done.10
  72.6 1.5 %correlate.1 = bf16[1024,128]{1,0:T(8,128)(2,1)} custom-call(bf16[1024,128]{1,0:T(8,128)(2,1)S(1)} %bitcast.12, f32[512,256]{1,0:T(8,128)S(1)} %get-tuple-element.26.vspec_ref, f32[128,256]{1,0:T(8,128)S(1)} %get-tuple-element.27.fspec_ref, bf16[256,256]{1,0:T(8,128)(2,1)S(1)} %copy-done.10, bf16[256,256]{1,0:T(8,128)(2,1)S(1)} %copy-done.5, ...), custom_call_target="tpu_custom_call" | custom-call | tf_op jit(solution)/shard_map/correlate/pallas_call | solution.py:249
  74.1 0.0 copy-start
  74.1 6.1 %all-to-all-start.2 = ((bf16[128,8,128]{2,1,0:T(8,128)(2,1)}), bf16[128,8,128]{2,1,0:T(8,128)(2,1)S(1)}, u32[]{:S(2)}, u32[]{:S(2)}) async-start(bf16[128,8,128]{2,1,0:T(8,128)(2,1)} %bitcast.9), calls=%async_computation.2 | async-start | bytes 524288 | tf_op jit(solution)/shard_map/all_to_all | solution.py:263
  80.2 0.0 copy-done
  80.2 1.0 %unpack_conv.1 = (bf16[512,128]{1,0:T(8,128)(2,1)S(1)}, bf16[512,128]{1,0:T(8,128)(2,1)}) custom-call(bf16[1024,128]{1,0:T(8,128)(2,1)S(1)} %bitcast.13, bf16[512,128]{1,0:T(8,128)(2,1)S(1)} %bitcast.17, f32[512,128]{1,0:T(8,128)S(1)} %get-tuple-element.23.grad_ref, bf16[256,256]{1,0:T(8,128)(2,1)S(1)} %copy-done), custom_call_target="tpu_custom_call" | custom-call | tf_op jit(solution)/shard_map/unpack_conv/pallas_call | solution.py:249
  81.2 10.8 %all_gather.3.gated_ref = bf16[2048,128]{1,0:T(8,128)(2,1)S(1)} all-gather(bf16[512,128]{1,0:T(8,128)(2,1)S(1)} %get-tuple-element.24), channel_id=1, replica_groups=mesh['dp'=4,'seq'=32,'tensor'=4] {'tensor'}, dimensions={0}, use_global_device_ids=true | all-gather | bytes 655360 | tf_op jit(solution)/shard_map/all_gather | solution.py:308
  92.0 2.1 %project.1 = bf16[512,1024]{1,0:T(8,128)(2,1)} custom-call(bf16[2048,128]{1,0:T(8,128)(2,1)S(1)} %all_gather.3.gated_ref, bf16[128,1024]{1,0:T(8,128)(2,1)S(1)} %get-tuple-element.32.refs_0_, bf16[128,1024]{1,0:T(8,128)(2,1)S(1)} %collective-permute-done.refs_1_, bf16[128,1024]{1,0:T(8,128)(2,1)S(1)} %collective-permute-done.1.refs_2_, ...), custom_call_target="tpu_custom_call" | custom-call | tf_op jit(solution)/shard_map/project/pallas_call | solution.py:249
  94.1 0.4 all-to-all-done.2
  94.5 1.1 %unpack_grads.1 = (bf16[512,128]{1,0:T(8,128)(2,1)}, f32[512,128]{1,0:T(8,128)}) custom-call(bf16[1024,128]{1,0:T(8,128)(2,1)S(1)} %bitcast.14, bf16[256,256]{1,0:T(8,128)(2,1)S(1)} %copy-done), custom_call_target="tpu_custom_call" | custom-call | tf_op jit(solution)/shard_map/unpack_grads/pallas_call | solution.py:249
Async XLA Ops:
  0.7 12.1 %copy-start.11 = (f32[512,128]{1,0:T(8,128)S(1)}, f32[512,128]{1,0:T(8,128)}, u32[]{:S(2)}) copy-start(f32[512,128]{1,0:T(8,128)} %filt_ref.1) | copy-start | bytes 786436
  0.7 12.1 %copy-start.12 = (bf16[1,512,128]{2,1,0:T(8,128)(2,1)S(1)}, bf16[1,512,128]{2,1,0:T(8,128)(2,1)}, u32[]{:S(2)}) copy-start(bf16[1,512,128]{2,1,0:T(8,128)(2,1)} %param.18) | copy-start | bytes 393220
  0.7 12.1 %copy-start.13 = (bf16[256,256]{1,0:T(8,128)(2,1)S(1)}, bf16[256,256]{1,0:T(8,128)(2,1)}, u32[]{:S(2)}) copy-start(bf16[256,256]{1,0:T(8,128)(2,1)} %constant.61.clone.spread_ref) | copy-start | bytes 393220
  2.0 32.7 %collective-permute-start.2 = (bf16[128,1024]{1,0:T(8,128)(2,1)S(1)}, bf16[128,1024]{1,0:T(8,128)(2,1)S(1)}, u32[]{:S(2)}, u32[]{:S(2)}) collective-permute-start(bf16[128,1024]{1,0:T(8,128)(2,1)S(1)} %get-tuple-element.30), channel_id=1, source_target_pairs={{0,3},{1,0},{2,1},{3,2},{4,7},{5,4},{6,5},{7,6},{8,11},{9,8},{10,9... | collective-permute-start | bytes 786440 | tf_op jit(solution)/shard_map/ppermute | solution.py:269
  7.3 27.5 %collective-permute-start = (bf16[128,1024]{1,0:T(8,128)(2,1)S(1)}, bf16[128,1024]{1,0:T(8,128)(2,1)S(1)}, u32[]{:S(2)}, u32[]{:S(2)}) collective-permute-start(bf16[128,1024]{1,0:T(8,128)(2,1)S(1)} %get-tuple-element.31), channel_id=1, source_target_pairs={{0,1},{1,2},{2,3},{3,0},{4,5},{5,6},{6,7},{7,4},{8,9},{9,10},{10,1... | collective-permute-start | bytes 786440 | tf_op jit(solution)/shard_map/ppermute | solution.py:269
  9.2 25.6 %collective-permute-start.1 = (bf16[128,1024]{1,0:T(8,128)(2,1)S(1)}, bf16[128,1024]{1,0:T(8,128)(2,1)S(1)}, u32[]{:S(2)}, u32[]{:S(2)}) collective-permute-start(bf16[128,1024]{1,0:T(8,128)(2,1)S(1)} %get-tuple-element.33), channel_id=1, source_target_pairs={{0,2},{1,3},{2,0},{3,1},{4,6},{5,7},{6,4},{7,5},{8,10},{9,11},{10,... | collective-permute-start | bytes 786440 | tf_op jit(solution)/shard_map/ppermute | solution.py:269
  14.0 32.1 %all-to-all-start = ((bf16[128,8,128]{2,1,0:T(8,128)(2,1)}), bf16[128,8,128]{2,1,0:T(8,128)(2,1)S(1)}, u32[]{:S(2)}, u32[]{:S(2)}) async-start(bf16[128,8,128]{2,1,0:T(8,128)(2,1)} %bitcast.2), calls=%async_computation | async-start | bytes 524288 | tf_op jit(solution)/shard_map/all_to_all | solution.py:263
  34.8 11.3 %copy-start.2 = (f32[2,128,128]{2,1,0:T(8,128)S(1)}, f32[2,128,128]{2,1,0:T(8,128)}, u32[]{:S(2)}) copy-start(f32[2,128,128]{2,1,0:T(8,128)} %constant.67.clone.twist_ref) | copy-start | bytes 393220
  34.8 11.3 %copy-start.3 = (bf16[256,256]{1,0:T(8,128)(2,1)S(1)}, bf16[256,256]{1,0:T(8,128)(2,1)}, u32[]{:S(2)}) copy-start(bf16[256,256]{1,0:T(8,128)(2,1)} %constant.66.clone.inner_t_ref) | copy-start | bytes 393220
  34.8 11.3 %copy-start.4 = (bf16[256,256]{1,0:T(8,128)(2,1)S(1)}, bf16[256,256]{1,0:T(8,128)(2,1)}, u32[]{:S(2)}) copy-start(bf16[256,256]{1,0:T(8,128)(2,1)} %constant.65.clone.inner_ref) | copy-start | bytes 393220
  34.8 11.3 %copy-start.5 = (bf16[256,256]{1,0:T(8,128)(2,1)S(1)}, bf16[256,256]{1,0:T(8,128)(2,1)}, u32[]{:S(2)}) copy-start(bf16[256,256]{1,0:T(8,128)(2,1)} %constant.64.clone.inv_ref.inv_first_ref) | copy-start | bytes 393220
  34.8 11.3 %copy-start.7 = (bf16[256,256]{1,0:T(8,128)(2,1)S(1)}, bf16[256,256]{1,0:T(8,128)(2,1)}, u32[]{:S(2)}) copy-start(bf16[256,256]{1,0:T(8,128)(2,1)} %constant.63.clone.second_ref) | copy-start | bytes 393220
  34.8 11.3 %copy-start.8 = (bf16[256,256]{1,0:T(8,128)(2,1)S(1)}, bf16[256,256]{1,0:T(8,128)(2,1)}, u32[]{:S(2)}) copy-start(bf16[256,256]{1,0:T(8,128)(2,1)} %constant.62.clone.first_ref) | copy-start | bytes 393220
  37.0 10.1 %collective-permute-start.3 = (bf16[512,128]{1,0:T(8,128)(2,1)S(1)}, bf16[512,128]{1,0:T(8,128)(2,1)S(1)}, u32[]{:S(2)}, u32[]{:S(2)}) collective-permute-start(bf16[512,128]{1,0:T(8,128)(2,1)S(1)} %get-tuple-element.19), channel_id=1, source_target_pairs={{0,3},{1,0},{2,1},{3,2},{4,7},{5,4},{6,5},{7,6},{8,11},{9,8},{10,9... | collective-permute-start | bytes 393224 | tf_op jit(solution)/shard_map/ppermute | solution.py:269
  39.7 7.8 %collective-permute-start.4 = (bf16[512,128]{1,0:T(8,128)(2,1)S(1)}, bf16[512,128]{1,0:T(8,128)(2,1)S(1)}, u32[]{:S(2)}, u32[]{:S(2)}) collective-permute-start(bf16[512,128]{1,0:T(8,128)(2,1)S(1)} %get-tuple-element.20), channel_id=1, source_target_pairs={{0,2},{1,3},{2,0},{3,1},{4,6},{5,7},{6,4},{7,5},{8,10},{9,11},{10,... | collective-permute-start | bytes 393224 | tf_op jit(solution)/shard_map/ppermute | solution.py:269
  44.1 6.9 %collective-permute-start.5 = (bf16[512,128]{1,0:T(8,128)(2,1)S(1)}, bf16[512,128]{1,0:T(8,128)(2,1)S(1)}, u32[]{:S(2)}, u32[]{:S(2)}) collective-permute-start(bf16[512,128]{1,0:T(8,128)(2,1)S(1)} %get-tuple-element.21), channel_id=1, source_target_pairs={{0,1},{1,2},{2,3},{3,0},{4,5},{5,6},{6,7},{7,4},{8,9},{9,10},{10,1... | collective-permute-start | bytes 393224 | tf_op jit(solution)/shard_map/ppermute | solution.py:269
  46.1 4.9 %copy-start.1 = (bf16[1,512,128]{2,1,0:T(8,128)(2,1)S(1)}, bf16[1,512,128]{2,1,0:T(8,128)(2,1)}, u32[]{:S(2)}) copy-start(bf16[1,512,128]{2,1,0:T(8,128)(2,1)} %param.17) | copy-start | bytes 393220
  46.1 4.9 %copy-start.6 = (bf16[256,256]{1,0:T(8,128)(2,1)S(1)}, bf16[256,256]{1,0:T(8,128)(2,1)}, u32[]{:S(2)}) copy-start(bf16[256,256]{1,0:T(8,128)(2,1)} %constant.68.clone.refs_2_) | copy-start | bytes 393220
  51.4 21.2 %copy-start.9 = (bf16[256,256]{1,0:T(8,128)(2,1)S(1)}, bf16[256,256]{1,0:T(8,128)(2,1)}, u32[]{:S(2)}) copy-start(bf16[256,256]{1,0:T(8,128)(2,1)} %constant.71.clone.inv_second_ref) | copy-start | bytes 393220
  51.4 21.2 %copy-start.10 = (bf16[256,256]{1,0:T(8,128)(2,1)S(1)}, bf16[256,256]{1,0:T(8,128)(2,1)}, u32[]{:S(2)}) copy-start(bf16[256,256]{1,0:T(8,128)(2,1)} %constant.70.clone.second_ref) | copy-start | bytes 393220
  74.1 6.1 %copy-start = (bf16[256,256]{1,0:T(8,128)(2,1)S(1)}, bf16[256,256]{1,0:T(8,128)(2,1)}, u32[]{:S(2)}) copy-start(bf16[256,256]{1,0:T(8,128)(2,1)} %constant.69.clone.gather_ref) | copy-start | bytes 393220
  74.1 20.4 %all-to-all-start.2 = ((bf16[128,8,128]{2,1,0:T(8,128)(2,1)}), bf16[128,8,128]{2,1,0:T(8,128)(2,1)S(1)}, u32[]{:S(2)}, u32[]{:S(2)}) async-start(bf16[128,8,128]{2,1,0:T(8,128)(2,1)} %bitcast.9), calls=%async_computation.2 | async-start | bytes 524288 | tf_op jit(solution)/shard_map/all_to_all | solution.py:263
